TPU v7x, 256 devices: a whole 4x4x8 slice. The times are simulated.
256 devices in a mesh: group: 8 (over y, x_hi), fsdp: 32 (over x_lo, z, core).
Axes of the slice: x: 4 (x_hi: 2, x_lo: 2; x = x_hi * 2 + x_lo), y: 4, z: 8, core: 2. Of those that a mesh axis runs over, the one named last changes fastest.
Arguments:
- inputs: bfloat16 [16384, 4096], P('group', 'fsdp'), may hold values from -6 to 6
- norm_gain: bfloat16 [4096], P('fsdp'), may hold values from 0.099609375 to 1.8984375
- cotangent: bfloat16 [16384, 16384], P('group', 'fsdp'), may hold values from -0.0234375 to 0.0234375
- owners: int32 [32, 8], P('fsdp'), may hold values from 0 to 7, each once within a row
- refresh: int32 [8, 32], P('group', 'fsdp'), may hold values 0 or 1
- left_stats: float32 [4096, 16384], P('group', 'fsdp'), may hold values from -1 to 16, as said below
- right_stats: float32 [4096, 16384], P('group', 'fsdp'), may hold values from -1 to 16, as said below
- left_inverse: float32 [4096, 16384], P('group', 'fsdp'), may hold values from -1 to 8, as said below
- right_inverse: float32 [4096, 16384], P('group', 'fsdp'), may hold values from -1 to 8, as said below
Outputs:
- update: bfloat16 [4096, 16384], P('group', 'fsdp')
- left_accum: float32 [4096, 16384], P('group', 'fsdp')
- right_accum: float32 [4096, 16384], P('group', 'fsdp')
- left_refreshed: float32 [4096, 16384], P('group', 'fsdp')
- right_refreshed: float32 [4096, 16384], P('group', 'fsdp')
Inputs may be any that keep to these rules, and one draw needn't show every extreme that they name: Each row owners[c] is a permutation of 0 to 8 - 1. `left_stats`: symmetric within each 512 x 512 block, diagonal entries at least 1. `right_stats`: symmetric within each 512 x 512 block, diagonal entries at least 1. `left_inverse`: symmetric within each 512 x 512 block. `right_inverse`: symmetric within each 512 x 512 block.
All inputs are finite; a program needn't handle non-finite values. No bound on the sum of `refresh` on one device may be relied on, other than what follows from the above.
Results may differ from a plain program's by a relative error of at most 0.013.
Values may be sent and summed in bfloat16 or wider, within the bound.
No kernel may reach another device: no remote copies, remote signals or barrier semaphores. Data moves between devices by JAX's collectives and lax.ppermute only.
A program may use at most 128 MiB of HBM per device.

v0:
```python
import jax
import jax.numpy as jnp
from jax import lax
from jax.sharding import PartitionSpec as P

BLK = 512
ITERS = 2


NORM_EPSILON = 1e-05
SCALE_EPSILON = 1e-06
DECAY_RATE = 0.95
RIDGE_TERM = 1e-06
HIGHEST = lax.Precision.HIGHEST


def from_everyone(x, axis):
    copies = jnp.broadcast_to(x, (lax.axis_size(axis), *x.shape))
    return lax.all_to_all(copies, axis, split_axis=0, concat_axis=0, tiled=True)


def of_everyone(x, axis):
    everything = from_everyone(x, axis)
    return jnp.sum(everything, axis=0)


def to_blocks(matrix, block_order):
    row_count, col_count = matrix.shape
    shaped = matrix.reshape(
        row_count // block_order, block_order, col_count // block_order, block_order
    )
    return shaped.transpose(0, 2, 1, 3).reshape(-1, block_order, block_order)


def from_blocks(blocks, row_count, col_count):
    block_order = blocks.shape[-1]
    shaped = blocks.reshape(
        row_count // block_order, col_count // block_order, block_order, block_order
    )
    return shaped.transpose(0, 2, 1, 3).reshape(row_count, col_count)


def inverse_fourth_root(statistic):
    block_order = statistic.shape[0]
    identity = jnp.eye(block_order, dtype=statistic.dtype)
    matrix = statistic + RIDGE_TERM * identity
    scaling = 2.5 / jnp.sqrt(jnp.sum(matrix * matrix))
    inverse_root = scaling**0.25 * identity
    scaled = scaling * matrix
    for iteration in range(ITERS):
        factor = 1.25 * identity - 0.25 * scaled
        inverse_root = jnp.dot(inverse_root, factor, precision=HIGHEST)
        if iteration + 1 < ITERS:
            square = jnp.dot(factor, factor, precision=HIGHEST)
            scaled = jnp.dot(jnp.dot(square, square, precision=HIGHEST), scaled, precision=HIGHEST)
    return inverse_root


def block_step(operands):
    grad_block, left_old, right_old, left_root, right_root, refresh_flag = operands
    left_gram = lax.dot_general(
        grad_block, grad_block, (((1,), (1,)), ((), ())), preferred_element_type=jnp.float32
    )
    right_gram = lax.dot_general(
        grad_block, grad_block, (((0,), (0,)), ((), ())), preferred_element_type=jnp.float32
    )
    left_accum = DECAY_RATE * left_old + (1.0 - DECAY_RATE) * left_gram
    right_accum = DECAY_RATE * right_old + (1.0 - DECAY_RATE) * right_gram
    local_grad = grad_block.astype(jnp.float32)
    conditioned = jnp.dot(
        jnp.dot(left_root, local_grad, precision=HIGHEST), right_root, precision=HIGHEST
    )
    own_update = (
        conditioned * lax.rsqrt(jnp.mean(conditioned * conditioned) + SCALE_EPSILON)
    ).astype(jnp.bfloat16)

    def recompute(unused):
        return (inverse_fourth_root(left_accum), inverse_fourth_root(right_accum))

    def keep_old(unused):
        return (left_root, right_root)

    left_new, right_new = lax.cond(refresh_flag > 0, recompute, keep_old, 0)
    return (own_update, left_accum, right_accum, left_new, right_new)


def body(
    inputs,
    norm_gain,
    cotangent,
    owners,
    refresh,
    left_stats,
    right_stats,
    left_inverse,
    right_inverse,
):
    my_group = lax.axis_index("group")
    slab_rows, local_cols = left_stats.shape
    col_blocks = local_cols // BLK
    width_total = inputs.shape[1] * lax.axis_size("fsdp")
    values = inputs.astype(jnp.float32)
    squares = of_everyone(jnp.sum(values * values, axis=1), "fsdp")
    scales = lax.rsqrt(squares / width_total + NORM_EPSILON)
    normed = (values * scales[:, None] * norm_gain.astype(jnp.float32)[None, :]).astype(
        jnp.bfloat16
    )
    partial_value = lax.dot_general(
        lax.all_gather(normed, "fsdp", axis=1, tiled=True),
        cotangent,
        (((0,), (0,)), ((), ())),
        preferred_element_type=jnp.float32,
    )
    summed = lax.psum_scatter(
        partial_value.astype(jnp.bfloat16), "group", scatter_dimension=0, tiled=True
    )
    portion = lax.all_gather(summed, "group", axis=0, tiled=True)
    shard_count = portion.shape[0] // slab_rows
    sources = jnp.arange(shard_count, dtype=jnp.int32)
    matches = jnp.take(owners, sources, axis=1).T == my_group
    pieces = portion.reshape(shard_count, slab_rows, col_blocks, BLK)
    chosen = jnp.where(matches[:, None, :, None], pieces, jnp.zeros_like(pieces))
    owned = (
        jnp.sum(chosen.astype(jnp.float32), axis=0)
        .reshape(slab_rows, local_cols)
        .astype(jnp.bfloat16)
    )
    results = lax.map(
        block_step,
        (
            to_blocks(owned, BLK),
            to_blocks(left_stats, BLK),
            to_blocks(right_stats, BLK),
            to_blocks(left_inverse, BLK),
            to_blocks(right_inverse, BLK),
            refresh.reshape(-1),
        ),
    )
    own_update, left_accum, right_accum, left_new, right_new = results
    own_update = from_blocks(own_update, slab_rows, local_cols)
    owner_here = owners[:, my_group]
    portion = lax.all_gather(own_update, "group", axis=0, tiled=True)
    shard_count = portion.shape[0] // slab_rows
    sources = jnp.arange(shard_count, dtype=jnp.int32)
    matches = sources[:, None] == owner_here[None, :]
    pieces = portion.reshape(shard_count, slab_rows, col_blocks, BLK)
    chosen = jnp.where(matches[:, None, :, None], pieces, jnp.zeros_like(pieces))
    update = (
        jnp.sum(chosen.astype(jnp.float32), axis=0)
        .reshape(slab_rows, local_cols)
        .astype(jnp.bfloat16)
    )
    return (
        update,
        from_blocks(left_accum, slab_rows, local_cols),
        from_blocks(right_accum, slab_rows, local_cols),
        from_blocks(left_new, slab_rows, local_cols),
        from_blocks(right_new, slab_rows, local_cols),
    )


def solution(mesh):
    in_specs = (
        P("group", "fsdp"),
        P("fsdp"),
        P("group", "fsdp"),
        P("fsdp", None),
        P("group", "fsdp"),
        P("group", "fsdp"),
        P("group", "fsdp"),
        P("group", "fsdp"),
        P("group", "fsdp"),
    )
    out_specs = (
        P("group", "fsdp"),
        P("group", "fsdp"),
        P("group", "fsdp"),
        P("group", "fsdp"),
        P("group", "fsdp"),
    )
    return jax.shard_map(body, mesh=mesh, in_specs=in_specs, out_specs=out_specs, check_vma=False)
```

profile of v0, /device:TPU:1, one launch (start us, length us, event | category | flops | bytes accessed | tf_op | source)
XLA Modules:
  0.0 437.0 jit_solution(1045666190124357930)
XLA Ops:
  7.2 2.4 copy.21
  9.6 2.3 copy.22
  12.2 0.8 broadcast_in_dim.40
  13.1 11.0 %all-to-all-start = ((f32[32,1,2048]{2,1,0:T(1,128)}), f32[32,1,2048]{2,1,0:T(1,128)S(1)}, u32[]{:S(2)}, u32[]{:S(2)}) async-start(f32[32,1,2048]{2,1,0:T(1,128)} %broadcast_in_dim.40), calls=%async_computation | async-start | bytes 524288 | tf_op jit(solution)/shard_map/all_to_all | solution.py:19
  24.2 11.8 %all-to-all-done = f32[32,1,2048]{2,1,0:T(1,128)S(1)} async-done(((f32[32,1,2048]{2,1,0:T(1,128)}), f32[32,1,2048]{2,1,0:T(1,128)S(1)}, u32[]{:S(2)}, u32[]{:S(2)}) %all-to-all-start) | async-done | bytes 262176 | tf_op jit(solution)/shard_map/all_to_all | solution.py:19
  36.2 1.1 fusion.52
  37.4 122.2 %all-gather.4.cloned.1.call-done = bf16[2048,4096]{1,0:T(8,128)(2,1)} async-done(((bf16[2048,128]{1,0:T(8,128)(2,1)}), bf16[2048,4096]{1,0:T(8,128)(2,1)}) %all-gather.4.cloned.1.call-update) | async-done | bytes 16777232 | tf_op jit(solution)/shard_map/all_gather | solution.py:109
  159.7 13.8 %convolution_convert_fusion = bf16[4096,512]{1,0:T(8,128)(2,1)} fusion(bf16[2048,4096]{1,0:T(8,128)(2,1)} %all-gather.4.cloned.1.call-done, bf16[2048,512]{1,0:T(8,128)(2,1)S(1)} %copy-done), kind=kOutput, calls=%fused_computation.60 | convolution fusion | flops 8592031744 | bytes 23068672 | tf_op jit(solution)/shard_map/dot_general | solution.py:108
  173.6 86.1 %reduce-scatter.2.cloned.1.call-done = bf16[512,512]{1,0:T(8,128)(2,1)} async-done(((bf16[4096,512]{1,0:T(8,128)(2,1)}), bf16[512,512]{1,0:T(8,128)(2,1)}) %reduce-scatter.2.cloned.1.call-update) | async-done | bytes 524304 | tf_op jit(solution)/shard_map/reduce_scatter | solution.py:114
  259.7 0.6 gather_fusion
  260.4 78.1 %all-gather.6.cloned.1.call-done = bf16[4096,512]{1,0:T(8,128)(2,1)} async-done(((bf16[512,512]{1,0:T(8,128)(2,1)}), bf16[4096,512]{1,0:T(8,128)(2,1)}) %all-gather.6.cloned.1.call-update) | async-done | bytes 4194320 | tf_op jit(solution)/shard_map/all_gather | solution.py:117
  338.5 3.4 select_reduce_fusion.1
  341.9 2.5 fusion.58
  344.3 4.6 %multiply_reduce_fusion.2 = (f32[]{:T(128)}, f32[512,512]{1,0:T(8,128)}) fusion(f32[512,512]{1,0:T(8,128)S(1)} %fusion.58, f32[512,512]{1,0:T(8,128)} %copy.22), kind=kOutput, calls=%fused_computation.73 | convolution fusion | flops 1611137024 | bytes 3145732 | tf_op jit(solution)/shard_map/while/body/eval_jaxpr/dot_general | solution.py:70
  349.7 2.1 multiply_convert_fusion
  353.1 0.7 iota_compare_fusion.3
  353.7 2.7 fusion.49
  356.4 2.7 fusion.48
  359.1 27.6 %conditional.1 = ((f32[512,512]{1,0:T(8,128)}, f32[512,512]{1,0:T(8,128)})) conditional(s32[]{:T(128)} %bitcast.4, (f32[512,512]{1,0:T(8,128)}, f32[512,512]{1,0:T(8,128)}) %tuple.17, (f32[512,512]{1,0:T(8,128)}, f32[512,512]{1,0:T(8,128)}) %tuple.18), branch_computations={%region_6.7_spmd, %region_7.10_spmd} | conditional | flops 16120807424 | bytes 35651768 | solution.py:83
  359.1 2.5 multiply_reduce_fusion
  362.2 3.2 fusion.2
  365.5 2.0 fusion.6
  367.5 1.8 fusion.54
  369.3 1.9 select_subtract_fusion.2
  371.2 2.8 fusion.55
  374.7 3.1 fusion
  377.8 2.3 fusion.7
  380.1 1.8 fusion.56
  382.0 1.9 select_subtract_fusion
  383.9 2.8 fusion.57
  386.7 39.7 %all-gather.8.cloned.1.call-done = bf16[4096,512]{1,0:T(8,128)(2,1)} async-done(((bf16[512,512]{1,0:T(8,128)(2,1)}), bf16[4096,512]{1,0:T(8,128)(2,1)}) %all-gather.8.cloned.1.call-update) | async-done | bytes 4194320 | tf_op jit(solution)/shard_map/all_gather | solution.py:142
  426.3 4.2 select_reduce_fusion
  (28 shorter events, 1.4 us)
Async XLA Ops:
  7.2 152.5 %copy-start = (bf16[2048,512]{1,0:T(8,128)(2,1)S(1)}, bf16[2048,512]{1,0:T(8,128)(2,1)}, u32[]{:S(2)}) copy-start(bf16[2048,512]{1,0:T(8,128)(2,1)} %param.13) | copy-start | bytes 6291460
  7.2 4.7 %copy-start.4 = (bf16[2048,128]{1,0:T(8,128)(2,1)S(1)}, bf16[2048,128]{1,0:T(8,128)(2,1)}, u32[]{:S(2)}) copy-start(bf16[2048,128]{1,0:T(8,128)(2,1)} %param.11) | copy-start | bytes 1572868
  7.2 17.0 %copy-start.5 = (bf16[128]{0:T(256)(128)(2,1)S(1)}, bf16[128]{0:T(256)(128)(2,1)}, u32[]{:S(2)}) copy-start(bf16[128]{0:T(256)(128)(2,1)} %param.12) | copy-start | bytes 772
  13.1 23.0 %all-to-all-start = ((f32[32,1,2048]{2,1,0:T(1,128)}), f32[32,1,2048]{2,1,0:T(1,128)S(1)}, u32[]{:S(2)}, u32[]{:S(2)}) async-start(f32[32,1,2048]{2,1,0:T(1,128)} %broadcast_in_dim.40), calls=%async_computation | async-start | bytes 524288 | tf_op jit(solution)/shard_map/all_to_all | solution.py:19
  24.1 135.5 %all-gather.4.cloned.1.call-start = ((), (), s32[]{:S(2)}) async-start(), calls=%async_computation.2 | async-start | bytes 17301504 | tf_op jit(solution)/shard_map/all_gather | solution.py:109
  37.4 222.2 %reduce-scatter.2.cloned.1.call-start = ((), (), s32[]{:S(2)}) async-start(), calls=%async_computation.3 | async-start | bytes 4718592 | tf_op jit(solution)/shard_map/reduce_scatter | solution.py:114
  173.5 86.2 %copy-start.1 = (s32[1,8]{1,0:T(1,128)S(1)}, s32[1,8]{1,0:T(1,128)}, u32[]{:S(2)}) copy-start(s32[1,8]{1,0:T(1,128)} %param.14) | copy-start | bytes 100
  173.5 165.0 %all-gather.6.cloned.1.call-start = ((), (), s32[]{:S(2)}) async-start(), calls=%async_computation.4 | async-start | bytes 4718592 | tf_op jit(solution)/shard_map/all_gather | solution.py:117
  259.7 166.7 %all-gather.8.cloned.1.call-start = ((), (), s32[]{:S(2)}) async-start(), calls=%async_computation.5 | async-start | bytes 4718592 | tf_op jit(solution)/shard_map/all_gather | solution.py:142
  359.1 6.4 %copy-start.2 = (f32[512,512]{1,0:T(8,128)S(1)}, f32[512,512]{1,0:T(8,128)}, u32[]{:S(2)}) copy-start(f32[512,512]{1,0:T(8,128)} %get-tuple-element.32) | copy-start | bytes 3145732 | tf_op jit(solution)/shard_map/while/body/eval_jaxpr/cond
  371.2 6.6 %copy-start.3 = (f32[512,512]{1,0:T(8,128)S(1)}, f32[512,512]{1,0:T(8,128)}, u32[]{:S(2)}) copy-start(f32[512,512]{1,0:T(8,128)} %get-tuple-element.33) | copy-start | bytes 3145732 | tf_op jit(solution)/shard_map/while/body/eval_jaxpr/cond
Sparse Core Ops, SparseCore 0:
  37.5 122.1 all-gather.3
  173.6 85.9 reduce-scatter.1
  262.6 75.8 all-gather.5
  351.9 74.3 all-gather.7
where the time goes:
time: 438 us; the launch traced here: 437 us
  waiting for transfers between devices  338 us (77%)
  matrix products  50 us (11%)
  between operations  15.2 us (3%)
  other arithmetic  14.5 us (3%)
  starting transfers between devices  11.2 us (3%)
  local copies, waits for them, and re-layouts  6.78 us (2%)
    all_gather x1, waiting for transfers between devices, body(): lax.all_gather(normed, 'fsdp', axis=1, tiled=True)  122 us
    reduce_scatter x1, waiting for transfers between devices, body(): lax.psum_scatter(partial_value.astype(jnp.bfloat16), 'group', scatter_dim...  86.1 us
    all_gather x1, waiting for transfers between devices, body(): portion = lax.all_gather(summed, 'group', axis=0, tiled=True)  78.1 us
    all_gather x1, waiting for transfers between devices, body(): portion = lax.all_gather(own_update, 'group', axis=0, tiled=True)  39.7 us
    dot_general x1, matrix products, body(): lax.dot_general(lax.all_gather(normed, 'fsdp', axis=1, tiled=True), cotan...  13.8 us
    dot_general x4, matrix products, inverse_fourth_root(): inverse_root = jnp.dot(inverse_root, factor, precision=HIGHEST)  12 us
    all_to_all x1, waiting for transfers between devices, from_everyone(): return lax.all_to_all(copies, axis, split_axis=0, concat_axis=0, tiled=True)  11.8 us
    all_to_all x1, starting transfers between devices, from_everyone(): return lax.all_to_all(copies, axis, split_axis=0, concat_axis=0, tiled=True)  11 us
  transfers between devices with their start and end apart: 5, of which 5 were waited for; matrix products, arithmetic and copies ran while one was open for 8% of the time, Pallas kernels for 0%

commit v1 on v0

v1 whole, which is shorter than its diff:
```python
import jax
import jax.numpy as jnp
from jax import lax
from jax.experimental import pallas as pl
from jax.experimental.pallas import tpu as pltpu
from jax.sharding import Mesh
from jax.sharding import PartitionSpec as P

NORM_EPSILON = 1e-05
SCALE_EPSILON = 1e-06
DECAY_RATE = 0.95
RIDGE_TERM = 1e-06
BLK = 512
ITERS = 2
N_GROUP = 8
CHUNK = BLK // N_GROUP
GROUP = ("y", "xh")
FSDP = ("xl", "z", "core")
BF16 = jnp.bfloat16
F32 = jnp.float32
NT = (((1,), (1,)), ((), ()))
TN = (((0,), (0,)), ((), ()))


def dot(a, b):
    return jnp.dot(a, b, preferred_element_type=F32)


def dot_dims(a, b, dims):
    return lax.dot_general(a, b, dims, preferred_element_type=F32)


def split2(a):
    high = a.astype(BF16)
    return high, (a - high.astype(F32)).astype(BF16)


def transpose_kernel(x_ref, o_ref):
    o_ref[...] = x_ref[...].T


def transposed(x):
    rows, cols = x.shape
    return pl.pallas_call(
        transpose_kernel,
        grid=(rows // BLK,),
        in_specs=[pl.BlockSpec((BLK, cols), lambda i: (i, 0))],
        out_specs=pl.BlockSpec((cols, BLK), lambda i: (0, i)),
        out_shape=jax.ShapeDtypeStruct((cols, rows), x.dtype),
        name="transpose",
    )(x)


def pick_kernel(idx_ref, x_ref, o_ref):
    o_ref[...] = x_ref[...]


def pick(x, idx):
    rest = x.shape[1:]
    return pl.pallas_call(
        pick_kernel,
        grid_spec=pltpu.PrefetchScalarGridSpec(
            num_scalar_prefetch=1,
            grid=(x.shape[0],),
            in_specs=[pl.BlockSpec((1, *rest), lambda i, idx: (idx[i], 0, 0, 0))],
            out_specs=pl.BlockSpec((1, *rest), lambda i, idx: (i, 0, 0, 0)),
        ),
        out_shape=jax.ShapeDtypeStruct(x.shape, x.dtype),
        name="pick",
    )(idx, x)


def partial_kernel(cot_ref, x_ref, gain_ref, o_ref):
    x = jnp.concatenate([x_ref[i] for i in range(4)], axis=1)
    for half in range(2):
        rows = dot(cot_ref[half * BLK : (half + 1) * BLK, :], x)
        rows = (rows * gain_ref[0]).astype(BF16)
        for j in range(N_GROUP):
            o_ref[j, half, 0] = rows[j * CHUNK : (j + 1) * CHUNK]


def partials(cot, x, gain):
    tokens = cot.shape[1]
    slabs = x.shape[0] // 4
    flops = 2 * cot.shape[0] * tokens * slabs * BLK
    return pl.pallas_call(
        partial_kernel,
        grid=(slabs,),
        in_specs=[
            pl.BlockSpec((2 * BLK, tokens), lambda i: (0, 0)),
            pl.BlockSpec((4, tokens, 128), lambda i: (i, 0, 0)),
            pl.BlockSpec((1, 1, BLK), lambda i: (i, 0, 0)),
        ],
        out_specs=pl.BlockSpec((N_GROUP, 2, 1, CHUNK, BLK), lambda i: (0, 0, i, 0, 0)),
        out_shape=jax.ShapeDtypeStruct((N_GROUP, 2, slabs, CHUNK, BLK), BF16),
        compiler_params=pltpu.CompilerParams(vmem_limit_bytes=48 * 2**20),
        cost_estimate=pl.CostEstimate(flops=flops, bytes_accessed=16 * 2**20, transcendentals=0),
        name="partials",
    )(cot, x, gain)


def reduce_kernel(owner_ref, x_ref, o_ref):
    slab = pl.program_id(0)
    total = x_ref[0, 0].astype(F32)
    for g in range(1, N_GROUP):
        total = total + x_ref[g, 0].astype(F32)
    total = total.astype(BF16)
    o_ref[slab, 1] = total
    o_ref[owner_ref[slab], 0] = total


def reduce_route(x, owner):
    return pl.pallas_call(
        reduce_kernel,
        grid_spec=pltpu.PrefetchScalarGridSpec(
            num_scalar_prefetch=1,
            grid=(N_GROUP,),
            in_specs=[pl.BlockSpec((N_GROUP, 1, CHUNK, BLK), lambda i, owner: (0, i, 0, 0))],
            out_specs=pl.BlockSpec((N_GROUP, 2, CHUNK, BLK), lambda i, owner: (0, 0, 0, 0)),
        ),
        out_shape=jax.ShapeDtypeStruct((N_GROUP, 2, CHUNK, BLK), BF16),
        name="reduce_route",
    )(owner, x)


def inverse_fourth_root(statistic, eye):
    matrix = statistic + RIDGE_TERM * eye
    scaling = 2.5 * lax.rsqrt(jnp.sum(matrix * matrix, keepdims=True))
    scaled = scaling * matrix
    factor = 1.25 * eye - 0.25 * scaled
    rounded = factor.astype(BF16)
    square = dot(rounded, rounded).astype(BF16)
    fourth = dot(square, square).astype(BF16)
    scaled = dot(fourth, scaled.astype(BF16))
    second = 1.25 * eye - 0.25 * scaled
    root = jnp.sqrt(jnp.sqrt(scaling))
    return root * dot(rounded, second.astype(BF16))


def block_kernel(
    refresh_ref, g_ref, r_ref, ls_ref, rs_ref, li_ref, ri_ref, upd_ref, la_ref, ra_ref, ln_ref, rn_ref
):
    grad_t = g_ref[:, 0].reshape(BLK, BLK)
    left_accum = DECAY_RATE * ls_ref[...] + (1.0 - DECAY_RATE) * dot_dims(grad_t, grad_t, TN)
    right_accum = DECAY_RATE * rs_ref[...] + (1.0 - DECAY_RATE) * dot_dims(grad_t, grad_t, NT)
    la_ref[...] = left_accum
    ra_ref[...] = right_accum

    left_root = r_ref[:, 0].reshape(BLK, BLK)
    right_root = r_ref[:, 1].reshape(BLK, BLK)
    high, low = split2(dot_dims(left_root, g_ref[:, 1].reshape(BLK, BLK), NT))
    conditioned = dot(high, right_root) + dot(low, right_root)
    mean = jnp.sum(conditioned * conditioned, keepdims=True) * (1.0 / (BLK * BLK))
    upd_ref[...] = (conditioned * lax.rsqrt(mean + SCALE_EPSILON)).astype(BF16)

    @pl.when(refresh_ref[0, 0] > 0)
    def _():
        rows = lax.broadcasted_iota(jnp.int32, (BLK, BLK), 0)
        cols = lax.broadcasted_iota(jnp.int32, (BLK, BLK), 1)
        eye = (rows == cols).astype(F32)
        ln_ref[...] = inverse_fourth_root(la_ref[...], eye)
        rn_ref[...] = inverse_fourth_root(ra_ref[...], eye)

    @pl.when(refresh_ref[0, 0] <= 0)
    def _():
        ln_ref[...] = li_ref[...]
        rn_ref[...] = ri_ref[...]


def block_step(refresh, grads, roots, left_stats, right_stats, left_inverse, right_inverse):
    vmem = pl.BlockSpec(memory_space=pltpu.VMEM)
    square = jax.ShapeDtypeStruct((BLK, BLK), F32)
    return pl.pallas_call(
        block_kernel,
        in_specs=[pl.BlockSpec(memory_space=pltpu.SMEM)] + [vmem] * 6,
        out_specs=[vmem] * 5,
        out_shape=[jax.ShapeDtypeStruct((BLK, BLK), BF16)] + [square] * 4,
        compiler_params=pltpu.CompilerParams(vmem_limit_bytes=48 * 2**20),
        cost_estimate=pl.CostEstimate(flops=2**31, bytes_accessed=11 * 2**20, transcendentals=0),
        name="block_step",
    )(refresh, grads, roots, left_stats, right_stats, left_inverse, right_inverse)


def body(inputs, norm_gain, cotangent, owners, refresh, left_stats, right_stats, left_inverse, right_inverse):
    xl = lax.axis_index("xl")
    owner = owners[0]
    fsdp = lax.axis_size(FSDP)
    tokens, width = inputs.shape

    features = lax.all_gather(inputs, ("z", "core"), axis=0, tiled=False)

    cot_own = transposed(cotangent)
    cot_other = lax.ppermute(cot_own, "xl", [(0, 1), (1, 0)])

    values = inputs.astype(F32)
    squares = jnp.sum(values * values, axis=1)
    notes = jnp.concatenate([squares, norm_gain.astype(F32)])
    notes = jnp.broadcast_to(notes, (fsdp, 1, tokens + width))
    notes = lax.all_to_all(notes, FSDP, split_axis=0, concat_axis=0, tiled=True)[:, 0]
    scales = lax.rsqrt(jnp.sum(notes[:, :tokens], axis=0) / (fsdp * width) + NORM_EPSILON)
    gains = notes[:, tokens:].reshape(2, N_GROUP // 2, 1, BLK)
    gain = lax.dynamic_index_in_dim(gains, xl, 0, keepdims=False)

    roots = jnp.stack(
        [left_inverse.reshape(N_GROUP, CHUNK, BLK), right_inverse.reshape(N_GROUP, CHUNK, BLK)], axis=1
    ).astype(BF16)
    roots = lax.all_to_all(roots, GROUP, split_axis=0, concat_axis=0, tiled=True)
    roots = pick(roots, owner)
    roots = lax.all_to_all(roots, GROUP, split_axis=0, concat_axis=0, tiled=True)

    first = xl == 0
    cot = jnp.concatenate([jnp.where(first, cot_own, cot_other), jnp.where(first, cot_other, cot_own)], axis=0)
    cot = (cot.astype(F32) * scales[None, :]).astype(BF16)

    pieces = partials(cot, features, gain)
    pieces = pieces.reshape(2 * N_GROUP, N_GROUP // 2, CHUNK, BLK)
    pieces = lax.all_to_all(pieces, ("y", "xh", "xl"), split_axis=0, concat_axis=0, tiled=True)
    grads = reduce_route(pieces.reshape(N_GROUP, N_GROUP, CHUNK, BLK), owner)
    grads = lax.all_to_all(grads, GROUP, split_axis=0, concat_axis=0, tiled=True)
    return tuple(
        block_step(refresh, grads, roots, left_stats, right_stats, left_inverse, right_inverse)
    )


def solution(mesh):
    split = Mesh(mesh.devices.reshape(4, 2, 2, 8, 2), ("y", "xh", "xl", "z", "core"))
    both = P(GROUP, FSDP)
    in_specs = (both, P(FSDP), both, P(FSDP, None), both, both, both, both, both)
    return jax.shard_map(body, mesh=split, in_specs=in_specs, out_specs=(both,) * 5, check_vma=False)
```

time: 438 us -> 217 us (0.50)
  waiting for transfers between devices: 338 us -> 115 us
  matrix products: 50 us -> 0 us
  Pallas kernels: 0 us -> 37.7 us
  starting transfers between devices: 11.2 us -> 32.8 us
    all_gather x3 -> x1, waiting for transfers between devices: 240 us -> 0.83 us  [body(): features = lax.all_gather(inputs, ('z', 'core'), axis=0, tiled=False)]
    all_to_all x1 -> x5, waiting for transfers between devices: 11.8 us -> 114 us  [the longest x1 56.8 us: body(): lax.all_to_all(pieces, ('y', 'xh', 'xl'), split_axis=0, concat_axis=0, ti...]
    reduce_scatter x1 -> x0, waiting for transfers between devices: 86.1 us -> none  [body(): lax.psum_scatter(partial_value.astype(jnp.bfloat16), 'group', scatter_dim...]
    dot_general x15 -> x0, matrix products: 50 us -> none  [the longest x1 13.8 us: body(): lax.dot_general(lax.all_gather(normed, 'fsdp', axis=1, tiled=True), cotan...]
    pallas_call x0 -> x5, Pallas kernels: none -> 37.7 us  [the longest x1 12.5 us: partials(): pl.pallas_call(partial_kernel, grid=(slabs,), in_specs=[pl.BlockSpec((2 *...]
    all_to_all x1 -> x5, starting transfers between devices: 11 us -> 30.7 us  [the longest x2 10.5 us: body(): lax.all_to_all(roots, GROUP, split_axis=0, concat_axis=0, tiled=True)]
    reduce_sum x5 -> x2, other arithmetic: 10.5 us -> 0.37 us  [the longest x1 0.34 us: body(): squares = jnp.sum(values * values, axis=1)]
    another operation x0 -> x3, other arithmetic: none -> 5.21 us
  transfers between devices with their start and end apart: 5 -> 7, of which waited for: 5 -> 5; matrix products, arithmetic and copies ran while one was open for 8% -> 5% of each run, Pallas kernels for 0% -> 13%
where the time goes in v1:
time: 217 us; the launch traced here: 216 us
  waiting for transfers between devices  115 us (53%)
  Pallas kernels  37.7 us (17%)
  starting transfers between devices  32.8 us (15%)
  between operations  14.8 us (7%)
  other arithmetic  10.2 us (5%)
  local copies, waits for them, and re-layouts  5.33 us (2%)
    all_to_all x1, waiting for transfers between devices, body(): lax.all_to_all(pieces, ('y', 'xh', 'xl'), split_axis=0, concat_axis=0, ti...  56.8 us
    all_to_all x1, waiting for transfers between devices, body(): lax.all_to_all(notes, FSDP, split_axis=0, concat_axis=0, tiled=True)[:, 0]  33.3 us
    all_to_all x1, waiting for transfers between devices, body(): lax.all_to_all(grads, GROUP, split_axis=0, concat_axis=0, tiled=True)  14.4 us
    pallas_call x1, Pallas kernels, partials(): pl.pallas_call(partial_kernel, grid=(slabs,), in_specs=[pl.BlockSpec((2 *...  12.5 us
    all_to_all x2, starting transfers between devices, body(): lax.all_to_all(roots, GROUP, split_axis=0, concat_axis=0, tiled=True)  10.5 us
    all_to_all x1, starting transfers between devices, body(): lax.all_to_all(notes, FSDP, split_axis=0, concat_axis=0, tiled=True)[:, 0]  9.57 us
    all_to_all x2, waiting for transfers between devices, body(): lax.all_to_all(roots, GROUP, split_axis=0, concat_axis=0, tiled=True)  8.93 us
    pallas_call x1, Pallas kernels, block_step(): pl.pallas_call(block_kernel, in_specs=[pl.BlockSpec(memory_space=pltpu.SM...  8.73 us
  transfers between devices with their start and end apart: 7, of which 5 were waited for; matrix products, arithmetic and copies ran while one was open for 5% of the time, Pallas kernels for 13%

profile of v1, /device:TPU:1, one launch (start us, length us, event | category | flops | bytes accessed | tf_op | source)
XLA Modules:
  0.0 215.9 jit_solution(11519529715121189130)
XLA Ops:
  7.2 0.0 copy-start.5
  7.2 0.0 all-gather.3.cloned.1.call-start
  7.2 0.7 all-gather.3.cloned.1.call-update
  7.9 4.2 %transpose.2 = bf16[512,2048]{1,0:T(8,128)(2,1)} custom-call(bf16[2048,512]{1,0:T(8,128)(2,1)} %x_ref.1), custom_call_target="tpu_custom_call" | custom-call | tf_op jit(solution)/shard_map/transpose/pallas_call | solution.py:44
  12.1 2.0 collective-permute-start
  14.2 0.0 copy-done.5
  14.2 0.3 multiply_reduce_fusion
  14.5 0.9 broadcast_in_dim.4
  15.4 9.6 %all-to-all-start = ((f32[32,1,2176]{2,1,0:T(1,128)}), f32[32,1,2176]{2,1,0:T(1,128)S(1)}, u32[]{:S(2)}, u32[]{:S(2)}) async-start(f32[32,1,2176]{2,1,0:T(1,128)} %broadcast_in_dim.4), calls=%async_computation | async-start | bytes 557056 | tf_op jit(solution)/shard_map/all_to_all | solution.py:199
  25.0 0.9 convert.8
  25.9 2.1 convert.9
  27.9 2.3 %pad_maximum_fusion = bf16[8,2,64,512]{3,2,1,0:T(8,128)(2,1)} fusion(bf16[8,1,64,512]{3,2,1,0:T(8,128)(2,1)} %bitcast.14, bf16[8,1,64,512]{3,2,1,0:T(8,128)(2,1)} %bitcast.13), kind=kLoop, calls=%fused_computation.3 | loop fusion | flops 524288 | bytes 2097152 | tf_op jit(solution)/shard_map/stack | solution.py:204
  30.2 33.3 %all-to-all-done = f32[32,1,2176]{2,1,0:T(1,128)S(1)} async-done(((f32[32,1,2176]{2,1,0:T(1,128)}), f32[32,1,2176]{2,1,0:T(1,128)S(1)}, u32[]{:S(2)}, u32[]{:S(2)}) %all-to-all-start) | async-done | bytes 278560 | tf_op jit(solution)/shard_map/all_to_all | solution.py:199
  63.6 6.9 %all-to-all-start.3 = ((bf16[8,2,64,512]{3,2,1,0:T(8,128)(2,1)}), bf16[8,2,64,512]{3,2,1,0:T(8,128)(2,1)}, u32[]{:S(2)}, u32[]{:S(2)}) async-start(bf16[8,2,64,512]{3,2,1,0:T(8,128)(2,1)} %pad_maximum_fusion), calls=%async_computation.3 | async-start | bytes 2097152 | tf_op jit(solution)/shard_map/all_to_all | solution.py:207
  70.6 0.0 collective-permute-done
  70.6 1.9 broadcast_select_fusion.1
  72.5 2.7 %multiply_convert_fusion.cot_ref = bf16[1024,2048]{1,0:T(8,128)(2,1)} fusion(bf16[512,2048]{1,0:T(8,128)(2,1)S(1)} %get-tuple-element.6, bf16[512,2048]{1,0:T(8,128)(2,1)S(1)} %get-tuple-element.5, f32[2048]{0:T(1024)S(1)} %add_rsqrt_fusion), kind=kLoop, calls=%fused_computation | loop fusion | flops 12582912 | bytes 8396800 | tf_op jit(solution)/shard_map/convert_element_type | solution.py:213
  75.2 0.8 all-gather.3.cloned.1.call-done
  76.0 12.5 %partials.1 = bf16[8,2,4,64,512]{4,3,2,1,0:T(8,128)(2,1)S(1)} custom-call(bf16[1024,2048]{1,0:T(8,128)(2,1)} %multiply_convert_fusion.cot_ref, bf16[16,2048,128]{2,1,0:T(8,128)(2,1)} %bitcast.20, f32[4,1,512]{2,1,0:T(1,128)S(1)} %dynamic-slice_bitcast_fusion.gain_ref), custom_call_target="tpu_custom_call" | custom-call | flops 8589934592 | bytes 16777216 | tf_op jit(solution)/shard_map/partials/pallas_call | solution.py:86
  88.5 2.0 copy-done
  90.4 0.0 all-to-all-done.3.x_ref
  90.4 6.6 %all-to-all-start.1 = ((bf16[16,4,64,512]{3,2,1,0:T(8,128)(2,1)}), bf16[16,4,64,512]{3,2,1,0:T(8,128)(2,1)}, u32[]{:S(2)}, u32[]{:S(2)}) async-start(bf16[16,4,64,512]{3,2,1,0:T(8,128)(2,1)} %bitcast.12), calls=%async_computation.1 | async-start | bytes 8388608 | tf_op jit(solution)/shard_map/all_to_all | solution.py:217
  97.0 5.9 %pick.1 = bf16[8,2,64,512]{3,2,1,0:T(8,128)(2,1)} custom-call(s32[8]{0:T(128)} %bitcast.18, bf16[8,2,64,512]{3,2,1,0:T(8,128)(2,1)} %all-to-all-done.3.x_ref), custom_call_target="tpu_custom_call" | custom-call | tf_op jit(solution)/shard_map/pick/pallas_call | solution.py:60
  102.9 56.8 %all-to-all-done.1 = bf16[16,4,64,512]{3,2,1,0:T(8,128)(2,1)} async-done(((bf16[16,4,64,512]{3,2,1,0:T(8,128)(2,1)}), bf16[16,4,64,512]{3,2,1,0:T(8,128)(2,1)}, u32[]{:S(2)}, u32[]{:S(2)}) %all-to-all-start.1) | async-done | bytes 4194336 | tf_op jit(solution)/shard_map/all_to_all | solution.py:217
  159.7 3.6 %all-to-all-start.4 = ((bf16[8,2,64,512]{3,2,1,0:T(8,128)(2,1)}), bf16[8,2,64,512]{3,2,1,0:T(8,128)(2,1)S(1)}, u32[]{:S(2)}, u32[]{:S(2)}) async-start(bf16[8,2,64,512]{3,2,1,0:T(8,128)(2,1)} %pick.1), calls=%async_computation.4 | async-start | bytes 2097152 | tf_op jit(solution)/shard_map/all_to_all | solution.py:209
  163.3 6.4 %reduce_route.1 = bf16[8,2,64,512]{3,2,1,0:T(8,128)(2,1)} custom-call(s32[8]{0:T(128)} %bitcast.19, bf16[8,8,64,512]{3,2,1,0:T(8,128)(2,1)} %bitcast.5.x_ref), custom_call_target="tpu_custom_call" | custom-call | tf_op jit(solution)/shard_map/reduce_route/pallas_call | solution.py:113
  169.7 8.9 %all-to-all-done.4.r_ref = bf16[8,2,64,512]{3,2,1,0:T(8,128)(2,1)S(1)} async-done(((bf16[8,2,64,512]{3,2,1,0:T(8,128)(2,1)}), bf16[8,2,64,512]{3,2,1,0:T(8,128)(2,1)S(1)}, u32[]{:S(2)}, u32[]{:S(2)}) %all-to-all-start.4) | async-done | bytes 1048608 | tf_op jit(solution)/shard_map/all_to_all | solution.py:209
  178.6 4.1 %all-to-all-start.2 = ((bf16[8,2,64,512]{3,2,1,0:T(8,128)(2,1)}), bf16[8,2,64,512]{3,2,1,0:T(8,128)(2,1)S(1)}, u32[]{:S(2)}, u32[]{:S(2)}) async-start(bf16[8,2,64,512]{3,2,1,0:T(8,128)(2,1)} %reduce_route.1), calls=%async_computation.2 | async-start | bytes 2097152 | tf_op jit(solution)/shard_map/all_to_all | solution.py:219
  183.4 14.4 %all-to-all-done.2.g_ref = bf16[8,2,64,512]{3,2,1,0:T(8,128)(2,1)S(1)} async-done(((bf16[8,2,64,512]{3,2,1,0:T(8,128)(2,1)}), bf16[8,2,64,512]{3,2,1,0:T(8,128)(2,1)S(1)}, u32[]{:S(2)}, u32[]{:S(2)}) %all-to-all-start.2) | async-done | bytes 1048608 | tf_op jit(solution)/shard_map/all_to_all | solution.py:219
  197.8 1.2 copy-done.2
  199.1 1.2 copy-done.3
  200.3 8.7 %block_step.1 = (bf16[512,512]{1,0:T(8,128)(2,1)}, f32[512,512]{1,0:T(8,128)}, f32[512,512]{1,0:T(8,128)}, f32[512,512]{1,0:T(8,128)}, f32[512,512]{1,0:T(8,128)}) custom-call(s32[1,1]{1,0:T(1,128)S(6)} %copy.18.refresh_ref, bf16[8,2,64,512]{3,2,1,0:T(8,128)(2,1)S(1)} %all-to-all-done.2.g_ref, bf16[8,2,64,512]{3,2,1,0:T(8,128)(2,1)S(1)} %all-to-all-done.4.r_ref, ...), custom_call_target="tpu_custom_call" | custom-call | flops 2147483648 | bytes 11534336 | tf_op jit(solution)/shard_map/block_step/pallas_call | solution.py:173
  (16 shorter events, 0.1 us)
Async XLA Ops:
  7.2 7.0 %copy-start.5 = (bf16[2048,128]{1,0:T(8,128)(2,1)S(1)}, bf16[2048,128]{1,0:T(8,128)(2,1)}, u32[]{:S(2)}) copy-start(bf16[2048,128]{1,0:T(8,128)(2,1)} %param.9) | copy-start | bytes 1572868
  7.2 7.0 %copy-start.6 = (bf16[128]{0:T(256)(128)(2,1)S(1)}, bf16[128]{0:T(256)(128)(2,1)}, u32[]{:S(2)}) copy-start(bf16[128]{0:T(256)(128)(2,1)} %param.10) | copy-start | bytes 772
  7.2 17.8 %copy-start.1 = (f32[512,512]{1,0:T(8,128)S(1)}, f32[512,512]{1,0:T(8,128)}, u32[]{:S(2)}) copy-start(f32[512,512]{1,0:T(8,128)} %li_ref.1) | copy-start | bytes 3145732
  7.2 68.8 %all-gather.3.cloned.1.call-start = ((), (), s32[]{:S(2)}) async-start(), calls=%async_computation.5 | async-start | bytes 8912896 | tf_op jit(solution)/shard_map/all_gather | solution.py:190
  12.1 58.4 %collective-permute-start = (bf16[512,2048]{1,0:T(8,128)(2,1)}, bf16[512,2048]{1,0:T(8,128)(2,1)}, u32[]{:S(2)}, u32[]{:S(2)}) collective-permute-start(bf16[512,2048]{1,0:T(8,128)(2,1)} %transpose.2), channel_id=1, source_target_pairs={{0,16},{16,0},{1,17},{17,1},{2,18},{18,2},{3,19},{19,3},{4,20},{20... | collective-permute-start | bytes 6291464 | tf_op jit(solution)/shard_map/ppermute | solution.py:193
  15.4 48.2 %all-to-all-start = ((f32[32,1,2176]{2,1,0:T(1,128)}), f32[32,1,2176]{2,1,0:T(1,128)S(1)}, u32[]{:S(2)}, u32[]{:S(2)}) async-start(f32[32,1,2176]{2,1,0:T(1,128)} %broadcast_in_dim.4), calls=%async_computation | async-start | bytes 557056 | tf_op jit(solution)/shard_map/all_to_all | solution.py:199
  25.0 45.6 %copy-start.4 = (bf16[512,2048]{1,0:T(8,128)(2,1)S(1)}, bf16[512,2048]{1,0:T(8,128)(2,1)}, u32[]{:S(2)}) copy-start(bf16[512,2048]{1,0:T(8,128)(2,1)} %transpose.2) | copy-start | bytes 6291460
  63.6 26.9 %all-to-all-start.3 = ((bf16[8,2,64,512]{3,2,1,0:T(8,128)(2,1)}), bf16[8,2,64,512]{3,2,1,0:T(8,128)(2,1)}, u32[]{:S(2)}, u32[]{:S(2)}) async-start(bf16[8,2,64,512]{3,2,1,0:T(8,128)(2,1)} %pad_maximum_fusion), calls=%async_computation.3 | async-start | bytes 2097152 | tf_op jit(solution)/shard_map/all_to_all | solution.py:207
  88.5 2.0 copy-start
  90.4 69.3 %all-to-all-start.1 = ((bf16[16,4,64,512]{3,2,1,0:T(8,128)(2,1)}), bf16[16,4,64,512]{3,2,1,0:T(8,128)(2,1)}, u32[]{:S(2)}, u32[]{:S(2)}) async-start(bf16[16,4,64,512]{3,2,1,0:T(8,128)(2,1)} %bitcast.12), calls=%async_computation.1 | async-start | bytes 8388608 | tf_op jit(solution)/shard_map/all_to_all | solution.py:217
  159.7 18.9 %all-to-all-start.4 = ((bf16[8,2,64,512]{3,2,1,0:T(8,128)(2,1)}), bf16[8,2,64,512]{3,2,1,0:T(8,128)(2,1)S(1)}, u32[]{:S(2)}, u32[]{:S(2)}) async-start(bf16[8,2,64,512]{3,2,1,0:T(8,128)(2,1)} %pick.1), calls=%async_computation.4 | async-start | bytes 2097152 | tf_op jit(solution)/shard_map/all_to_all | solution.py:209
  178.6 19.2 %all-to-all-start.2 = ((bf16[8,2,64,512]{3,2,1,0:T(8,128)(2,1)}), bf16[8,2,64,512]{3,2,1,0:T(8,128)(2,1)S(1)}, u32[]{:S(2)}, u32[]{:S(2)}) async-start(bf16[8,2,64,512]{3,2,1,0:T(8,128)(2,1)} %reduce_route.1), calls=%async_computation.2 | async-start | bytes 2097152 | tf_op jit(solution)/shard_map/all_to_all | solution.py:219
  197.8 1.2 copy-start.2
  199.1 1.2 copy-start.3
Sparse Core Ops, SparseCore 0:
  9.9 66.0 all-gather.2

commit v2 on v1

v2 whole, which is shorter than its diff:
```python
import jax
import jax.numpy as jnp
from jax import lax
from jax.experimental import pallas as pl
from jax.experimental.pallas import tpu as pltpu
from jax.sharding import Mesh
from jax.sharding import PartitionSpec as P

NORM_EPSILON = 1e-05
SCALE_EPSILON = 1e-06
DECAY_RATE = 0.95
RIDGE_TERM = 1e-06
BLK = 512
ITERS = 2
N_GROUP = 8
CHUNK = BLK // N_GROUP
GROUP = ("y", "xh")
FSDP = ("xl", "z", "core")
BF16 = jnp.bfloat16
F32 = jnp.float32
NT = (((1,), (1,)), ((), ()))
TN = (((0,), (0,)), ((), ()))


def dot(a, b):
    return jnp.dot(a, b, preferred_element_type=F32)


def dot_dims(a, b, dims):
    return lax.dot_general(a, b, dims, preferred_element_type=F32)


def split2(a):
    high = a.astype(BF16)
    return high, (a - high.astype(F32)).astype(BF16)


def prepare_kernel(x_ref, gain_ref, xt_ref, sq_ref):
    values = x_ref[...].astype(F32)
    xt_ref[...] = (values * gain_ref[...].astype(F32)).T.astype(BF16)
    sq_ref[...] = jnp.sum((values * values).T, axis=0, keepdims=True)


def prepare(x, gain):
    tokens, width = x.shape
    return pl.pallas_call(
        prepare_kernel,
        grid=(tokens // BLK,),
        in_specs=[pl.BlockSpec((BLK, width), lambda i: (i, 0)), pl.BlockSpec((1, width), lambda i: (0, 0))],
        out_specs=[pl.BlockSpec((width, BLK), lambda i: (0, i)), pl.BlockSpec((1, BLK), lambda i: (0, i))],
        out_shape=[jax.ShapeDtypeStruct((width, tokens), BF16), jax.ShapeDtypeStruct((1, tokens), F32)],
        name="prepare",
    )(x, gain.reshape(1, width))


def stack_roots_kernel(l_ref, r_ref, o_ref):
    o_ref[0, 0] = l_ref[...].astype(BF16)
    o_ref[0, 1] = r_ref[...].astype(BF16)


def stack_roots(left, right):
    rows = pl.BlockSpec((CHUNK, BLK), lambda i: (i, 0))
    return pl.pallas_call(
        stack_roots_kernel,
        grid=(N_GROUP,),
        in_specs=[rows, rows],
        out_specs=pl.BlockSpec((1, 2, CHUNK, BLK), lambda i: (i, 0, 0, 0)),
        out_shape=jax.ShapeDtypeStruct((N_GROUP, 2, CHUNK, BLK), BF16),
        name="stack_roots",
    )(left, right)


def pick_kernel(idx_ref, x_ref, o_ref):
    o_ref[...] = x_ref[...]


def pick(x, idx):
    rest = x.shape[1:]
    return pl.pallas_call(
        pick_kernel,
        grid_spec=pltpu.PrefetchScalarGridSpec(
            num_scalar_prefetch=1,
            grid=(x.shape[0],),
            in_specs=[pl.BlockSpec((1, *rest), lambda i, idx: (idx[i], 0, 0, 0))],
            out_specs=pl.BlockSpec((1, *rest), lambda i, idx: (i, 0, 0, 0)),
        ),
        out_shape=jax.ShapeDtypeStruct(x.shape, x.dtype),
        name="pick",
    )(idx, x)


def partial_kernel(xl_ref, x_ref, scale_ref, own_ref, other_ref, o_ref):
    rows = (x_ref[...].astype(F32) * scale_ref[...]).astype(BF16)
    for cot_ref, place in ((own_ref, xl_ref[0]), (other_ref, 1 - xl_ref[0])):
        part = dot(rows, cot_ref[...]).astype(BF16)
        for j in range(N_GROUP):
            o_ref[j, place, 0] = part[j * CHUNK : (j + 1) * CHUNK]


def partials(xl, x, scale, own, other, half):
    tokens = x.shape[1]
    whole = pl.BlockSpec((tokens, BLK), lambda i, xl: (0, 0))
    return pl.pallas_call(
        partial_kernel,
        grid_spec=pltpu.PrefetchScalarGridSpec(
            num_scalar_prefetch=1,
            grid=(2,),
            in_specs=[
                pl.BlockSpec((BLK, tokens), lambda i, xl: (2 * half + i, 0)),
                pl.BlockSpec((1, tokens), lambda i, xl: (0, 0)),
                whole,
                whole,
            ],
            out_specs=pl.BlockSpec((N_GROUP, 2, 1, CHUNK, BLK), lambda i, xl: (0, 0, i, 0, 0)),
        ),
        out_shape=pltpu.HBM((N_GROUP, 2, 2, CHUNK, BLK), BF16),
        compiler_params=pltpu.CompilerParams(vmem_limit_bytes=48 * 2**20),
        cost_estimate=pl.CostEstimate(flops=8 * tokens * BLK * BLK, bytes_accessed=10 * 2**20, transcendentals=0),
        name="partials",
    )(xl, x, scale, own, other)


def total(x_ref):
    acc = x_ref[0, 0, 0].astype(F32)
    for g in range(1, N_GROUP):
        acc = acc + x_ref[g, 0, 0].astype(F32)
    return acc.astype(BF16)


def reduce_kernel(x_ref, o_ref):
    o_ref[0] = total(x_ref)


def reduce_half(x):
    return pl.pallas_call(
        reduce_kernel,
        grid=(4,),
        in_specs=[pl.BlockSpec((N_GROUP, 1, 1, CHUNK, BLK), lambda i: (0, i // 2, i % 2, 0, 0))],
        out_specs=pl.BlockSpec((1, CHUNK, BLK), lambda i: (i, 0, 0)),
        out_shape=jax.ShapeDtypeStruct((4, CHUNK, BLK), BF16),
        name="reduce_half",
    )(x)


def route_kernel(owner_ref, first_ref, x_ref, o_ref):
    i = pl.program_id(0)

    def place(slab, value):
        o_ref[slab, 1] = value
        o_ref[owner_ref[slab], 0] = value

    slab = 4 * (i // 2) + i % 2
    place(slab, first_ref[0])
    place(slab + 2, total(x_ref))


def reduce_route(first, x, owner):
    return pl.pallas_call(
        route_kernel,
        grid_spec=pltpu.PrefetchScalarGridSpec(
            num_scalar_prefetch=1,
            grid=(4,),
            in_specs=[
                pl.BlockSpec((1, CHUNK, BLK), lambda i, owner: (i, 0, 0)),
                pl.BlockSpec((N_GROUP, 1, 1, CHUNK, BLK), lambda i, owner: (0, i // 2, i % 2, 0, 0)),
            ],
            out_specs=pl.BlockSpec((N_GROUP, 2, CHUNK, BLK), lambda i, owner: (0, 0, 0, 0)),
        ),
        out_shape=pltpu.HBM((N_GROUP, 2, CHUNK, BLK), BF16),
        name="reduce_route",
    )(owner, first, x)


def inverse_fourth_root(statistic, eye):
    matrix = statistic + RIDGE_TERM * eye
    scaling = 2.5 * lax.rsqrt(jnp.sum(matrix * matrix, keepdims=True))
    scaled = scaling * matrix
    factor = 1.25 * eye - 0.25 * scaled
    rounded = factor.astype(BF16)
    square = dot(rounded, rounded).astype(BF16)
    fourth = dot(square, square).astype(BF16)
    scaled = dot(fourth, scaled.astype(BF16))
    second = 1.25 * eye - 0.25 * scaled
    root = jnp.sqrt(jnp.sqrt(scaling))
    return root * dot(rounded, second.astype(BF16))


def block_kernel(
    refresh_ref, g_ref, r_ref, ls_ref, rs_ref, li_ref, ri_ref, upd_ref, la_ref, ra_ref, ln_ref, rn_ref
):
    grad = g_ref[:, 0].reshape(BLK, BLK)
    left_accum = DECAY_RATE * ls_ref[...] + (1.0 - DECAY_RATE) * dot_dims(grad, grad, NT)
    right_accum = DECAY_RATE * rs_ref[...] + (1.0 - DECAY_RATE) * dot_dims(grad, grad, TN)
    la_ref[...] = left_accum
    ra_ref[...] = right_accum

    left_root = r_ref[:, 0].reshape(BLK, BLK)
    right_root = r_ref[:, 1].reshape(BLK, BLK)
    high, low = split2(dot(left_root, g_ref[:, 1].reshape(BLK, BLK)))
    conditioned = dot(high, right_root) + dot(low, right_root)
    mean = jnp.sum(conditioned * conditioned, keepdims=True) * (1.0 / (BLK * BLK))
    upd_ref[...] = (conditioned * lax.rsqrt(mean + SCALE_EPSILON)).astype(BF16)

    @pl.when(refresh_ref[0, 0] > 0)
    def _():
        rows = lax.broadcasted_iota(jnp.int32, (BLK, BLK), 0)
        cols = lax.broadcasted_iota(jnp.int32, (BLK, BLK), 1)
        eye = (rows == cols).astype(F32)
        ln_ref[...] = inverse_fourth_root(la_ref[...], eye)
        rn_ref[...] = inverse_fourth_root(ra_ref[...], eye)

    @pl.when(refresh_ref[0, 0] <= 0)
    def _():
        ln_ref[...] = li_ref[...]
        rn_ref[...] = ri_ref[...]


def block_step(refresh, grads, roots, left_stats, right_stats, left_inverse, right_inverse):
    vmem = pl.BlockSpec(memory_space=pltpu.VMEM)
    square = jax.ShapeDtypeStruct((BLK, BLK), F32)
    return pl.pallas_call(
        block_kernel,
        in_specs=[pl.BlockSpec(memory_space=pltpu.SMEM)] + [vmem] * 6,
        out_specs=[vmem] * 5,
        out_shape=[jax.ShapeDtypeStruct((BLK, BLK), BF16)] + [square] * 4,
        compiler_params=pltpu.CompilerParams(vmem_limit_bytes=48 * 2**20),
        cost_estimate=pl.CostEstimate(flops=2**31, bytes_accessed=11 * 2**20, transcendentals=0),
        name="block_step",
    )(refresh, grads, roots, left_stats, right_stats, left_inverse, right_inverse)


def body(inputs, norm_gain, cotangent, owners, refresh, left_stats, right_stats, left_inverse, right_inverse):
    xl = lax.axis_index("xl").reshape(1)
    owner = owners[0]
    fsdp = lax.axis_size(FSDP)
    tokens, width = inputs.shape

    xt, squares = prepare(inputs, norm_gain)
    features = lax.all_gather(xt, ("z", "core"), axis=0, tiled=True)
    squares = jnp.broadcast_to(squares, (fsdp, tokens))
    squares, cotangent = lax.optimization_barrier((squares, cotangent))
    cot_other = lax.ppermute(cotangent, "xl", [(0, 1), (1, 0)])
    squares = lax.all_to_all(squares, FSDP, split_axis=0, concat_axis=0, tiled=True)
    squares = jnp.sum(squares, axis=0, keepdims=True)
    scale = lax.rsqrt(squares / (fsdp * width) + NORM_EPSILON)

    roots = stack_roots(left_inverse, right_inverse)
    roots, scale = lax.optimization_barrier((roots, scale))
    roots = lax.all_to_all(roots, GROUP, split_axis=0, concat_axis=0, tiled=True)
    roots = pick(roots, owner)
    roots = lax.all_to_all(roots, GROUP, split_axis=0, concat_axis=0, tiled=True)
    roots, features = lax.optimization_barrier((roots, features))

    halves = []
    for half in range(2):
        pieces = partials(xl, features, scale, cotangent, cot_other, half)
        pieces = pieces.reshape(2 * N_GROUP, 2, CHUNK, BLK)
        pieces = lax.all_to_all(pieces, ("y", "xh", "xl"), split_axis=0, concat_axis=0, tiled=True)
        halves.append(pieces.reshape(N_GROUP, 2, 2, CHUNK, BLK))
    grads = reduce_route(reduce_half(halves[0]), halves[1], owner)
    grads = lax.all_to_all(grads, GROUP, split_axis=0, concat_axis=0, tiled=True)
    return tuple(
        block_step(refresh, grads, roots, left_stats, right_stats, left_inverse, right_inverse)
    )


def solution(mesh):
    split = Mesh(mesh.devices.reshape(4, 2, 2, 8, 2), ("y", "xh", "xl", "z", "core"))
    both = P(GROUP, FSDP)
    in_specs = (both, P(FSDP), both, P(FSDP, None), both, both, both, both, both)
    return jax.shard_map(body, mesh=split, in_specs=in_specs, out_specs=(both,) * 5, check_vma=False)
```

time: 217 us -> 234 us (1.078)
  blocking collectives: 0 us -> 52.9 us
  waiting for transfers between devices: 115 us -> 77.4 us
  Pallas kernels: 37.7 us -> 48.4 us
  other arithmetic: 10.2 us -> 0.17 us
    all_to_all x0 -> x1, blocking collectives: none -> 52.9 us  [body(): lax.all_to_all(roots, GROUP, split_axis=0, concat_axis=0, tiled=True)]
    all_to_all x1, waiting for transfers between devices: 33.3 us -> 5.8 us  [body(): lax.all_to_all(squares, FSDP, split_axis=0, concat_axis=0, tiled=True)]
    all_to_all x1 -> x2, waiting for transfers between devices: 56.8 us -> 41 us  [body(): lax.all_to_all(pieces, ('y', 'xh', 'xl'), split_axis=0, concat_axis=0, ti...]
    pallas_call x3 -> x6, Pallas kernels: 23.1 us -> 33.8 us  [the longest x2 17.1 us: partials(): pl.pallas_call(partial_kernel, grid_spec=pltpu.PrefetchScalarGridSpec(num...]
    all_to_all x2 -> x1, starting transfers between devices: 10.5 us -> 3.56 us  [body(): lax.all_to_all(roots, GROUP, split_axis=0, concat_axis=0, tiled=True)]
    all_to_all x2 -> x1, waiting for transfers between devices: 8.93 us -> 15.8 us  [body(): lax.all_to_all(roots, GROUP, split_axis=0, concat_axis=0, tiled=True)]
    all_to_all x1 -> x2, starting transfers between devices: 6.58 us -> 11.8 us  [body(): lax.all_to_all(pieces, ('y', 'xh', 'xl'), split_axis=0, concat_axis=0, ti...]
    another operation x3 -> x0, other arithmetic: 5.21 us -> none
  transfers between devices with their start and end apart: 7 -> 7, of which waited for: 5 -> 5; matrix products, arithmetic and copies ran while one was open for 5% -> 0% of each run, Pallas kernels for 13% -> 10%
where the time goes in v2:
time: 234 us; the launch traced here: 232 us
  waiting for transfers between devices  77.4 us (33%)
  blocking collectives  52.9 us (23%)
  Pallas kernels  48.4 us (21%)
  starting transfers between devices  34.8 us (15%)
  between operations  14.7 us (6%)
  local copies, waits for them, and re-layouts  4.05 us (2%)
    all_to_all x1, blocking collectives, body(): lax.all_to_all(roots, GROUP, split_axis=0, concat_axis=0, tiled=True)  52.9 us
    all_to_all x2, waiting for transfers between devices, body(): lax.all_to_all(pieces, ('y', 'xh', 'xl'), split_axis=0, concat_axis=0, ti...  41 us
    pallas_call x2, Pallas kernels, partials(): pl.pallas_call(partial_kernel, grid_spec=pltpu.PrefetchScalarGridSpec(num...  17.1 us
    all_to_all x1, waiting for transfers between devices, body(): lax.all_to_all(roots, GROUP, split_axis=0, concat_axis=0, tiled=True)  15.8 us
    all_to_all x1, waiting for transfers between devices, body(): lax.all_to_all(grads, GROUP, split_axis=0, concat_axis=0, tiled=True)  14.8 us
    all_to_all x2, starting transfers between devices, body(): lax.all_to_all(pieces, ('y', 'xh', 'xl'), split_axis=0, concat_axis=0, ti...  11.8 us
    all_to_all x1, starting transfers between devices, body(): lax.all_to_all(squares, FSDP, split_axis=0, concat_axis=0, tiled=True)  11 us
    pallas_call x1, Pallas kernels, block_step(): pl.pallas_call(block_kernel, in_specs=[pl.BlockSpec(memory_space=pltpu.SM...  8.72 us
  transfers between devices with their start and end apart: 7, of which 5 were waited for; matrix products, arithmetic and copies ran while one was open for 0% of the time, Pallas kernels for 10%

profile of v2, /device:TPU:1, one launch (start us, length us, event | category | flops | bytes accessed | tf_op | source)
XLA Modules:
  0.0 232.4 jit_solution(4325860205044470475)
XLA Ops:
  7.2 0.0 all-gather.2.cloned.1.call-start
  7.2 3.4 %prepare.1 = (bf16[128,2048]{1,0:T(8,128)(2,1)}, f32[1,2048]{1,0:T(1,128)}) custom-call(bf16[2048,128]{1,0:T(8,128)(2,1)} %x_ref.1, bf16[1,128]{1,0:T(2,128)(2,1)} %bitcast.16), custom_call_target="tpu_custom_call" | custom-call | tf_op jit(solution)/shard_map/prepare/pallas_call | solution.py:46
  10.6 0.0 all-gather.2.cloned.1.call-update
  10.6 0.7 broadcast_in_dim.9
  11.3 0.9 all_to_all.21
  12.2 11.0 %all-to-all-start = ((f32[32,1,2048]{2,1,0:T(1,128)}), f32[32,1,2048]{2,1,0:T(1,128)S(1)}, u32[]{:S(2)}, u32[]{:S(2)}) async-start(f32[32,1,2048]{2,1,0:T(1,128)} %all_to_all.21), calls=%async_computation | async-start | bytes 524288 | tf_op jit(solution)/shard_map/all_to_all | solution.py:243
  23.3 1.5 collective-permute-start
  24.7 5.5 %stack_roots.1 = bf16[8,2,64,512]{3,2,1,0:T(8,128)(2,1)} custom-call(f32[512,512]{1,0:T(8,128)} %li_ref.1, f32[512,512]{1,0:T(8,128)} %ri_ref.1), custom_call_target="tpu_custom_call" | custom-call | tf_op jit(solution)/shard_map/stack_roots/pallas_call | solution.py:63
  30.3 5.8 %all-to-all-done = f32[32,1,2048]{2,1,0:T(1,128)S(1)} async-done(((f32[32,1,2048]{2,1,0:T(1,128)}), f32[32,1,2048]{2,1,0:T(1,128)S(1)}, u32[]{:S(2)}, u32[]{:S(2)}) %all-to-all-start) | async-done | bytes 262176 | tf_op jit(solution)/shard_map/all_to_all | solution.py:243
  36.1 0.2 reduce_sum.9
  36.2 52.9 %all_to_all.34.x_ref = bf16[8,2,64,512]{3,2,1,0:T(8,128)(2,1)} all-to-all(bf16[8,2,64,512]{3,2,1,0:T(8,128)(2,1)} %stack_roots.1), channel_id=1, replica_groups=mesh['y'=4,'xh'=2,'xl'=2,'z'=8,'core'=2] {'y','xh'}, dimensions={0} | all-to-all | bytes 2097152 | tf_op jit(solution)/shard_map/all_to_all | solution.py:249
  89.1 5.9 %pick.1 = bf16[8,2,64,512]{3,2,1,0:T(8,128)(2,1)} custom-call(s32[8]{0:T(128)} %bitcast.14, bf16[8,2,64,512]{3,2,1,0:T(8,128)(2,1)} %all_to_all.34.x_ref), custom_call_target="tpu_custom_call" | custom-call | tf_op jit(solution)/shard_map/pick/pallas_call | solution.py:79
  94.9 3.6 %all-to-all-start.2 = ((bf16[8,2,64,512]{3,2,1,0:T(8,128)(2,1)}), bf16[8,2,64,512]{3,2,1,0:T(8,128)(2,1)S(1)}, u32[]{:S(2)}, u32[]{:S(2)}) async-start(bf16[8,2,64,512]{3,2,1,0:T(8,128)(2,1)} %pick.1), calls=%async_computation.2 | async-start | bytes 2097152 | tf_op jit(solution)/shard_map/all_to_all | solution.py:251
  98.5 15.8 %all-to-all-done.2.r_ref = bf16[8,2,64,512]{3,2,1,0:T(8,128)(2,1)S(1)} async-done(((bf16[8,2,64,512]{3,2,1,0:T(8,128)(2,1)}), bf16[8,2,64,512]{3,2,1,0:T(8,128)(2,1)S(1)}, u32[]{:S(2)}, u32[]{:S(2)}) %all-to-all-start.2) | async-done | bytes 1048608 | tf_op jit(solution)/shard_map/all_to_all | solution.py:251
  114.3 0.0 all-gather.2.cloned.1.call-done.x_ref
  114.3 0.0 collective-permute-done.other_ref
  114.3 8.5 %partials.2 = bf16[8,2,2,64,512]{4,3,2,1,0:T(8,128)(2,1)} custom-call(s32[1]{0:T(128)} %bitcast.1.xl_ref, bf16[2048,2048]{1,0:T(8,128)(2,1)} %all-gather.2.cloned.1.call-done.x_ref, f32[1,2048]{1,0:T(1,128)S(1)} %bitcast.9, bf16[2048,512]{1,0:T(8,128)(2,1)} %own_ref.1, bf16[2048,512]{1,0:T(8,128)(2,1)} %collective-permute-done.other_ref), custom_call_target="tpu_custom_call" | custom-call | flops 4294967296 | bytes 10485760 | tf_op jit(solution)/shard_map/partials/pallas_call | solution.py:103
  122.8 4.4 %all-to-all-start.3 = ((bf16[16,2,64,512]{3,2,1,0:T(8,128)(2,1)}), bf16[16,2,64,512]{3,2,1,0:T(8,128)(2,1)}, u32[]{:S(2)}, u32[]{:S(2)}) async-start(bf16[16,2,64,512]{3,2,1,0:T(8,128)(2,1)} %bitcast.12), calls=%async_computation.3 | async-start | bytes 4194304 | tf_op jit(solution)/shard_map/all_to_all | solution.py:258
  127.3 8.6 %partials.3 = bf16[8,2,2,64,512]{4,3,2,1,0:T(8,128)(2,1)} custom-call(s32[1]{0:T(128)} %bitcast.1.xl_ref, bf16[2048,2048]{1,0:T(8,128)(2,1)} %all-gather.2.cloned.1.call-done.x_ref, f32[1,2048]{1,0:T(1,128)S(1)} %bitcast.10, bf16[2048,512]{1,0:T(8,128)(2,1)} %own_ref.1, bf16[2048,512]{1,0:T(8,128)(2,1)} %collective-permute-done.other_ref), custom_call_target="tpu_custom_call" | custom-call | flops 4294967296 | bytes 10485760 | tf_op jit(solution)/shard_map/partials/pallas_call | solution.py:103
  135.9 17.8 %all-to-all-done.3 = bf16[16,2,64,512]{3,2,1,0:T(8,128)(2,1)} async-done(((bf16[16,2,64,512]{3,2,1,0:T(8,128)(2,1)}), bf16[16,2,64,512]{3,2,1,0:T(8,128)(2,1)}, u32[]{:S(2)}, u32[]{:S(2)}) %all-to-all-start.3) | async-done | bytes 2097184 | tf_op jit(solution)/shard_map/all_to_all | solution.py:258
  153.6 7.4 %all-to-all-start.4 = ((bf16[16,2,64,512]{3,2,1,0:T(8,128)(2,1)}), bf16[16,2,64,512]{3,2,1,0:T(8,128)(2,1)}, u32[]{:S(2)}, u32[]{:S(2)}) async-start(bf16[16,2,64,512]{3,2,1,0:T(8,128)(2,1)} %bitcast.11), calls=%async_computation.4 | async-start | bytes 4194304 | tf_op jit(solution)/shard_map/all_to_all | solution.py:258
  161.0 3.5 %reduce_half.1.first_ref = bf16[4,64,512]{2,1,0:T(8,128)(2,1)} custom-call(bf16[8,2,2,64,512]{4,3,2,1,0:T(8,128)(2,1)} %bitcast.6.x_ref), custom_call_target="tpu_custom_call" | custom-call | tf_op jit(solution)/shard_map/reduce_half/pallas_call | solution.py:135
  164.6 23.2 %all-to-all-done.4 = bf16[16,2,64,512]{3,2,1,0:T(8,128)(2,1)} async-done(((bf16[16,2,64,512]{3,2,1,0:T(8,128)(2,1)}), bf16[16,2,64,512]{3,2,1,0:T(8,128)(2,1)}, u32[]{:S(2)}, u32[]{:S(2)}) %all-to-all-start.4) | async-done | bytes 2097184 | tf_op jit(solution)/shard_map/all_to_all | solution.py:258
  187.8 0.0 copy-start
  187.8 4.3 %reduce_route.1 = bf16[8,2,64,512]{3,2,1,0:T(8,128)(2,1)} custom-call(s32[8]{0:T(128)} %bitcast.15, bf16[4,64,512]{2,1,0:T(8,128)(2,1)} %reduce_half.1.first_ref, bf16[8,2,2,64,512]{4,3,2,1,0:T(8,128)(2,1)} %bitcast.8.x_ref), custom_call_target="tpu_custom_call" | custom-call | tf_op jit(solution)/shard_map/reduce_route/pallas_call | solution.py:158
  192.1 6.8 %all-to-all-start.5 = ((bf16[8,2,64,512]{3,2,1,0:T(8,128)(2,1)}), bf16[8,2,64,512]{3,2,1,0:T(8,128)(2,1)S(1)}, u32[]{:S(2)}, u32[]{:S(2)}) async-start(bf16[8,2,64,512]{3,2,1,0:T(8,128)(2,1)} %reduce_route.1), calls=%async_computation.5 | async-start | bytes 2097152 | tf_op jit(solution)/shard_map/all_to_all | solution.py:261
  199.6 14.8 %all-to-all-done.5.g_ref = bf16[8,2,64,512]{3,2,1,0:T(8,128)(2,1)S(1)} async-done(((bf16[8,2,64,512]{3,2,1,0:T(8,128)(2,1)}), bf16[8,2,64,512]{3,2,1,0:T(8,128)(2,1)S(1)}, u32[]{:S(2)}, u32[]{:S(2)}) %all-to-all-start.5) | async-done | bytes 1048608 | tf_op jit(solution)/shard_map/all_to_all | solution.py:261
  214.4 0.0 copy-done
  214.4 0.0 copy-start.1
  214.4 1.2 copy-done.1
  215.6 1.2 copy-done.2
  216.9 8.7 %block_step.1 = (bf16[512,512]{1,0:T(8,128)(2,1)}, f32[512,512]{1,0:T(8,128)}, f32[512,512]{1,0:T(8,128)}, f32[512,512]{1,0:T(8,128)}, f32[512,512]{1,0:T(8,128)}) custom-call(s32[1,1]{1,0:T(1,128)S(6)} %copy.14.refresh_ref, bf16[8,2,64,512]{3,2,1,0:T(8,128)(2,1)S(1)} %all-to-all-done.5.g_ref, bf16[8,2,64,512]{3,2,1,0:T(8,128)(2,1)S(1)} %all-to-all-done.2.r_ref, ...), custom_call_target="tpu_custom_call" | custom-call | flops 2147483648 | bytes 11534336 | tf_op jit(solution)/shard_map/block_step/pallas_call | solution.py:221
  (2 shorter events, 0.0 us)
Async XLA Ops:
  7.2 107.2 %all-gather.2.cloned.1.call-start = ((), (), s32[]{:S(2)}) async-start(), calls=%async_computation.6 | async-start | bytes 8912896 | tf_op jit(solution)/shard_map/all_gather | solution.py:239
  12.2 23.8 %all-to-all-start = ((f32[32,1,2048]{2,1,0:T(1,128)}), f32[32,1,2048]{2,1,0:T(1,128)S(1)}, u32[]{:S(2)}, u32[]{:S(2)}) async-start(f32[32,1,2048]{2,1,0:T(1,128)} %all_to_all.21), calls=%async_computation | async-start | bytes 524288 | tf_op jit(solution)/shard_map/all_to_all | solution.py:243
  23.3 91.1 %collective-permute-start = (bf16[2048,512]{1,0:T(8,128)(2,1)}, bf16[2048,512]{1,0:T(8,128)(2,1)}, u32[]{:S(2)}, u32[]{:S(2)}) collective-permute-start(bf16[2048,512]{1,0:T(8,128)(2,1)} %own_ref.1), channel_id=1, source_target_pairs={{0,16},{16,0},{1,17},{17,1},{2,18},{18,2},{3,19},{19,3},{4,20},{20... | collective-permute-start | bytes 6291464 | tf_op jit(solution)/shard_map/ppermute | solution.py:242
  94.9 19.4 %all-to-all-start.2 = ((bf16[8,2,64,512]{3,2,1,0:T(8,128)(2,1)}), bf16[8,2,64,512]{3,2,1,0:T(8,128)(2,1)S(1)}, u32[]{:S(2)}, u32[]{:S(2)}) async-start(bf16[8,2,64,512]{3,2,1,0:T(8,128)(2,1)} %pick.1), calls=%async_computation.2 | async-start | bytes 2097152 | tf_op jit(solution)/shard_map/all_to_all | solution.py:251
  122.8 30.8 %all-to-all-start.3 = ((bf16[16,2,64,512]{3,2,1,0:T(8,128)(2,1)}), bf16[16,2,64,512]{3,2,1,0:T(8,128)(2,1)}, u32[]{:S(2)}, u32[]{:S(2)}) async-start(bf16[16,2,64,512]{3,2,1,0:T(8,128)(2,1)} %bitcast.12), calls=%async_computation.3 | async-start | bytes 4194304 | tf_op jit(solution)/shard_map/all_to_all | solution.py:258
  153.6 34.2 %all-to-all-start.4 = ((bf16[16,2,64,512]{3,2,1,0:T(8,128)(2,1)}), bf16[16,2,64,512]{3,2,1,0:T(8,128)(2,1)}, u32[]{:S(2)}, u32[]{:S(2)}) async-start(bf16[16,2,64,512]{3,2,1,0:T(8,128)(2,1)} %bitcast.11), calls=%async_computation.4 | async-start | bytes 4194304 | tf_op jit(solution)/shard_map/all_to_all | solution.py:258
  187.8 26.6 %copy-start = (f32[512,512]{1,0:T(8,128)S(1)}, f32[512,512]{1,0:T(8,128)}, u32[]{:S(2)}) copy-start(f32[512,512]{1,0:T(8,128)} %li_ref.1) | copy-start | bytes 3145732
  192.1 22.3 %all-to-all-start.5 = ((bf16[8,2,64,512]{3,2,1,0:T(8,128)(2,1)}), bf16[8,2,64,512]{3,2,1,0:T(8,128)(2,1)S(1)}, u32[]{:S(2)}, u32[]{:S(2)}) async-start(bf16[8,2,64,512]{3,2,1,0:T(8,128)(2,1)} %reduce_route.1), calls=%async_computation.5 | async-start | bytes 2097152 | tf_op jit(solution)/shard_map/all_to_all | solution.py:261
  214.4 1.2 copy-start.1
  215.6 1.2 copy-start.2
Sparse Core Ops, SparseCore 0:
  10.7 63.2 all-gather.1

commit v3 on v2

v3 whole, which is shorter than its diff:
```python
import jax
import jax.numpy as jnp
from jax import lax
from jax.experimental import pallas as pl
from jax.experimental.pallas import tpu as pltpu
from jax.sharding import Mesh
from jax.sharding import PartitionSpec as P

NORM_EPSILON = 1e-05
SCALE_EPSILON = 1e-06
DECAY_RATE = 0.95
RIDGE_TERM = 1e-06
BLK = 512
N_GROUP = 8
Z = 8
CHUNK = BLK // N_GROUP
WIDTH = 128
PER_SLAB = BLK // WIDTH
ROWS = WIDTH // N_GROUP
GROUP = ("y", "xh")
FSDP = ("xl", "z", "core")
SWAP = [(0, 1), (1, 0)]
BF16 = jnp.bfloat16
F32 = jnp.float32
NT = (((1,), (1,)), ((), ()))
TN = (((0,), (0,)), ((), ()))
EARLY = (0, -1, 1, -2, 2)
LATE = (-3, 3, 4)
HBM = pl.BlockSpec(memory_space=pltpu.HBM)
VMEM = pl.BlockSpec(memory_space=pltpu.VMEM)
SMEM = pl.BlockSpec(memory_space=pltpu.SMEM)


def in_hbm(x):
    return pltpu.with_memory_space_constraint(x, pltpu.HBM)


def params():
    return pltpu.CompilerParams(vmem_limit_bytes=48 * 2**20)


def dot(a, b):
    return jnp.dot(a, b, preferred_element_type=F32)


def dot_dims(a, b, dims):
    return lax.dot_general(a, b, dims, preferred_element_type=F32)


def split2(a):
    high = a.astype(BF16)
    return high, (a - high.astype(F32)).astype(BF16)


def prepare_kernel(x_ref, gain_ref, xt_ref, sq_ref):
    values = x_ref[...].astype(F32)
    xt_ref[...] = (values * gain_ref[...].astype(F32)).astype(BF16).T
    high, low = split2(values * values)
    ones = jnp.ones((8, values.shape[1]), BF16)
    sq_ref[...] = (dot_dims(ones, high, NT) + dot_dims(ones, low, NT))[:1]


def prepare(x, gain):
    tokens, width = x.shape
    step = tokens // 2
    return pl.pallas_call(
        prepare_kernel,
        grid=(2,),
        in_specs=[pl.BlockSpec((step, width), lambda i: (i, 0)), pl.BlockSpec((1, width), lambda i: (0, 0))],
        out_specs=[pl.BlockSpec((width, step), lambda i: (0, i)), pl.BlockSpec((1, step), lambda i: (0, i))],
        out_shape=[pltpu.HBM((width, tokens), BF16), jax.ShapeDtypeStruct((1, tokens), F32)],
        name="prepare",
    )(x, gain.reshape(1, width))


def stack_roots_kernel(l_ref, r_ref, o_ref):
    for i in range(N_GROUP):
        o_ref[i, 0] = l_ref[i * CHUNK : (i + 1) * CHUNK].astype(BF16)
        o_ref[i, 1] = r_ref[i * CHUNK : (i + 1) * CHUNK].astype(BF16)


def stack_roots(left, right):
    return pl.pallas_call(
        stack_roots_kernel,
        in_specs=[VMEM, VMEM],
        out_specs=VMEM,
        out_shape=pltpu.HBM((N_GROUP, 2, CHUNK, BLK), BF16),
        compiler_params=params(),
        name="stack_roots",
    )(left, right)


def partials_kernel(sizes, steps, *refs):
    count = len(sizes)
    xl_ref, scale_ref = refs[:2]
    x_refs = refs[2 : 2 + count]
    cot_refs = refs[2 + count : 4 + count]
    o_ref, x_buf, cot_buf, sems = refs[4 + count :]
    copies, start = [], 0
    for n, (x_ref, size) in enumerate(zip(x_refs, sizes)):
        copies.append(pltpu.make_async_copy(x_ref, x_buf.at[pl.ds(start, size)], sems.at[n]))
        start += size
    cot_copies = [pltpu.make_async_copy(cot_refs[n], cot_buf.at[n], sems.at[count + n]) for n in range(2)]
    cot_copies[0].start()
    for copy in copies:
        copy.start()
    cot_copies[1].start()
    span = start // steps
    for place in range(2):
        where = xl_ref[0] if place == 0 else 1 - xl_ref[0]
        for step in range(steps):
            if place == 0:
                if step == 0:
                    cot_copies[0].wait()
                taken = 0
                for n, size in enumerate(sizes):
                    if step * span <= taken < (step + 1) * span:
                        copies[n].wait()
                    taken += size
                rows = x_buf[step * span : (step + 1) * span].astype(F32) * scale_ref[...]
                x_buf[step * span : (step + 1) * span] = rows.astype(BF16)
            elif step == 0:
                cot_copies[1].wait()
            part = dot(x_buf[step * span : (step + 1) * span], cot_buf[place]).astype(BF16)
            for block in range(span // WIDTH):
                for g in range(N_GROUP):
                    first = block * WIDTH + g * ROWS
                    o_ref[g, where, step * (span // WIDTH) + block] = part[first : first + ROWS]


def partials(xl, scale, blocks, own, other, steps):
    sizes = tuple(b.shape[0] for b in blocks)
    rows, tokens = sum(sizes), own.shape[0]
    assert rows % (steps * WIDTH) == 0
    return pl.pallas_call(
        lambda *refs: partials_kernel(sizes, steps, *refs),
        in_specs=[SMEM, VMEM] + [HBM] * (len(sizes) + 2),
        out_specs=VMEM,
        out_shape=pltpu.HBM((N_GROUP, 2, rows // WIDTH, ROWS, BLK), BF16),
        scratch_shapes=[
            pltpu.VMEM((rows, tokens), BF16),
            pltpu.VMEM((2, tokens, BLK), BF16),
            pltpu.SemaphoreType.DMA((len(sizes) + 2,)),
        ],
        compiler_params=params(),
        cost_estimate=pl.CostEstimate(flops=4 * rows * tokens * BLK, bytes_accessed=10 * 2**20, transcendentals=0),
        name="partials",
    )(xl, scale, *[in_hbm(a) for a in (*blocks, own, other)])


def total(x_ref, block):
    acc = x_ref[0, 0, block].astype(F32)
    for g in range(1, N_GROUP):
        acc = acc + x_ref[g, 0, block].astype(F32)
    return acc.astype(BF16)


def reduce_kernel(x_ref, o_ref):
    for block in range(x_ref.shape[2]):
        o_ref[0, block] = total(x_ref, block)


def reduce_early(x):
    blocks = x.shape[2]
    return pl.pallas_call(
        reduce_kernel,
        grid=(2,),
        in_specs=[pl.BlockSpec((N_GROUP, 1, blocks, ROWS, BLK), lambda i: (0, i, 0, 0, 0))],
        out_specs=pl.BlockSpec((1, blocks, ROWS, BLK), lambda i: (i, 0, 0, 0)),
        out_shape=jax.ShapeDtypeStruct((2, blocks, ROWS, BLK), BF16),
        compiler_params=params(),
        name="reduce_early",
    )(x)


def route_kernel(owner_ref, place_ref, early_ref, roots_ref, x_ref, o_ref):
    half = pl.program_id(0)

    def put(offset, mate, value):
        z = lax.rem(place_ref[0] + offset + Z, Z)
        core = place_ref[1] if mate == 0 else 1 - place_ref[1]
        block = half * 2 * Z + z * 2 + core
        slab = block // PER_SLAB
        within = lax.rem(block, PER_SLAB)
        o_ref[slab, 1, within] = value
        o_ref[owner_ref[slab], 0, within] = value

    for n, offset in enumerate(EARLY):
        for mate in range(2):
            put(offset, mate, early_ref[0, 2 * n + mate])
    for i in range(N_GROUP // 2):
        dest = half * (N_GROUP // 2) + i
        o_ref[dest, 2] = roots_ref[owner_ref[dest], 0]
        o_ref[dest, 3] = roots_ref[owner_ref[dest], 1]
    for n, offset in enumerate(LATE):
        for mate in range(2):
            put(offset, mate, total(x_ref, 2 * n + mate))


def route(owner, place, early, roots, late):
    return pl.pallas_call(
        route_kernel,
        grid_spec=pltpu.PrefetchScalarGridSpec(
            num_scalar_prefetch=2,
            grid=(2,),
            in_specs=[
                pl.BlockSpec((1, *early.shape[1:]), lambda i, *s: (i, 0, 0, 0)),
                pl.BlockSpec(roots.shape, lambda i, *s: (0, 0, 0, 0, 0)),
                pl.BlockSpec((N_GROUP, 1, *late.shape[2:]), lambda i, *s: (0, i, 0, 0, 0)),
            ],
            out_specs=pl.BlockSpec((N_GROUP, 4, PER_SLAB, ROWS, BLK), lambda i, *s: (0, 0, 0, 0, 0)),
        ),
        out_shape=pltpu.HBM((N_GROUP, 4, PER_SLAB, ROWS, BLK), BF16),
        compiler_params=params(),
        name="route",
    )(owner, place, early, roots, late)


def inverse_fourth_root(statistic):
    rows = lax.broadcasted_iota(jnp.int32, (BLK, BLK), 0)
    cols = lax.broadcasted_iota(jnp.int32, (BLK, BLK), 1)
    eye = (rows == cols).astype(F32)
    matrix = statistic + RIDGE_TERM * eye
    scaling = 2.5 * lax.rsqrt(jnp.sum(matrix * matrix, keepdims=True))
    scaled = scaling * matrix
    factor = (1.25 * eye - 0.25 * scaled).astype(BF16)
    square = dot(factor, factor).astype(BF16)
    fourth = dot(square, square).astype(BF16)
    second = 1.25 * eye - 0.25 * dot(fourth, scaled.astype(BF16))
    return jnp.sqrt(jnp.sqrt(scaling)) * dot(factor, second.astype(BF16))


def block_kernel(
    refresh_ref, u_ref, ls_ref, rs_ref, li_ref, ri_ref, upd_ref, la_ref, ra_ref, ln_ref, rn_ref,
    left, right, left_new, right_new, grad, natural, sems,
):
    loads = [pltpu.make_async_copy(ls_ref, left, sems.at[0]), pltpu.make_async_copy(rs_ref, right, sems.at[1])]
    for load in loads:
        load.start()
    fresh = refresh_ref[0, 0] > 0
    keeps = [pltpu.make_async_copy(li_ref, ln_ref, sems.at[2]), pltpu.make_async_copy(ri_ref, rn_ref, sems.at[3])]

    @pl.when(jnp.logical_not(fresh))
    def _():
        for keep in keeps:
            keep.start()

    for i in range(PER_SLAB):
        for g in range(N_GROUP):
            first = i * WIDTH + g * ROWS
            grad[first : first + ROWS] = u_ref[g, 0, i]
            natural[first : first + ROWS] = u_ref[g, 1, i]

    stores = [pltpu.make_async_copy(left, la_ref, sems.at[4]), pltpu.make_async_copy(right, ra_ref, sems.at[5])]
    news = [pltpu.make_async_copy(left_new, ln_ref, sems.at[2]), pltpu.make_async_copy(right_new, rn_ref, sems.at[3])]
    for n, (accum, dims) in enumerate(((left, NT), (right, TN))):
        gram = dot_dims(grad[...], grad[...], dims)
        loads[n].wait()
        accum[...] = DECAY_RATE * accum[...] + (1.0 - DECAY_RATE) * gram
        stores[n].start()

    @pl.when(fresh)
    def _():
        for accum, new, copy in ((left, left_new, news[0]), (right, right_new, news[1])):
            new[...] = inverse_fourth_root(accum[...])
            copy.start()

    left_root = u_ref[:, 2].reshape(BLK, BLK)
    right_root = u_ref[:, 3].reshape(BLK, BLK)
    high, low = split2(dot(left_root, natural[...]))
    conditioned = dot(high, right_root) + dot(low, right_root)
    mean = jnp.sum(conditioned * conditioned, keepdims=True) * (1.0 / (BLK * BLK))
    upd_ref[...] = (conditioned * lax.rsqrt(mean + SCALE_EPSILON)).astype(BF16)

    for store in stores:
        store.wait()

    @pl.when(fresh)
    def _():
        for new in news:
            new.wait()

    @pl.when(jnp.logical_not(fresh))
    def _():
        for keep in keeps:
            keep.wait()


def block_step(refresh, received, left_stats, right_stats, left_inverse, right_inverse):
    square = pltpu.HBM((BLK, BLK), F32)
    return pl.pallas_call(
        block_kernel,
        in_specs=[SMEM, VMEM] + [HBM] * 4,
        out_specs=[VMEM] + [HBM] * 4,
        out_shape=[jax.ShapeDtypeStruct((BLK, BLK), BF16)] + [square] * 4,
        scratch_shapes=[pltpu.VMEM((BLK, BLK), F32)] * 4
        + [pltpu.VMEM((BLK, BLK), BF16)] * 2
        + [pltpu.SemaphoreType.DMA((6,))],
        compiler_params=params(),
        cost_estimate=pl.CostEstimate(flops=2**31, bytes_accessed=11 * 2**20, transcendentals=0),
        name="block_step",
    )(refresh, received, *[in_hbm(a) for a in (left_stats, right_stats, left_inverse, right_inverse)])


def shift(x, axis, by):
    size = lax.axis_size(axis)
    return lax.ppermute(x, axis, [(i, (i + by) % size) for i in range(size)])


def mate(x):
    return lax.ppermute(x, "core", SWAP)


def ring(block, squares):
    up = down = block
    order = [block, mate(block)]
    for step in range(3):
        up, down = shift(up, "z", 1), shift(down, "z", -1)
        if step == 0:
            up, down, squares = lax.optimization_barrier((up, down, squares))
        order += [up, mate(up), down, mate(down)]
    half = WIDTH // 2
    last = [shift(up[:half], "z", 1), shift(down[half:], "z", -1)]
    order += last + [mate(part) for part in last]
    return order[: 2 * len(EARLY)], order[2 * len(EARLY) :], squares


def body(inputs, norm_gain, cotangent, owners, refresh, left_stats, right_stats, left_inverse, right_inverse):
    xl, z, core = (lax.axis_index(name) for name in FSDP)
    owner = owners[0]
    tokens, width = inputs.shape
    features = lax.axis_size(FSDP) * width

    other = lax.ppermute(cotangent, "xl", SWAP)
    block, squares = prepare(inputs, norm_gain)

    peers = lax.axis_size(("z", "core"))
    squares = jnp.broadcast_to(squares, (peers, tokens))
    squares = lax.all_to_all(squares, ("z", "core"), split_axis=0, concat_axis=0, tiled=True)
    squares = jnp.sum(squares, axis=0, keepdims=True)
    early, late, squares = ring(block, squares)

    roots = stack_roots(left_inverse, right_inverse)
    roots, squares = lax.optimization_barrier((roots, squares))
    roots = lax.all_to_all(roots, GROUP, split_axis=0, concat_axis=0, tiled=True)
    early, late[0], late[2], squares = lax.optimization_barrier((early, late[0], late[2], squares))
    scale = lax.rsqrt((squares + lax.ppermute(squares, "xl", SWAP)) / features + NORM_EPSILON)

    received = []
    for blocks, steps in ((early, 2), (late, 1)):
        pieces = partials(xl.reshape(1), scale, blocks, cotangent, other, steps)
        shape = pieces.shape
        pieces = pieces.reshape(2 * N_GROUP, *shape[2:])
        pieces = lax.all_to_all(pieces, ("y", "xh", "xl"), split_axis=0, concat_axis=0, tiled=True)
        received.append(pieces.reshape(shape))
    roots = roots.reshape(N_GROUP, 2, PER_SLAB, ROWS, BLK)
    sent = route(owner, jnp.stack([z, core]), reduce_early(received[0]), roots, received[1])
    sent = lax.all_to_all(sent, GROUP, split_axis=0, concat_axis=0, tiled=True)
    return tuple(block_step(refresh, sent, left_stats, right_stats, left_inverse, right_inverse))


def solution(mesh):
    split = Mesh(mesh.devices.reshape(4, 2, 2, 8, 2), ("y", "xh", "xl", "z", "core"))
    both = P(GROUP, FSDP)
    in_specs = (both, P(FSDP), both, P(FSDP, None), both, both, both, both, both)
    return jax.shard_map(body, mesh=split, in_specs=in_specs, out_specs=(both,) * 5, check_vma=False)
```

time: 234 us -> 251 us (1.073)
  Pallas kernels: 48.4 us -> 89.9 us
  blocking collectives: 52.9 us -> 14.2 us
  starting transfers between devices: 34.8 us -> 48.8 us
  between operations: 14.7 us -> 1.69 us
  waiting for transfers between devices: 77.4 us -> 87.2 us
  local copies, waits for them, and re-layouts: 4.05 us -> 8.09 us
    pallas_call x8 -> x7, Pallas kernels: 48.4 us -> 89.9 us  [the longest x1 65.5 us: block_step(): pl.pallas_call(block_kernel, in_specs=[SMEM, VMEM] + [HBM] * 4, out_specs...]
    all_to_all x1, blocking collectives: 52.9 us -> 14.2 us  [body(): lax.all_to_all(squares, ('z', 'core'), split_axis=0, concat_axis=0, tiled...]
    ppermute x1 -> x19, starting transfers between devices: 1.48 us -> 26.7 us  [the longest x8 14.8 us: shift(): return lax.ppermute(x, axis, [(i, (i + by) % size) for i in range(size)])]
    ppermute x1 -> x19, waiting for transfers between devices: 0.01 us -> 21.3 us  [the longest x8 20.1 us: shift(): return lax.ppermute(x, axis, [(i, (i + by) % size) for i in range(size)])]
    all_to_all x2 -> x1, starting transfers between devices: 17.9 us -> 5.54 us  [body(): sent = lax.all_to_all(sent, GROUP, split_axis=0, concat_axis=0, tiled=True)]
    all_to_all x1, waiting for transfers between devices: 15.8 us -> 5.61 us  [body(): lax.all_to_all(roots, GROUP, split_axis=0, concat_axis=0, tiled=True)]
    all_to_all x2, waiting for transfers between devices: 41 us -> 34.4 us  [body(): lax.all_to_all(pieces, ('y', 'xh', 'xl'), split_axis=0, concat_axis=0, ti...]
    all_to_all x2 -> x1, waiting for transfers between devices: 20.6 us -> 25.9 us  [body(): sent = lax.all_to_all(sent, GROUP, split_axis=0, concat_axis=0, tiled=True)]
  transfers between devices with their start and end apart: 7 -> 23, of which waited for: 5 -> 10; matrix products, arithmetic and copies ran while one was open for 0% -> 1% of each run, Pallas kernels for 10% -> 8%
where the time goes in v3:
time: 251 us; the launch traced here: 250 us
  Pallas kernels  89.9 us (36%)
  waiting for transfers between devices  87.2 us (35%)
  starting transfers between devices  48.8 us (19%)
  blocking collectives  14.2 us (6%)
  local copies, waits for them, and re-layouts  8.09 us (3%)
    pallas_call x1, Pallas kernels, block_step(): pl.pallas_call(block_kernel, in_specs=[SMEM, VMEM] + [HBM] * 4, out_specs...  65.5 us
    all_to_all x2, waiting for transfers between devices, body(): lax.all_to_all(pieces, ('y', 'xh', 'xl'), split_axis=0, concat_axis=0, ti...  34.4 us
    all_to_all x1, waiting for transfers between devices, body(): sent = lax.all_to_all(sent, GROUP, split_axis=0, concat_axis=0, tiled=True)  25.9 us
    ppermute x8, waiting for transfers between devices, shift(): return lax.ppermute(x, axis, [(i, (i + by) % size) for i in range(size)])  20.1 us
    pallas_call x2, Pallas kernels, partials(): pl.pallas_call(lambda *refs: partials_kernel(sizes, steps, *refs), in_spe...  17.2 us
    ppermute x8, starting transfers between devices, shift(): return lax.ppermute(x, axis, [(i, (i + by) % size) for i in range(size)])  14.8 us
    all_to_all x1, blocking collectives, body(): lax.all_to_all(squares, ('z', 'core'), split_axis=0, concat_axis=0, tiled...  14.2 us
    all_to_all x2, starting transfers between devices, body(): lax.all_to_all(pieces, ('y', 'xh', 'xl'), split_axis=0, concat_axis=0, ti...  9.87 us
  transfers between devices with their start and end apart: 23, of which 10 were waited for; matrix products, arithmetic and copies ran while one was open for 1% of the time, Pallas kernels for 8%

profile of v3, /device:TPU:1, one launch (start us, length us, event | category | flops | bytes accessed | tf_op | source)
XLA Modules:
  0.0 250.1 jit_solution(15711067386437980470)
XLA Ops:
  0.6 2.1 collective-permute-start.12
  2.8 2.1 prepare.1
  4.9 1.6 collective-permute-start.1
  6.5 3.9 %collective-permute-start.2 = (bf16[128,2048]{1,0:T(8,128)(2,1)}, bf16[128,2048]{1,0:T(8,128)(2,1)S(1)}, u32[]{:S(2)}, u32[]{:S(2)}) collective-permute-start(bf16[128,2048]{1,0:T(8,128)(2,1)} %get-tuple-element.32.refs_2_), channel_id=1, source_target_pairs={{0,14},{2,0},{4,2},{6,4},{8,6},{10,8},{12,10},{14,12},{1,15},{3,1}... | collective-permute-start | bytes 1572872 | tf_op jit(solution)/shard_map/ppermute | solution.py:307
  10.5 1.2 collective-permute-start
  12.5 14.2 %all_to_all.26 = f32[16,1,2048]{2,1,0:T(1,128)S(1)} all-to-all(f32[16,1,2048]{2,1,0:T(1,128)S(1)} %broadcast_in_dim.8), channel_id=1, replica_groups=mesh['y'=4,'xh'=2,'xl'=2,'z'=8,'core'=2] {'z','core'}, dimensions={0} | all-to-all | bytes 262144 | tf_op jit(solution)/shard_map/all_to_all | solution.py:339
  26.8 3.2 %collective-permute-start.5 = (bf16[128,2048]{1,0:T(8,128)(2,1)S(1)}, bf16[128,2048]{1,0:T(8,128)(2,1)S(1)}, u32[]{:S(2)}, u32[]{:S(2)}) collective-permute-start(bf16[128,2048]{1,0:T(8,128)(2,1)S(1)} %collective-permute-done.1.refs_4_), channel_id=1, source_target_pairs={{0,2},{2,4},{4,6},{6,8},{8,10},{10,12},{12,14},{14,0},{1,3},{3,5},... | collective-permute-start | bytes 1572872 | tf_op jit(solution)/shard_map/ppermute | solution.py:307
  30.8 10.8 %collective-permute-done.5.refs_8_ = bf16[128,2048]{1,0:T(8,128)(2,1)S(1)} collective-permute-done((bf16[128,2048]{1,0:T(8,128)(2,1)S(1)}, bf16[128,2048]{1,0:T(8,128)(2,1)S(1)}, u32[]{:S(2)}, u32[]{:S(2)}) %collective-permute-start.5) | collective-permute-done | bytes 524320 | tf_op jit(solution)/shard_map/ppermute | solution.py:307
  42.5 1.9 collective-permute-start.9
  45.1 1.2 collective-permute-start.10
  46.3 1.2 copy-done.2
  47.5 1.2 copy-done.3
  48.8 1.1 stack_roots.1
  49.8 7.3 %collective-permute-done.9.refs_2_ = bf16[128,2048]{1,0:T(8,128)(2,1)S(1)} collective-permute-done((bf16[128,2048]{1,0:T(8,128)(2,1)S(1)}, bf16[128,2048]{1,0:T(8,128)(2,1)S(1)}, u32[]{:S(2)}, u32[]{:S(2)}) %collective-permute-start.9) | collective-permute-done | bytes 524320 | tf_op jit(solution)/shard_map/ppermute | solution.py:307
  57.2 1.5 collective-permute-done.10.refs_4_
  59.0 6.7 %all-to-all-start.2 = ((bf16[8,2,64,512]{3,2,1,0:T(8,128)(2,1)}), bf16[8,2,64,512]{3,2,1,0:T(8,128)(2,1)S(1)}, u32[]{:S(2)}, u32[]{:S(2)}) async-start(bf16[8,2,64,512]{3,2,1,0:T(8,128)(2,1)} %stack_roots.1), calls=%async_computation.2 | async-start | bytes 2097152 | tf_op jit(solution)/shard_map/all_to_all | solution.py:345
  65.7 9.9 %partials.2 = bf16[8,2,10,16,512]{4,3,2,1,0:T(8,128)(2,1)} custom-call(s32[1]{0:T(128)} %bitcast.3.refs_0_, f32[1,2048]{1,0:T(1,128)S(1)} %add_rsqrt_fusion.refs_1_, bf16[128,2048]{1,0:T(8,128)(2,1)} %get-tuple-element.32.refs_2_, bf16[128,2048]{1,0:T(8,128)(2,1)} %copy-done.8, bf16[128,2048]{1,0:T(8,128)(2,1)} %copy-done.6, bf16[128,2048]{1,0:T(8,128)(2,1)} %copy-done.10, ...), custom_call_target="tpu_custom_call" | custom-call | flops 5368709120 | bytes 10485760 | tf_op jit(solution)/shard_map/partials/pallas_call | solution.py:135
  75.5 5.6 %all-to-all-done.2 = bf16[8,2,64,512]{3,2,1,0:T(8,128)(2,1)S(1)} async-done(((bf16[8,2,64,512]{3,2,1,0:T(8,128)(2,1)}), bf16[8,2,64,512]{3,2,1,0:T(8,128)(2,1)S(1)}, u32[]{:S(2)}, u32[]{:S(2)}) %all-to-all-start.2) | async-done | bytes 1048608 | tf_op jit(solution)/shard_map/all_to_all | solution.py:345
  81.2 1.0 copy-done
  82.1 4.3 %all-to-all-start.1 = ((bf16[16,10,16,512]{3,2,1,0:T(8,128)(2,1)}), bf16[16,10,16,512]{3,2,1,0:T(8,128)(2,1)S(1)}, u32[]{:S(2)}, u32[]{:S(2)}) async-start(bf16[16,10,16,512]{3,2,1,0:T(8,128)(2,1)} %bitcast.15), calls=%async_computation.1 | async-start | bytes 5242880 | tf_op jit(solution)/shard_map/all_to_all | solution.py:354
  87.8 2.4 collective-permute-start.16
  90.2 2.7 %collective-permute-start.13 = (bf16[128,2048]{1,0:T(8,128)(2,1)S(1)}, bf16[128,2048]{1,0:T(8,128)(2,1)S(1)}, u32[]{:S(2)}, u32[]{:S(2)}) collective-permute-start(bf16[128,2048]{1,0:T(8,128)(2,1)S(1)} %collective-permute-done.9.refs_2_), channel_id=1, source_target_pairs={{0,1},{1,0},{2,3},{3,2},{4,5},{5,4},{6,7},{7,6},{8,9},{9,8},{10,11... | collective-permute-start | bytes 1572872 | tf_op jit(solution)/shard_map/ppermute | solution.py:311
  93.4 3.0 %collective-permute-start.17 = (bf16[64,2048]{1,0:T(8,128)(2,1)S(1)}, bf16[64,2048]{1,0:T(8,128)(2,1)S(1)}, u32[]{:S(2)}, u32[]{:S(2)}) collective-permute-start(bf16[64,2048]{1,0:T(8,128)(2,1)S(1)} %collective-permute-done.15.refs_6_), channel_id=1, source_target_pairs={{0,1},{1,0},{2,3},{3,2},{4,5},{5,4},{6,7},{7,6},{8,9},{9,8},{10,11... | collective-permute-start | bytes 786440 | tf_op jit(solution)/shard_map/ppermute | solution.py:311
  99.6 7.3 %partials.3 = bf16[8,2,6,16,512]{4,3,2,1,0:T(8,128)(2,1)} custom-call(s32[1]{0:T(128)} %bitcast.3.refs_0_, f32[1,2048]{1,0:T(1,128)S(1)} %add_rsqrt_fusion.refs_1_, bf16[128,2048]{1,0:T(8,128)(2,1)} %copy-done.5, bf16[128,2048]{1,0:T(8,128)(2,1)} %copy-done.15, bf16[128,2048]{1,0:T(8,128)(2,1)} %collective-permute-done.10.refs_4_, ...), custom_call_target="tpu_custom_call" | custom-call | flops 3221225472 | bytes 10485760 | tf_op jit(solution)/shard_map/partials/pallas_call | solution.py:135
  107.0 14.4 %all-to-all-done.1 = bf16[16,10,16,512]{3,2,1,0:T(8,128)(2,1)S(1)} async-done(((bf16[16,10,16,512]{3,2,1,0:T(8,128)(2,1)}), bf16[16,10,16,512]{3,2,1,0:T(8,128)(2,1)S(1)}, u32[]{:S(2)}, u32[]{:S(2)}) %all-to-all-start.1) | async-done | bytes 2621472 | tf_op jit(solution)/shard_map/all_to_all | solution.py:354
  121.4 5.6 %all-to-all-start.3 = ((bf16[16,6,16,512]{3,2,1,0:T(8,128)(2,1)}), bf16[16,6,16,512]{3,2,1,0:T(8,128)(2,1)}, u32[]{:S(2)}, u32[]{:S(2)}) async-start(bf16[16,6,16,512]{3,2,1,0:T(8,128)(2,1)} %bitcast.16), calls=%async_computation.3 | async-start | bytes 3145728 | tf_op jit(solution)/shard_map/all_to_all | solution.py:354
  127.7 20.0 %all-to-all-done.3 = bf16[16,6,16,512]{3,2,1,0:T(8,128)(2,1)} async-done(((bf16[16,6,16,512]{3,2,1,0:T(8,128)(2,1)}), bf16[16,6,16,512]{3,2,1,0:T(8,128)(2,1)}, u32[]{:S(2)}, u32[]{:S(2)}) %all-to-all-start.3) | async-done | bytes 1572896 | tf_op jit(solution)/shard_map/all_to_all | solution.py:354
  147.7 1.2 copy-done.1
  148.9 3.5 %route.1 = bf16[8,4,4,16,512]{4,3,2,1,0:T(8,128)(2,1)} custom-call(s32[8]{0:T(128)S(1)} %bitcast.14, s32[2]{0:T(128)S(1)} %pad_add_fusion.place_ref, bf16[2,10,16,512]{3,2,1,0:T(8,128)(2,1)S(1)} %reduce_early.1.early_ref, bf16[8,2,4,16,512]{4,3,2,1,0:T(8,128)(2,1)S(1)} %bitcast.13, bf16[8,2,6,16,512]{4,3,2,1,0:T(8,128)(2,1)} %bitcast.11.x_ref), custom_call_target="tpu_custom_call" | custom-call | tf_op jit(solution)/shard_map/route/pallas_call | solution.py:201
  152.4 5.5 %all-to-all-start.4 = ((bf16[8,4,4,16,512]{4,3,2,1,0:T(8,128)(2,1)}), bf16[8,4,4,16,512]{4,3,2,1,0:T(8,128)(2,1)S(1)}, u32[]{:S(2)}, u32[]{:S(2)}) async-start(bf16[8,4,4,16,512]{4,3,2,1,0:T(8,128)(2,1)} %route.1), calls=%async_computation.4 | async-start | bytes 4194304 | tf_op jit(solution)/shard_map/all_to_all | solution.py:358
  158.6 25.9 %all-to-all-done.4.u_ref = bf16[8,4,4,16,512]{4,3,2,1,0:T(8,128)(2,1)S(1)} async-done(((bf16[8,4,4,16,512]{4,3,2,1,0:T(8,128)(2,1)}), bf16[8,4,4,16,512]{4,3,2,1,0:T(8,128)(2,1)S(1)}, u32[]{:S(2)}, u32[]{:S(2)}) %all-to-all-start.4) | async-done | bytes 2097184 | tf_op jit(solution)/shard_map/all_to_all | solution.py:358
  184.5 65.5 %block_step.1 = (bf16[512,512]{1,0:T(8,128)(2,1)}, f32[512,512]{1,0:T(8,128)}, f32[512,512]{1,0:T(8,128)}, f32[512,512]{1,0:T(8,128)}, f32[512,512]{1,0:T(8,128)}) custom-call(s32[1,1]{1,0:T(1,128)S(6)} %copy.16.refresh_ref, bf16[8,4,4,16,512]{4,3,2,1,0:T(8,128)(2,1)S(1)} %all-to-all-done.4.u_ref, f32[512,512]{1,0:T(8,128)} %ls_ref.1, f32[512,512]{1,0:T(8,128)} %rs_ref.1, ...), custom_call_target="tpu_custom_call" | custom-call | flops 2147483648 | bytes 11534336 | tf_op jit(solution)/shard_map/block_step/pallas_call | solution.py:291
  (70 shorter events, 9.2 us)
Async XLA Ops:
  0.6 65.0 %collective-permute-start.12 = (bf16[2048,512]{1,0:T(8,128)(2,1)}, bf16[2048,512]{1,0:T(8,128)(2,1)}, u32[]{:S(2)}, u32[]{:S(2)}) collective-permute-start(bf16[2048,512]{1,0:T(8,128)(2,1)} %refs_10_.1), channel_id=1, source_target_pairs={{0,16},{16,0},{1,17},{17,1},{2,18},{18,2},{3,19},{19,3},{4,20},{20... | collective-permute-start | bytes 6291464 | tf_op jit(solution)/shard_map/ppermute | solution.py:334
  4.9 21.9 %collective-permute-start.1 = (bf16[128,2048]{1,0:T(8,128)(2,1)}, bf16[128,2048]{1,0:T(8,128)(2,1)S(1)}, u32[]{:S(2)}, u32[]{:S(2)}) collective-permute-start(bf16[128,2048]{1,0:T(8,128)(2,1)} %get-tuple-element.32.refs_2_), channel_id=1, source_target_pairs={{0,2},{2,4},{4,6},{6,8},{8,10},{10,12},{12,14},{14,0},{1,3},{3,5},... | collective-permute-start | bytes 1572872 | tf_op jit(solution)/shard_map/ppermute | solution.py:307
  6.5 20.3 %collective-permute-start.2 = (bf16[128,2048]{1,0:T(8,128)(2,1)}, bf16[128,2048]{1,0:T(8,128)(2,1)S(1)}, u32[]{:S(2)}, u32[]{:S(2)}) collective-permute-start(bf16[128,2048]{1,0:T(8,128)(2,1)} %get-tuple-element.32.refs_2_), channel_id=1, source_target_pairs={{0,14},{2,0},{4,2},{6,4},{8,6},{10,8},{12,10},{14,12},{1,15},{3,1}... | collective-permute-start | bytes 1572872 | tf_op jit(solution)/shard_map/ppermute | solution.py:307
  10.5 20.2 %collective-permute-start = (bf16[128,2048]{1,0:T(8,128)(2,1)}, bf16[128,2048]{1,0:T(8,128)(2,1)S(1)}, u32[]{:S(2)}, u32[]{:S(2)}) collective-permute-start(bf16[128,2048]{1,0:T(8,128)(2,1)} %get-tuple-element.32.refs_2_), channel_id=1, source_target_pairs={{0,1},{1,0},{2,3},{3,2},{4,5},{5,4},{6,7},{7,6},{8,9},{9,8},{10,11... | collective-permute-start | bytes 1572872 | tf_op jit(solution)/shard_map/ppermute | solution.py:311
  26.8 32.1 %copy-start.6 = (bf16[128,2048]{1,0:T(8,128)(2,1)}, bf16[128,2048]{1,0:T(8,128)(2,1)S(1)}, u32[]{:S(2)}) copy-start(bf16[128,2048]{1,0:T(8,128)(2,1)S(1)} %collective-permute-done.1.refs_4_) | copy-start | bytes 1572868
  26.8 32.1 %copy-start.7 = (bf16[128,2048]{1,0:T(8,128)(2,1)}, bf16[128,2048]{1,0:T(8,128)(2,1)S(1)}, u32[]{:S(2)}) copy-start(bf16[128,2048]{1,0:T(8,128)(2,1)S(1)} %collective-permute-done.2.refs_6_) | copy-start | bytes 1572868
  26.8 14.8 %collective-permute-start.5 = (bf16[128,2048]{1,0:T(8,128)(2,1)S(1)}, bf16[128,2048]{1,0:T(8,128)(2,1)S(1)}, u32[]{:S(2)}, u32[]{:S(2)}) collective-permute-start(bf16[128,2048]{1,0:T(8,128)(2,1)S(1)} %collective-permute-done.1.refs_4_), channel_id=1, source_target_pairs={{0,2},{2,4},{4,6},{6,8},{8,10},{10,12},{12,14},{14,0},{1,3},{3,5},... | collective-permute-start | bytes 1572872 | tf_op jit(solution)/shard_map/ppermute | solution.py:307
  30.1 12.4 %collective-permute-start.3 = (bf16[128,2048]{1,0:T(8,128)(2,1)S(1)}, bf16[128,2048]{1,0:T(8,128)(2,1)S(1)}, u32[]{:S(2)}, u32[]{:S(2)}) collective-permute-start(bf16[128,2048]{1,0:T(8,128)(2,1)S(1)} %collective-permute-done.1.refs_4_), channel_id=1, source_target_pairs={{0,1},{1,0},{2,3},{3,2},{4,5},{5,4},{6,7},{7,6},{8,9},{9,8},{10,11... | collective-permute-start | bytes 1572872 | tf_op jit(solution)/shard_map/ppermute | solution.py:311
  30.7 13.7 %collective-permute-start.7 = (bf16[128,2048]{1,0:T(8,128)(2,1)S(1)}, bf16[128,2048]{1,0:T(8,128)(2,1)S(1)}, u32[]{:S(2)}, u32[]{:S(2)}) collective-permute-start(bf16[128,2048]{1,0:T(8,128)(2,1)S(1)} %collective-permute-done.2.refs_6_), channel_id=1, source_target_pairs={{0,14},{2,0},{4,2},{6,4},{8,6},{10,8},{12,10},{14,12},{1,15},{3,1}... | collective-permute-start | bytes 1572872 | tf_op jit(solution)/shard_map/ppermute | solution.py:307
  30.7 28.2 %copy-start.8 = (bf16[128,2048]{1,0:T(8,128)(2,1)}, bf16[128,2048]{1,0:T(8,128)(2,1)S(1)}, u32[]{:S(2)}) copy-start(bf16[128,2048]{1,0:T(8,128)(2,1)S(1)} %collective-permute-done.refs_3_) | copy-start | bytes 1572868
  30.7 14.3 %collective-permute-start.4 = (bf16[128,2048]{1,0:T(8,128)(2,1)S(1)}, bf16[128,2048]{1,0:T(8,128)(2,1)S(1)}, u32[]{:S(2)}, u32[]{:S(2)}) collective-permute-start(bf16[128,2048]{1,0:T(8,128)(2,1)S(1)} %collective-permute-done.2.refs_6_), channel_id=1, source_target_pairs={{0,1},{1,0},{2,3},{3,2},{4,5},{5,4},{6,7},{7,6},{8,9},{9,8},{10,11... | collective-permute-start | bytes 1572872 | tf_op jit(solution)/shard_map/ppermute | solution.py:311
  41.7 15.5 %copy-start.9 = (bf16[128,2048]{1,0:T(8,128)(2,1)}, bf16[128,2048]{1,0:T(8,128)(2,1)S(1)}, u32[]{:S(2)}) copy-start(bf16[128,2048]{1,0:T(8,128)(2,1)S(1)} %collective-permute-done.5.refs_8_) | copy-start | bytes 1572868
  41.7 8.2 %collective-permute-start.6 = (bf16[128,2048]{1,0:T(8,128)(2,1)S(1)}, bf16[128,2048]{1,0:T(8,128)(2,1)S(1)}, u32[]{:S(2)}, u32[]{:S(2)}) collective-permute-start(bf16[128,2048]{1,0:T(8,128)(2,1)S(1)} %collective-permute-done.5.refs_8_), channel_id=1, source_target_pairs={{0,1},{1,0},{2,3},{3,2},{4,5},{5,4},{6,7},{7,6},{8,9},{9,8},{10,11... | collective-permute-start | bytes 1572872 | tf_op jit(solution)/shard_map/ppermute | solution.py:311
  42.5 16.2 %copy-start.10 = (bf16[128,2048]{1,0:T(8,128)(2,1)}, bf16[128,2048]{1,0:T(8,128)(2,1)S(1)}, u32[]{:S(2)}) copy-start(bf16[128,2048]{1,0:T(8,128)(2,1)S(1)} %collective-permute-done.3.refs_5_) | copy-start | bytes 1572868
  42.5 14.7 %collective-permute-start.9 = (bf16[128,2048]{1,0:T(8,128)(2,1)S(1)}, bf16[128,2048]{1,0:T(8,128)(2,1)S(1)}, u32[]{:S(2)}, u32[]{:S(2)}) collective-permute-start(bf16[128,2048]{1,0:T(8,128)(2,1)S(1)} %collective-permute-done.5.refs_8_), channel_id=1, source_target_pairs={{0,2},{2,4},{4,6},{6,8},{8,10},{10,12},{12,14},{14,0},{1,3},{3,5},... | collective-permute-start | bytes 1572872 | tf_op jit(solution)/shard_map/ppermute | solution.py:307
  44.4 14.5 %copy-start.11 = (bf16[128,2048]{1,0:T(8,128)(2,1)}, bf16[128,2048]{1,0:T(8,128)(2,1)S(1)}, u32[]{:S(2)}) copy-start(bf16[128,2048]{1,0:T(8,128)(2,1)S(1)} %collective-permute-done.7.refs_10_) | copy-start | bytes 1572868
  44.4 5.4 %collective-permute-start.8 = (bf16[128,2048]{1,0:T(8,128)(2,1)S(1)}, bf16[128,2048]{1,0:T(8,128)(2,1)S(1)}, u32[]{:S(2)}, u32[]{:S(2)}) collective-permute-start(bf16[128,2048]{1,0:T(8,128)(2,1)S(1)} %collective-permute-done.7.refs_10_), channel_id=1, source_target_pairs={{0,1},{1,0},{2,3},{3,2},{4,5},{5,4},{6,7},{7,6},{8,9},{9,8},{10,11... | collective-permute-start | bytes 1572872 | tf_op jit(solution)/shard_map/ppermute | solution.py:311
  45.1 13.9 %copy-start.12 = (bf16[128,2048]{1,0:T(8,128)(2,1)}, bf16[128,2048]{1,0:T(8,128)(2,1)S(1)}, u32[]{:S(2)}) copy-start(bf16[128,2048]{1,0:T(8,128)(2,1)S(1)} %collective-permute-done.4.refs_7_) | copy-start | bytes 1572868
  45.1 13.6 %collective-permute-start.10 = (bf16[128,2048]{1,0:T(8,128)(2,1)S(1)}, bf16[128,2048]{1,0:T(8,128)(2,1)}, u32[]{:S(2)}, u32[]{:S(2)}) collective-permute-start(bf16[128,2048]{1,0:T(8,128)(2,1)S(1)} %collective-permute-done.7.refs_10_), channel_id=1, source_target_pairs={{0,14},{2,0},{4,2},{6,4},{8,6},{10,8},{12,10},{14,12},{1,15},{3,1}... | collective-permute-start | bytes 1572872 | tf_op jit(solution)/shard_map/ppermute | solution.py:307
  57.2 33.0 %copy-start.5 = (bf16[128,2048]{1,0:T(8,128)(2,1)}, bf16[128,2048]{1,0:T(8,128)(2,1)S(1)}, u32[]{:S(2)}) copy-start(bf16[128,2048]{1,0:T(8,128)(2,1)S(1)} %collective-permute-done.9.refs_2_) | copy-start | bytes 1572868
  58.7 7.0 %collective-permute-start.11 = (f32[1,2048]{1,0:T(1,128)S(1)}, f32[1,2048]{1,0:T(1,128)S(1)}, u32[]{:S(2)}, u32[]{:S(2)}) collective-permute-start(f32[1,2048]{1,0:T(1,128)S(1)} %bitcast.17), channel_id=1, source_target_pairs={{0,16},{16,0},{1,17},{17,1},{2,18},{18,2},{3,19},{19,3},{4,20},{20... | collective-permute-start | bytes 24584 | tf_op jit(solution)/shard_map/ppermute | solution.py:347
  59.0 22.2 %all-to-all-start.2 = ((bf16[8,2,64,512]{3,2,1,0:T(8,128)(2,1)}), bf16[8,2,64,512]{3,2,1,0:T(8,128)(2,1)S(1)}, u32[]{:S(2)}, u32[]{:S(2)}) async-start(bf16[8,2,64,512]{3,2,1,0:T(8,128)(2,1)} %stack_roots.1), calls=%async_computation.2 | async-start | bytes 2097152 | tf_op jit(solution)/shard_map/all_to_all | solution.py:345
  82.1 39.3 %all-to-all-start.1 = ((bf16[16,10,16,512]{3,2,1,0:T(8,128)(2,1)}), bf16[16,10,16,512]{3,2,1,0:T(8,128)(2,1)S(1)}, u32[]{:S(2)}, u32[]{:S(2)}) async-start(bf16[16,10,16,512]{3,2,1,0:T(8,128)(2,1)} %bitcast.15), calls=%async_computation.1 | async-start | bytes 5242880 | tf_op jit(solution)/shard_map/all_to_all | solution.py:354
  86.4 7.0 %collective-permute-start.15 = (bf16[64,2048]{1,0:T(8,128)(2,1)S(1)}, bf16[64,2048]{1,0:T(8,128)(2,1)S(1)}, u32[]{:S(2)}, u32[]{:S(2)}) collective-permute-start(bf16[64,2048]{1,0:T(8,128)(2,1)S(1)} %slice.8), channel_id=1, source_target_pairs={{0,2},{2,4},{4,6},{6,8},{8,10},{10,12},{12,14},{14,0},{1,3},{3,5},... | collective-permute-start | bytes 786440 | tf_op jit(solution)/shard_map/ppermute | solution.py:307
  87.8 8.6 %collective-permute-start.16 = (bf16[64,2048]{1,0:T(8,128)(2,1)S(1)}, bf16[64,2048]{1,0:T(8,128)(2,1)S(1)}, u32[]{:S(2)}, u32[]{:S(2)}) collective-permute-start(bf16[64,2048]{1,0:T(8,128)(2,1)S(1)} %slice.9), channel_id=1, source_target_pairs={{0,14},{2,0},{4,2},{6,4},{8,6},{10,8},{12,10},{14,12},{1,15},{3,1}... | collective-permute-start | bytes 786440 | tf_op jit(solution)/shard_map/ppermute | solution.py:307
  90.2 7.8 %collective-permute-start.13 = (bf16[128,2048]{1,0:T(8,128)(2,1)S(1)}, bf16[128,2048]{1,0:T(8,128)(2,1)S(1)}, u32[]{:S(2)}, u32[]{:S(2)}) collective-permute-start(bf16[128,2048]{1,0:T(8,128)(2,1)S(1)} %collective-permute-done.9.refs_2_), channel_id=1, source_target_pairs={{0,1},{1,0},{2,3},{3,2},{4,5},{5,4},{6,7},{7,6},{8,9},{9,8},{10,11... | collective-permute-start | bytes 1572872 | tf_op jit(solution)/shard_map/ppermute | solution.py:311
  92.9 5.1 %collective-permute-start.14 = (bf16[128,2048]{1,0:T(8,128)(2,1)}, bf16[128,2048]{1,0:T(8,128)(2,1)S(1)}, u32[]{:S(2)}, u32[]{:S(2)}) collective-permute-start(bf16[128,2048]{1,0:T(8,128)(2,1)} %collective-permute-done.10.refs_4_), channel_id=1, source_target_pairs={{0,1},{1,0},{2,3},{3,2},{4,5},{5,4},{6,7},{7,6},{8,9},{9,8},{10,11... | collective-permute-start | bytes 1572872 | tf_op jit(solution)/shard_map/ppermute | solution.py:311
  93.4 4.2 %collective-permute-start.17 = (bf16[64,2048]{1,0:T(8,128)(2,1)S(1)}, bf16[64,2048]{1,0:T(8,128)(2,1)S(1)}, u32[]{:S(2)}, u32[]{:S(2)}) collective-permute-start(bf16[64,2048]{1,0:T(8,128)(2,1)S(1)} %collective-permute-done.15.refs_6_), channel_id=1, source_target_pairs={{0,1},{1,0},{2,3},{3,2},{4,5},{5,4},{6,7},{7,6},{8,9},{9,8},{10,11... | collective-permute-start | bytes 786440 | tf_op jit(solution)/shard_map/ppermute | solution.py:311
  96.4 1.5 collective-permute-start.18
  121.4 26.2 %all-to-all-start.3 = ((bf16[16,6,16,512]{3,2,1,0:T(8,128)(2,1)}), bf16[16,6,16,512]{3,2,1,0:T(8,128)(2,1)}, u32[]{:S(2)}, u32[]{:S(2)}) async-start(bf16[16,6,16,512]{3,2,1,0:T(8,128)(2,1)} %bitcast.16), calls=%async_computation.3 | async-start | bytes 3145728 | tf_op jit(solution)/shard_map/all_to_all | solution.py:354
  127.0 20.6 %copy-start.4 = (s32[1,8]{1,0:T(1,128)S(1)}, s32[1,8]{1,0:T(1,128)}, u32[]{:S(2)}) copy-start(s32[1,8]{1,0:T(1,128)} %param.12) | copy-start | bytes 100
  152.4 32.1 %all-to-all-start.4 = ((bf16[8,4,4,16,512]{4,3,2,1,0:T(8,128)(2,1)}), bf16[8,4,4,16,512]{4,3,2,1,0:T(8,128)(2,1)S(1)}, u32[]{:S(2)}, u32[]{:S(2)}) async-start(bf16[8,4,4,16,512]{4,3,2,1,0:T(8,128)(2,1)} %route.1), calls=%async_computation.4 | async-start | bytes 4194304 | tf_op jit(solution)/shard_map/all_to_all | solution.py:358
  (12 other events, 32.1 us)

commit v4 on v2

v4 whole, which is shorter than its diff:
```python
import jax
import jax.numpy as jnp
from jax import lax
from jax.experimental import pallas as pl
from jax.experimental.pallas import tpu as pltpu
from jax.sharding import Mesh
from jax.sharding import PartitionSpec as P

NORM_EPSILON = 1e-05
SCALE_EPSILON = 1e-06
DECAY_RATE = 0.95
RIDGE_TERM = 1e-06
BLK = 512
N_GROUP = 8
CHUNK = BLK // N_GROUP
PACKED = CHUNK + 16
GROUP = ("y", "xh")
FSDP = ("xl", "z", "core")
SWAP = [(0, 1), (1, 0)]
BF16 = jnp.bfloat16
F32 = jnp.float32
NT = (((1,), (1,)), ((), ()))
TN = (((0,), (0,)), ((), ()))
HBM = pl.BlockSpec(memory_space=pltpu.HBM)
VMEM = pl.BlockSpec(memory_space=pltpu.VMEM)
SMEM = pl.BlockSpec(memory_space=pltpu.SMEM)


def in_hbm(x):
    return pltpu.with_memory_space_constraint(x, pltpu.HBM)


def params():
    return pltpu.CompilerParams(vmem_limit_bytes=48 * 2**20)


def dot(a, b):
    return jnp.dot(a, b, preferred_element_type=F32)


def dot_dims(a, b, dims):
    return lax.dot_general(a, b, dims, preferred_element_type=F32)


def split2(a):
    high = a.astype(BF16)
    return high, (a - high.astype(F32)).astype(BF16)


def prepare_kernel(x_ref, gain_ref, xt_ref, sq_ref):
    values = x_ref[...].astype(F32)
    xt_ref[...] = (values * gain_ref[...].astype(F32)).astype(BF16).T
    high, low = split2(values * values)
    ones = jnp.ones((8, values.shape[1]), BF16)
    sq_ref[...] = (dot_dims(ones, high, NT) + dot_dims(ones, low, NT))[:1]


def prepare(x, gain):
    tokens, width = x.shape
    step = tokens // 2
    return pl.pallas_call(
        prepare_kernel,
        grid=(2,),
        in_specs=[pl.BlockSpec((step, width), lambda i: (i, 0)), pl.BlockSpec((1, width), lambda i: (0, 0))],
        out_specs=[pl.BlockSpec((width, step), lambda i: (0, i)), pl.BlockSpec((1, step), lambda i: (0, i))],
        out_shape=[pltpu.HBM((width, tokens), BF16), jax.ShapeDtypeStruct((1, tokens), F32)],
        name="prepare",
    )(x, gain.reshape(1, width))


def triangle():
    rows = lax.broadcasted_iota(jnp.int32, (BLK, BLK), 0)
    cols = lax.broadcasted_iota(jnp.int32, (BLK, BLK), 1)
    return rows, cols


def pack_roots_kernel(l_ref, r_ref, o_ref):
    rows, cols = triangle()
    left = l_ref[...]
    packed = jnp.where(cols > rows, left, r_ref[...]).astype(BF16)
    diagonal = jnp.sum(jnp.where(cols == rows, left, 0.0), axis=0, keepdims=True)
    diagonal = jnp.broadcast_to(diagonal, (PACKED - CHUNK, BLK)).astype(BF16)
    for i in range(N_GROUP):
        o_ref[i, :CHUNK] = packed[i * CHUNK : (i + 1) * CHUNK]
        o_ref[i, CHUNK:] = diagonal


def pack_roots(left, right):
    return pl.pallas_call(
        pack_roots_kernel,
        in_specs=[VMEM, VMEM],
        out_specs=VMEM,
        out_shape=pltpu.HBM((N_GROUP, PACKED, BLK), BF16),
        compiler_params=params(),
        name="pack_roots",
    )(left, right)


def pick_kernel(owner_ref, x_ref, o_ref):
    for i in range(N_GROUP):
        o_ref[i] = x_ref[owner_ref[i]]


def pick(owner, x):
    return pl.pallas_call(
        pick_kernel,
        in_specs=[SMEM, VMEM],
        out_specs=VMEM,
        out_shape=pltpu.HBM(x.shape, x.dtype),
        compiler_params=params(),
        name="pick",
    )(owner, x)


def unpack_roots_kernel(x_ref, l_ref, r_ref):
    rows, cols = triangle()
    packed = jnp.concatenate([x_ref[i, :CHUNK] for i in range(N_GROUP)], axis=0).astype(F32)
    upper = jnp.where(cols > rows, packed, 0.0)
    lower = jnp.where(cols < rows, packed, 0.0)
    diagonal = x_ref[0, CHUNK:].astype(F32)[:1]
    l_ref[...] = (upper + upper.T + jnp.where(cols == rows, diagonal, 0.0)).astype(BF16)
    r_ref[...] = (packed - upper + lower.T).astype(BF16)


def unpack_roots(x):
    square = jax.ShapeDtypeStruct((BLK, BLK), BF16)
    return pl.pallas_call(
        unpack_roots_kernel,
        in_specs=[VMEM],
        out_specs=[VMEM, VMEM],
        out_shape=[square, square],
        compiler_params=params(),
        name="unpack_roots",
    )(x)


def scale_kernel(scale_ref, x_ref, o_ref):
    column = jnp.broadcast_to(scale_ref[...], (8, scale_ref.shape[1])).T[:, :1]
    o_ref[...] = (x_ref[...].astype(F32) * column).astype(BF16)


def scaled(scale, x):
    tokens, cols = x.shape
    step = tokens // 4
    block = pl.BlockSpec((step, cols), lambda i: (i, 0))
    return pl.pallas_call(
        scale_kernel,
        grid=(4,),
        in_specs=[pl.BlockSpec((1, step), lambda i: (0, i)), block],
        out_specs=block,
        out_shape=jax.ShapeDtypeStruct(x.shape, BF16),
        name="scaled",
    )(scale, x)


def partial_kernel(xl_ref, x_ref, own_ref, other_ref, o_ref):
    for cot_ref, place in ((own_ref, xl_ref[0]), (other_ref, 1 - xl_ref[0])):
        part = dot(x_ref[...], cot_ref[...]).astype(BF16)
        for j in range(part.shape[0] // CHUNK):
            o_ref[j, place, 0] = part[j * CHUNK : (j + 1) * CHUNK]


def partials(xl, x, own, other, half):
    tokens = x.shape[1]
    whole = pl.BlockSpec((tokens, BLK), lambda i, xl: (0, 0))
    return pl.pallas_call(
        partial_kernel,
        grid_spec=pltpu.PrefetchScalarGridSpec(
            num_scalar_prefetch=1,
            grid=(4,),
            in_specs=[pl.BlockSpec((BLK // 2, tokens), lambda i, xl: (4 * half + i, 0)), whole, whole],
            out_specs=pl.BlockSpec((N_GROUP // 2, 2, 1, CHUNK, BLK), lambda i, xl: (i % 2, 0, i // 2, 0, 0)),
        ),
        out_shape=pltpu.HBM((N_GROUP, 2, 2, CHUNK, BLK), BF16),
        compiler_params=params(),
        cost_estimate=pl.CostEstimate(flops=8 * tokens * BLK * BLK, bytes_accessed=10 * 2**20, transcendentals=0),
        name="partials",
    )(xl, x, own, other)


def total(x_ref, slab):
    acc = x_ref[0, 0, slab].astype(F32)
    for g in range(1, N_GROUP):
        acc = acc + x_ref[g, 0, slab].astype(F32)
    return acc.astype(BF16)


def reduce_kernel(x_ref, o_ref):
    for slab in range(2):
        o_ref[0, slab] = total(x_ref, slab)


def reduce_half(x):
    return pl.pallas_call(
        reduce_kernel,
        grid=(2,),
        in_specs=[pl.BlockSpec((N_GROUP, 1, 2, CHUNK, BLK), lambda i: (0, i, 0, 0, 0))],
        out_specs=pl.BlockSpec((1, 2, CHUNK, BLK), lambda i: (i, 0, 0, 0)),
        out_shape=jax.ShapeDtypeStruct((2, 2, CHUNK, BLK), BF16),
        name="reduce_half",
    )(x)


def route_kernel(owner_ref, first_ref, x_ref, o_ref):
    base = 4 * pl.program_id(0)
    for n in range(2):
        for slab, value in ((base + n, first_ref[0, n]), (base + 2 + n, total(x_ref, n))):
            o_ref[slab, 1] = value
            o_ref[owner_ref[slab], 0] = value


def route(owner, first, x):
    return pl.pallas_call(
        route_kernel,
        grid_spec=pltpu.PrefetchScalarGridSpec(
            num_scalar_prefetch=1,
            grid=(2,),
            in_specs=[
                pl.BlockSpec((1, 2, CHUNK, BLK), lambda i, owner: (i, 0, 0, 0)),
                pl.BlockSpec((N_GROUP, 1, 2, CHUNK, BLK), lambda i, owner: (0, i, 0, 0, 0)),
            ],
            out_specs=pl.BlockSpec((N_GROUP, 2, CHUNK, BLK), lambda i, owner: (0, 0, 0, 0)),
        ),
        out_shape=pltpu.HBM((N_GROUP, 2, CHUNK, BLK), BF16),
        name="route",
    )(owner, first, in_hbm(x))


def inverse_fourth_root(statistic):
    rows, cols = triangle()
    eye = (rows == cols).astype(F32)
    matrix = statistic + RIDGE_TERM * eye
    scaling = 2.5 * lax.rsqrt(jnp.sum(matrix * matrix, keepdims=True))
    scaled = scaling * matrix
    factor = (1.25 * eye - 0.25 * scaled).astype(BF16)
    square = dot(factor, factor).astype(BF16)
    fourth = dot(square, square).astype(BF16)
    second = 1.25 * eye - 0.25 * dot(fourth, scaled.astype(BF16))
    return jnp.sqrt(jnp.sqrt(scaling)) * dot(factor, second.astype(BF16))


def block_kernel(
    refresh_ref, u_ref, lroot_ref, rroot_ref, ls_ref, rs_ref, li_ref, ri_ref,
    upd_ref, la_ref, ra_ref, ln_ref, rn_ref, left, right, left_new, right_new, sems,
):
    fresh = refresh_ref[0, 0] > 0
    loads = [pltpu.make_async_copy(ls_ref, left, sems.at[0]), pltpu.make_async_copy(rs_ref, right, sems.at[1])]
    keeps = [pltpu.make_async_copy(li_ref, left_new, sems.at[2]), pltpu.make_async_copy(ri_ref, right_new, sems.at[3])]
    stores = [pltpu.make_async_copy(left, la_ref, sems.at[4]), pltpu.make_async_copy(right, ra_ref, sems.at[5])]
    news = [pltpu.make_async_copy(left_new, ln_ref, sems.at[6]), pltpu.make_async_copy(right_new, rn_ref, sems.at[7])]
    for load in loads:
        load.start()

    @pl.when(jnp.logical_not(fresh))
    def _():
        for keep in keeps:
            keep.start()

    grad = u_ref[:, 0].reshape(BLK, BLK)
    for n, (accum, dims) in enumerate(((left, NT), (right, TN))):
        gram = dot_dims(grad, grad, dims)
        loads[n].wait()
        accum[...] = DECAY_RATE * accum[...] + (1.0 - DECAY_RATE) * gram
        stores[n].start()

    @pl.when(fresh)
    def _():
        for accum, new, copy in ((left, left_new, news[0]), (right, right_new, news[1])):
            new[...] = inverse_fourth_root(accum[...])
            copy.start()

    @pl.when(jnp.logical_not(fresh))
    def _():
        for keep, copy in zip(keeps, news):
            keep.wait()
            copy.start()

    right_root = rroot_ref[...]
    high, low = split2(dot(lroot_ref[...], u_ref[:, 1].reshape(BLK, BLK)))
    conditioned = dot(high, right_root) + dot(low, right_root)
    mean = jnp.sum(conditioned * conditioned, keepdims=True) * (1.0 / (BLK * BLK))
    upd_ref[...] = (conditioned * lax.rsqrt(mean + SCALE_EPSILON)).astype(BF16)
    for copy in stores + news:
        copy.wait()


def block_step(refresh, received, left_root, right_root, *state):
    square = pltpu.HBM((BLK, BLK), F32)
    return pl.pallas_call(
        block_kernel,
        in_specs=[SMEM, VMEM, VMEM, VMEM] + [HBM] * 4,
        out_specs=[VMEM] + [HBM] * 4,
        out_shape=[jax.ShapeDtypeStruct((BLK, BLK), BF16)] + [square] * 4,
        scratch_shapes=[pltpu.VMEM((BLK, BLK), F32)] * 4 + [pltpu.SemaphoreType.DMA((8,))],
        compiler_params=params(),
        cost_estimate=pl.CostEstimate(flops=2**31, bytes_accessed=11 * 2**20, transcendentals=0),
        name="block_step",
    )(refresh, received, left_root, right_root, *[in_hbm(a) for a in state])


def body(inputs, norm_gain, cotangent, owners, refresh, left_stats, right_stats, left_inverse, right_inverse):
    xl = lax.axis_index("xl").reshape(1)
    owner = owners[0]
    tokens, width = inputs.shape
    count = lax.axis_size(FSDP) * width
    peers = lax.axis_size(("z", "core"))

    block, squares = prepare(inputs, norm_gain)
    features = lax.all_gather(block, ("z", "core"), axis=0, tiled=True)
    squares_other = lax.ppermute(squares, "xl", SWAP)
    squares_other, cotangent = lax.optimization_barrier((squares_other, cotangent))
    other = lax.ppermute(cotangent, "xl", SWAP)

    roots = pack_roots(left_inverse, right_inverse)
    roots = lax.all_to_all(roots, GROUP, split_axis=0, concat_axis=0, tiled=True)
    squares = jnp.broadcast_to(squares + squares_other, (peers, tokens))
    roots, squares = lax.optimization_barrier((roots, squares))
    squares = lax.all_to_all(squares, ("z", "core"), split_axis=0, concat_axis=0, tiled=True)
    scale = lax.rsqrt(jnp.sum(squares, axis=0, keepdims=True) / count + NORM_EPSILON)
    roots = pick(owner, roots)
    roots, scale = lax.optimization_barrier((roots, scale))
    roots = lax.all_to_all(roots, GROUP, split_axis=0, concat_axis=0, tiled=True)
    own, other = scaled(scale, cotangent), scaled(scale, other)
    roots, features = lax.optimization_barrier((roots, features))

    halves = []
    for half in range(2):
        pieces = partials(xl, features, own, other, half)
        shape = pieces.shape
        pieces = pieces.reshape(2 * N_GROUP, *shape[2:])
        pieces = lax.all_to_all(pieces, ("y", "xh", "xl"), split_axis=0, concat_axis=0, tiled=True)
        halves.append(pieces.reshape(shape))
    grads = route(owner, reduce_half(halves[0]), halves[1])
    grads = lax.all_to_all(grads, GROUP, split_axis=0, concat_axis=0, tiled=True)
    left_root, right_root = unpack_roots(roots)
    state = (left_stats, right_stats, left_inverse, right_inverse)
    return tuple(block_step(refresh, grads, left_root, right_root, *state))


def solution(mesh):
    split = Mesh(mesh.devices.reshape(4, 2, 2, 8, 2), ("y", "xh", "xl", "z", "core"))
    both = P(GROUP, FSDP)
    in_specs = (both, P(FSDP), both, P(FSDP, None), both, both, both, both, both)
    return jax.shard_map(body, mesh=split, in_specs=in_specs, out_specs=(both,) * 5, check_vma=False)
```

time: 234 us -> 228 us (0.974)
  blocking collectives: 52.9 us -> 0 us
  waiting for transfers between devices: 77.4 us -> 125 us
  Pallas kernels: 48.4 us -> 38.9 us
  local copies, waits for them, and re-layouts: 4.05 us -> 7.73 us
  starting transfers between devices: 34.8 us -> 37.8 us
    all_to_all x1 -> x0, blocking collectives: 52.9 us -> none  [body(): lax.all_to_all(roots, GROUP, split_axis=0, concat_axis=0, tiled=True)]
    all_to_all x1 -> x2, waiting for transfers between devices: 15.8 us -> 50.7 us  [body(): lax.all_to_all(roots, GROUP, split_axis=0, concat_axis=0, tiled=True)]
    all_to_all x2, waiting for transfers between devices: 41 us -> 50.7 us  [body(): lax.all_to_all(pieces, ('y', 'xh', 'xl'), split_axis=0, concat_axis=0, ti...]
    pallas_call x6 -> x9, Pallas kernels: 31.3 us -> 24.2 us  [the longest x2 8.83 us: scaled(): pl.pallas_call(scale_kernel, grid=(4,), in_specs=[pl.BlockSpec((1, step),...]
    all_to_all x1 -> x2, starting transfers between devices: 3.56 us -> 9.9 us  [body(): lax.all_to_all(roots, GROUP, split_axis=0, concat_axis=0, tiled=True)]
    unnamed x6 -> x16, local copies, waits for them, and re-layouts: 2.45 us -> 6.98 us
    all_to_all x2, starting transfers between devices: 11.8 us -> 8.16 us  [body(): lax.all_to_all(pieces, ('y', 'xh', 'xl'), split_axis=0, concat_axis=0, ti...]
    pallas_call x2, Pallas kernels: 17.1 us -> 14.6 us  [partials(): pl.pallas_call(partial_kernel, grid_spec=pltpu.PrefetchScalarGridSpec(num...]
  transfers between devices with their start and end apart: 7 -> 9, of which waited for: 5 -> 7; matrix products, arithmetic and copies ran while one was open for 0% -> 0% of each run, Pallas kernels for 10% -> 9%
where the time goes in v4:
time: 228 us; the launch traced here: 225 us
  waiting for transfers between devices  125 us (55%)
  Pallas kernels  38.9 us (17%)
  starting transfers between devices  37.8 us (17%)
  between operations  14.8 us (6%)
  local copies, waits for them, and re-layouts  7.73 us (3%)
    all_to_all x2, waiting for transfers between devices, body(): lax.all_to_all(roots, GROUP, split_axis=0, concat_axis=0, tiled=True)  50.7 us
    all_to_all x2, waiting for transfers between devices, body(): lax.all_to_all(pieces, ('y', 'xh', 'xl'), split_axis=0, concat_axis=0, ti...  50.7 us
    all_to_all x1, waiting for transfers between devices, body(): lax.all_to_all(grads, GROUP, split_axis=0, concat_axis=0, tiled=True)  14.8 us
    pallas_call x2, Pallas kernels, partials(): pl.pallas_call(partial_kernel, grid_spec=pltpu.PrefetchScalarGridSpec(num...  14.6 us
    all_to_all x1, starting transfers between devices, body(): lax.all_to_all(squares, ('z', 'core'), split_axis=0, concat_axis=0, tiled...  11.2 us
    all_to_all x2, starting transfers between devices, body(): lax.all_to_all(roots, GROUP, split_axis=0, concat_axis=0, tiled=True)  9.9 us
    pallas_call x2, Pallas kernels, scaled(): pl.pallas_call(scale_kernel, grid=(4,), in_specs=[pl.BlockSpec((1, step),...  8.83 us
    all_to_all x2, starting transfers between devices, body(): lax.all_to_all(pieces, ('y', 'xh', 'xl'), split_axis=0, concat_axis=0, ti...  8.16 us
  transfers between devices with their start and end apart: 9, of which 7 were waited for; matrix products, arithmetic and copies ran while one was open for 0% of the time, Pallas kernels for 9%

profile of v4, /device:TPU:1, one launch (start us, length us, event | category | flops | bytes accessed | tf_op | source)
XLA Modules:
  0.0 225.1 jit_solution(4690529223789183428)
XLA Ops:
  7.2 2.2 prepare.1
  9.4 2.1 collective-permute-start
  11.5 1.3 collective-permute-done
  12.8 1.5 collective-permute-start.1
  14.3 1.2 copy-done.3
  15.5 1.2 copy-done.4
  16.7 0.9 pack_roots.1
  17.6 6.4 %all-to-all-start = ((bf16[8,80,512]{2,1,0:T(8,128)(2,1)}), bf16[8,80,512]{2,1,0:T(8,128)(2,1)S(1)}, u32[]{:S(2)}, u32[]{:S(2)}) async-start(bf16[8,80,512]{2,1,0:T(8,128)(2,1)} %pack_roots.1), calls=%async_computation | async-start | bytes 1310720 | tf_op jit(solution)/shard_map/all_to_all | solution.py:315
  24.0 46.2 %all-to-all-done.x_ref = bf16[8,80,512]{2,1,0:T(8,128)(2,1)S(1)} async-done(((bf16[8,80,512]{2,1,0:T(8,128)(2,1)}), bf16[8,80,512]{2,1,0:T(8,128)(2,1)S(1)}, u32[]{:S(2)}, u32[]{:S(2)}) %all-to-all-start) | async-done | bytes 655392 | tf_op jit(solution)/shard_map/all_to_all | solution.py:315
  70.2 0.7 all_to_all.22
  71.0 11.2 %all-to-all-start.1 = ((f32[16,1,2048]{2,1,0:T(1,128)}), f32[16,1,2048]{2,1,0:T(1,128)S(1)}, u32[]{:S(2)}, u32[]{:S(2)}) async-start(f32[16,1,2048]{2,1,0:T(1,128)} %all_to_all.22), calls=%async_computation.1 | async-start | bytes 262144 | tf_op jit(solution)/shard_map/all_to_all | solution.py:318
  82.2 1.4 pick.1
  83.6 7.7 %all-to-all-done.1 = f32[16,1,2048]{2,1,0:T(1,128)S(1)} async-done(((f32[16,1,2048]{2,1,0:T(1,128)}), f32[16,1,2048]{2,1,0:T(1,128)S(1)}, u32[]{:S(2)}, u32[]{:S(2)}) %all-to-all-start.1) | async-done | bytes 131104 | tf_op jit(solution)/shard_map/all_to_all | solution.py:318
  91.5 0.6 add_rsqrt_fusion
  92.1 3.5 %all-to-all-start.2 = ((bf16[8,80,512]{2,1,0:T(8,128)(2,1)}), bf16[8,80,512]{2,1,0:T(8,128)(2,1)S(1)}, u32[]{:S(2)}, u32[]{:S(2)}) async-start(bf16[8,80,512]{2,1,0:T(8,128)(2,1)} %pick.1), calls=%async_computation.2 | async-start | bytes 1310720 | tf_op jit(solution)/shard_map/all_to_all | solution.py:322
  95.6 4.4 %scaled.2.own_ref = bf16[2048,512]{1,0:T(8,128)(2,1)} custom-call(f32[1,2048]{1,0:T(1,128)} %bitcast.14, bf16[2048,512]{1,0:T(8,128)(2,1)} %x_ref.2), custom_call_target="tpu_custom_call" | custom-call | tf_op jit(solution)/shard_map/scaled/pallas_call | solution.py:146
  100.0 4.4 %scaled.3.other_ref = bf16[2048,512]{1,0:T(8,128)(2,1)} custom-call(f32[1,2048]{1,0:T(1,128)} %bitcast.15, bf16[2048,512]{1,0:T(8,128)(2,1)} %collective-permute-done.1.x_ref), custom_call_target="tpu_custom_call" | custom-call | tf_op jit(solution)/shard_map/scaled/pallas_call | solution.py:146
  104.5 4.5 %all-to-all-done.2.x_ref = bf16[8,80,512]{2,1,0:T(8,128)(2,1)S(1)} async-done(((bf16[8,80,512]{2,1,0:T(8,128)(2,1)}), bf16[8,80,512]{2,1,0:T(8,128)(2,1)S(1)}, u32[]{:S(2)}, u32[]{:S(2)}) %all-to-all-start.2) | async-done | bytes 655392 | tf_op jit(solution)/shard_map/all_to_all | solution.py:322
  109.0 1.6 copy-done.1
  110.6 7.3 %partials.2 = bf16[8,2,2,64,512]{4,3,2,1,0:T(8,128)(2,1)} custom-call(s32[1]{0:T(128)} %bitcast.1.xl_ref, bf16[2048,2048]{1,0:T(8,128)(2,1)} %all-gather.2.cloned.1.call-done.x_ref, bf16[2048,512]{1,0:T(8,128)(2,1)S(1)} %copy-done, bf16[2048,512]{1,0:T(8,128)(2,1)S(1)} %copy-done.1), custom_call_target="tpu_custom_call" | custom-call | flops 4294967296 | bytes 10485760 | tf_op jit(solution)/shard_map/partials/pallas_call | solution.py:166
  117.9 4.4 %all-to-all-start.3 = ((bf16[16,2,64,512]{3,2,1,0:T(8,128)(2,1)}), bf16[16,2,64,512]{3,2,1,0:T(8,128)(2,1)}, u32[]{:S(2)}, u32[]{:S(2)}) async-start(bf16[16,2,64,512]{3,2,1,0:T(8,128)(2,1)} %bitcast.13), calls=%async_computation.3 | async-start | bytes 4194304 | tf_op jit(solution)/shard_map/all_to_all | solution.py:331
  122.3 1.6 copy-done.2
  123.9 7.3 %partials.3 = bf16[8,2,2,64,512]{4,3,2,1,0:T(8,128)(2,1)} custom-call(s32[1]{0:T(128)} %bitcast.1.xl_ref, bf16[2048,2048]{1,0:T(8,128)(2,1)} %all-gather.2.cloned.1.call-done.x_ref, bf16[2048,512]{1,0:T(8,128)(2,1)S(1)} %copy-done, bf16[2048,512]{1,0:T(8,128)(2,1)S(1)} %copy-done.2), custom_call_target="tpu_custom_call" | custom-call | flops 4294967296 | bytes 10485760 | tf_op jit(solution)/shard_map/partials/pallas_call | solution.py:166
  131.2 23.7 %all-to-all-done.3 = bf16[16,2,64,512]{3,2,1,0:T(8,128)(2,1)} async-done(((bf16[16,2,64,512]{3,2,1,0:T(8,128)(2,1)}), bf16[16,2,64,512]{3,2,1,0:T(8,128)(2,1)}, u32[]{:S(2)}, u32[]{:S(2)}) %all-to-all-start.3) | async-done | bytes 2097184 | tf_op jit(solution)/shard_map/all_to_all | solution.py:331
  154.9 3.7 %all-to-all-start.4 = ((bf16[16,2,64,512]{3,2,1,0:T(8,128)(2,1)}), bf16[16,2,64,512]{3,2,1,0:T(8,128)(2,1)S(1)}, u32[]{:S(2)}, u32[]{:S(2)}) async-start(bf16[16,2,64,512]{3,2,1,0:T(8,128)(2,1)} %bitcast.12), calls=%async_computation.4 | async-start | bytes 4194304 | tf_op jit(solution)/shard_map/all_to_all | solution.py:331
  158.7 2.4 %reduce_half.1.first_ref = bf16[2,2,64,512]{3,2,1,0:T(8,128)(2,1)} custom-call(bf16[8,2,2,64,512]{4,3,2,1,0:T(8,128)(2,1)} %bitcast.6.x_ref), custom_call_target="tpu_custom_call" | custom-call | tf_op jit(solution)/shard_map/reduce_half/pallas_call | solution.py:194
  161.0 27.0 %all-to-all-done.4 = bf16[16,2,64,512]{3,2,1,0:T(8,128)(2,1)S(1)} async-done(((bf16[16,2,64,512]{3,2,1,0:T(8,128)(2,1)}), bf16[16,2,64,512]{3,2,1,0:T(8,128)(2,1)S(1)}, u32[]{:S(2)}, u32[]{:S(2)}) %all-to-all-start.4) | async-done | bytes 2097184 | tf_op jit(solution)/shard_map/all_to_all | solution.py:331
  188.0 1.3 copy-done.6
  189.3 3.4 %route.1 = bf16[8,2,64,512]{3,2,1,0:T(8,128)(2,1)} custom-call(s32[8]{0:T(128)} %bitcast.9, bf16[2,2,64,512]{3,2,1,0:T(8,128)(2,1)} %reduce_half.1.first_ref, bf16[8,2,2,64,512]{4,3,2,1,0:T(8,128)(2,1)} %bitcast.11), custom_call_target="tpu_custom_call" | custom-call | tf_op jit(solution)/shard_map/route/pallas_call | solution.py:213
  192.8 4.9 %all-to-all-start.5 = ((bf16[8,2,64,512]{3,2,1,0:T(8,128)(2,1)}), bf16[8,2,64,512]{3,2,1,0:T(8,128)(2,1)S(1)}, u32[]{:S(2)}, u32[]{:S(2)}) async-start(bf16[8,2,64,512]{3,2,1,0:T(8,128)(2,1)} %route.1), calls=%async_computation.5 | async-start | bytes 2097152 | tf_op jit(solution)/shard_map/all_to_all | solution.py:334
  198.6 14.8 %all-to-all-done.5.u_ref = bf16[8,2,64,512]{3,2,1,0:T(8,128)(2,1)S(1)} async-done(((bf16[8,2,64,512]{3,2,1,0:T(8,128)(2,1)}), bf16[8,2,64,512]{3,2,1,0:T(8,128)(2,1)S(1)}, u32[]{:S(2)}, u32[]{:S(2)}) %all-to-all-start.5) | async-done | bytes 1048608 | tf_op jit(solution)/shard_map/all_to_all | solution.py:334
  213.5 4.8 %block_step.1 = (bf16[512,512]{1,0:T(8,128)(2,1)}, f32[512,512]{1,0:T(8,128)}, f32[512,512]{1,0:T(8,128)}, f32[512,512]{1,0:T(8,128)}, f32[512,512]{1,0:T(8,128)}) custom-call(s32[1,1]{1,0:T(1,128)S(6)} %copy.14.refresh_ref, bf16[8,2,64,512]{3,2,1,0:T(8,128)(2,1)S(1)} %all-to-all-done.5.u_ref, bf16[512,512]{1,0:T(8,128)(2,1)S(1)} %get-tuple-element.27.lroot_ref, ...), custom_call_target="tpu_custom_call" | custom-call | flops 2147483648 | bytes 11534336 | tf_op jit(solution)/shard_map/block_step/pallas_call | solution.py:289
  (19 shorter events, 0.5 us)
Async XLA Ops:
  7.2 101.8 %all-gather.2.cloned.1.call-start = ((), (), s32[]{:S(2)}) async-start(), calls=%async_computation.6 | async-start | bytes 8912896 | tf_op jit(solution)/shard_map/all_gather | solution.py:309
  9.4 14.6 %copy-start.7 = (f32[1,2048]{1,0:T(1,128)S(1)}, f32[1,2048]{1,0:T(1,128)}, u32[]{:S(2)}) copy-start(f32[1,2048]{1,0:T(1,128)} %get-tuple-element.17) | copy-start | bytes 24580
  9.4 72.8 %copy-start.5 = (s32[1,8]{1,0:T(1,128)S(1)}, s32[1,8]{1,0:T(1,128)}, u32[]{:S(2)}) copy-start(s32[1,8]{1,0:T(1,128)} %param.12) | copy-start | bytes 100
  9.4 3.4 %collective-permute-start = (f32[1,2048]{1,0:T(1,128)}, f32[1,2048]{1,0:T(1,128)S(1)}, u32[]{:S(2)}, u32[]{:S(2)}) collective-permute-start(f32[1,2048]{1,0:T(1,128)} %get-tuple-element.17), channel_id=1, source_target_pairs={{0,16},{16,0},{1,17},{17,1},{2,18},{18,2},{3,19},{19,3},{4,20},{20... | collective-permute-start | bytes 24584 | tf_op jit(solution)/shard_map/ppermute | solution.py:310
  12.8 87.2 %collective-permute-start.1 = (bf16[2048,512]{1,0:T(8,128)(2,1)}, bf16[2048,512]{1,0:T(8,128)(2,1)}, u32[]{:S(2)}, u32[]{:S(2)}) collective-permute-start(bf16[2048,512]{1,0:T(8,128)(2,1)} %x_ref.2), channel_id=1, source_target_pairs={{0,16},{16,0},{1,17},{17,1},{2,18},{18,2},{3,19},{19,3},{4,20},{20... | collective-permute-start | bytes 6291464 | tf_op jit(solution)/shard_map/ppermute | solution.py:312
  14.3 1.2 copy-start.3
  15.5 1.2 copy-start.4
  17.6 52.6 %all-to-all-start = ((bf16[8,80,512]{2,1,0:T(8,128)(2,1)}), bf16[8,80,512]{2,1,0:T(8,128)(2,1)S(1)}, u32[]{:S(2)}, u32[]{:S(2)}) async-start(bf16[8,80,512]{2,1,0:T(8,128)(2,1)} %pack_roots.1), calls=%async_computation | async-start | bytes 1310720 | tf_op jit(solution)/shard_map/all_to_all | solution.py:315
  71.0 20.4 %all-to-all-start.1 = ((f32[16,1,2048]{2,1,0:T(1,128)}), f32[16,1,2048]{2,1,0:T(1,128)S(1)}, u32[]{:S(2)}, u32[]{:S(2)}) async-start(f32[16,1,2048]{2,1,0:T(1,128)} %all_to_all.22), calls=%async_computation.1 | async-start | bytes 262144 | tf_op jit(solution)/shard_map/all_to_all | solution.py:318
  92.1 16.9 %all-to-all-start.2 = ((bf16[8,80,512]{2,1,0:T(8,128)(2,1)}), bf16[8,80,512]{2,1,0:T(8,128)(2,1)S(1)}, u32[]{:S(2)}, u32[]{:S(2)}) async-start(bf16[8,80,512]{2,1,0:T(8,128)(2,1)} %pick.1), calls=%async_computation.2 | async-start | bytes 1310720 | tf_op jit(solution)/shard_map/all_to_all | solution.py:322
  100.0 9.0 %copy-start = (bf16[2048,512]{1,0:T(8,128)(2,1)S(1)}, bf16[2048,512]{1,0:T(8,128)(2,1)}, u32[]{:S(2)}) copy-start(bf16[2048,512]{1,0:T(8,128)(2,1)} %scaled.2.own_ref) | copy-start | bytes 6291460
  109.0 1.6 copy-start.1
  117.9 37.1 %all-to-all-start.3 = ((bf16[16,2,64,512]{3,2,1,0:T(8,128)(2,1)}), bf16[16,2,64,512]{3,2,1,0:T(8,128)(2,1)}, u32[]{:S(2)}, u32[]{:S(2)}) async-start(bf16[16,2,64,512]{3,2,1,0:T(8,128)(2,1)} %bitcast.13), calls=%async_computation.3 | async-start | bytes 4194304 | tf_op jit(solution)/shard_map/all_to_all | solution.py:331
  122.3 1.6 copy-start.2
  154.9 33.0 %all-to-all-start.4 = ((bf16[16,2,64,512]{3,2,1,0:T(8,128)(2,1)}), bf16[16,2,64,512]{3,2,1,0:T(8,128)(2,1)S(1)}, u32[]{:S(2)}, u32[]{:S(2)}) async-start(bf16[16,2,64,512]{3,2,1,0:T(8,128)(2,1)} %bitcast.12), calls=%async_computation.4 | async-start | bytes 4194304 | tf_op jit(solution)/shard_map/all_to_all | solution.py:331
  188.0 1.3 copy-start.6
  192.8 20.7 %all-to-all-start.5 = ((bf16[8,2,64,512]{3,2,1,0:T(8,128)(2,1)}), bf16[8,2,64,512]{3,2,1,0:T(8,128)(2,1)S(1)}, u32[]{:S(2)}, u32[]{:S(2)}) async-start(bf16[8,2,64,512]{3,2,1,0:T(8,128)(2,1)} %route.1), calls=%async_computation.5 | async-start | bytes 2097152 | tf_op jit(solution)/shard_map/all_to_all | solution.py:334
Sparse Core Ops, SparseCore 0:
  10.4 60.1 all-gather.1

commit v5 on v4

--- a/solution.py
+++ b/solution.py
@@ -160,20 +160,20 @@
             o_ref[j, place, 0] = part[j * CHUNK : (j + 1) * CHUNK]
 
 
-def partials(xl, x, own, other, half):
-    tokens = x.shape[1]
-    whole = pl.BlockSpec((tokens, BLK), lambda i, xl: (0, 0))
+def partials(xl, x, own, other):
+    rows, tokens = x.shape
+    slabs = rows // BLK
     return pl.pallas_call(
         partial_kernel,
         grid_spec=pltpu.PrefetchScalarGridSpec(
             num_scalar_prefetch=1,
-            grid=(4,),
-            in_specs=[pl.BlockSpec((BLK // 2, tokens), lambda i, xl: (4 * half + i, 0)), whole, whole],
+            grid=(2 * slabs,),
+            in_specs=[pl.BlockSpec((BLK // 2, tokens), lambda i, xl: (i, 0)), VMEM, VMEM],
             out_specs=pl.BlockSpec((N_GROUP // 2, 2, 1, CHUNK, BLK), lambda i, xl: (i % 2, 0, i // 2, 0, 0)),
         ),
-        out_shape=pltpu.HBM((N_GROUP, 2, 2, CHUNK, BLK), BF16),
-        compiler_params=params(),
-        cost_estimate=pl.CostEstimate(flops=8 * tokens * BLK * BLK, bytes_accessed=10 * 2**20, transcendentals=0),
+        out_shape=pltpu.HBM((N_GROUP, 2, slabs, CHUNK, BLK), BF16),
+        compiler_params=params(),
+        cost_estimate=pl.CostEstimate(flops=4 * rows * tokens * BLK, bytes_accessed=16 * 2**20, transcendentals=0),
         name="partials",
     )(xl, x, own, other)
 
@@ -185,45 +185,27 @@
     return acc.astype(BF16)
 
 
-def reduce_kernel(x_ref, o_ref):
-    for slab in range(2):
-        o_ref[0, slab] = total(x_ref, slab)
-
-
-def reduce_half(x):
-    return pl.pallas_call(
-        reduce_kernel,
-        grid=(2,),
-        in_specs=[pl.BlockSpec((N_GROUP, 1, 2, CHUNK, BLK), lambda i: (0, i, 0, 0, 0))],
-        out_specs=pl.BlockSpec((1, 2, CHUNK, BLK), lambda i: (i, 0, 0, 0)),
-        out_shape=jax.ShapeDtypeStruct((2, 2, CHUNK, BLK), BF16),
-        name="reduce_half",
-    )(x)
-
-
-def route_kernel(owner_ref, first_ref, x_ref, o_ref):
-    base = 4 * pl.program_id(0)
+def route_kernel(owner_ref, x_ref, o_ref):
+    base = 2 * pl.program_id(0)
     for n in range(2):
-        for slab, value in ((base + n, first_ref[0, n]), (base + 2 + n, total(x_ref, n))):
-            o_ref[slab, 1] = value
-            o_ref[owner_ref[slab], 0] = value
-
-
-def route(owner, first, x):
+        value = total(x_ref, n)
+        o_ref[base + n, 1] = value
+        o_ref[owner_ref[base + n], 0] = value
+
+
+def route(owner, x):
     return pl.pallas_call(
         route_kernel,
         grid_spec=pltpu.PrefetchScalarGridSpec(
             num_scalar_prefetch=1,
-            grid=(2,),
-            in_specs=[
-                pl.BlockSpec((1, 2, CHUNK, BLK), lambda i, owner: (i, 0, 0, 0)),
-                pl.BlockSpec((N_GROUP, 1, 2, CHUNK, BLK), lambda i, owner: (0, i, 0, 0, 0)),
-            ],
+            grid=(4,),
+            in_specs=[pl.BlockSpec((N_GROUP, 1, 2, CHUNK, BLK), lambda i, owner: (0, i // 2, i % 2, 0, 0))],
             out_specs=pl.BlockSpec((N_GROUP, 2, CHUNK, BLK), lambda i, owner: (0, 0, 0, 0)),
         ),
         out_shape=pltpu.HBM((N_GROUP, 2, CHUNK, BLK), BF16),
+        compiler_params=params(),
         name="route",
-    )(owner, first, in_hbm(x))
+    )(owner, x)
 
 
 def inverse_fourth_root(statistic):
@@ -305,32 +287,24 @@
     count = lax.axis_size(FSDP) * width
     peers = lax.axis_size(("z", "core"))
 
+    other = lax.ppermute(cotangent, "xl", SWAP)
     block, squares = prepare(inputs, norm_gain)
     features = lax.all_gather(block, ("z", "core"), axis=0, tiled=True)
-    squares_other = lax.ppermute(squares, "xl", SWAP)
-    squares_other, cotangent = lax.optimization_barrier((squares_other, cotangent))
-    other = lax.ppermute(cotangent, "xl", SWAP)
+    squares = jnp.broadcast_to(squares, (peers, tokens))
+    squares = lax.all_to_all(squares, ("z", "core"), split_axis=0, concat_axis=0, tiled=True)
+    squares = jnp.sum(squares, axis=0, keepdims=True)
 
     roots = pack_roots(left_inverse, right_inverse)
+    roots, squares = lax.optimization_barrier((roots, squares))
+    scale = lax.rsqrt((squares + lax.ppermute(squares, "xl", SWAP)) / count + NORM_EPSILON)
     roots = lax.all_to_all(roots, GROUP, split_axis=0, concat_axis=0, tiled=True)
-    squares = jnp.broadcast_to(squares + squares_other, (peers, tokens))
-    roots, squares = lax.optimization_barrier((roots, squares))
-    squares = lax.all_to_all(squares, ("z", "core"), split_axis=0, concat_axis=0, tiled=True)
-    scale = lax.rsqrt(jnp.sum(squares, axis=0, keepdims=True) / count + NORM_EPSILON)
-    roots = pick(owner, roots)
-    roots, scale = lax.optimization_barrier((roots, scale))
-    roots = lax.all_to_all(roots, GROUP, split_axis=0, concat_axis=0, tiled=True)
-    own, other = scaled(scale, cotangent), scaled(scale, other)
-    roots, features = lax.optimization_barrier((roots, features))
-
-    halves = []
-    for half in range(2):
-        pieces = partials(xl, features, own, other, half)
-        shape = pieces.shape
-        pieces = pieces.reshape(2 * N_GROUP, *shape[2:])
-        pieces = lax.all_to_all(pieces, ("y", "xh", "xl"), split_axis=0, concat_axis=0, tiled=True)
-        halves.append(pieces.reshape(shape))
-    grads = route(owner, reduce_half(halves[0]), halves[1])
+    roots = lax.all_to_all(pick(owner, roots), GROUP, split_axis=0, concat_axis=0, tiled=True)
+
+    pieces = partials(xl, features, scaled(scale, cotangent), scaled(scale, other))
+    shape = pieces.shape
+    pieces, roots = lax.optimization_barrier((pieces.reshape(2 * N_GROUP, *shape[2:]), roots))
+    pieces = lax.all_to_all(pieces, ("y", "xh", "xl"), split_axis=0, concat_axis=0, tiled=True)
+    grads = route(owner, pieces.reshape(shape))
     grads = lax.all_to_all(grads, GROUP, split_axis=0, concat_axis=0, tiled=True)
     left_root, right_root = unpack_roots(roots)
     state = (left_stats, right_stats, left_inverse, right_inverse)

time: 228 us -> 191 us (0.84)
  the two profiles are of different devices: /device:TPU:1 before, /device:TPU:96 now
where the time goes in v5:
time: 191 us; the launch traced here: 190 us
  blocking collectives  58.2 us (30%)
  waiting for transfers between devices  49 us (26%)
  Pallas kernels  36.6 us (19%)
  starting transfers between devices  26.7 us (14%)
  between operations  14.8 us (8%)
  local copies, waits for them, and re-layouts  4.24 us (2%)
    all_to_all x1, blocking collectives, body(): lax.all_to_all(pieces, ('y', 'xh', 'xl'), split_axis=0, concat_axis=0, ti...  58.2 us
    ppermute x1, waiting for transfers between devices, body(): lax.ppermute(squares, 'xl', SWAP)  30.8 us
    all_to_all x1, waiting for transfers between devices, body(): lax.all_to_all(grads, GROUP, split_axis=0, concat_axis=0, tiled=True)  14 us
    pallas_call x1, Pallas kernels, partials(): pl.pallas_call(partial_kernel, grid_spec=pltpu.PrefetchScalarGridSpec(num...  12.8 us
    pallas_call x2, Pallas kernels, scaled(): pl.pallas_call(scale_kernel, grid=(4,), in_specs=[pl.BlockSpec((1, step),...  8.83 us
    all_to_all x1, starting transfers between devices, body(): lax.all_to_all(squares, ('z', 'core'), split_axis=0, concat_axis=0, tiled...  7.68 us
    pallas_call x1, Pallas kernels, block_step(): pl.pallas_call(block_kernel, in_specs=[SMEM, VMEM, VMEM, VMEM] + [HBM] *...  7.6 us
    all_to_all x1, starting transfers between devices, body(): lax.all_to_all(pick(owner, roots), GROUP, split_axis=0, concat_axis=0, ti...  6.97 us
  transfers between devices with their start and end apart: 7, of which 3 were waited for; matrix products, arithmetic and copies ran while one was open for 1% of the time, Pallas kernels for 13%

profile of v5, /device:TPU:96, one launch (start us, length us, event | category | flops | bytes accessed | tf_op | source)
XLA Modules:
  0.0 190.2 jit_solution(3293262718120875257)
XLA Ops:
  7.2 0.0 copy-start.2
  7.2 0.0 all-gather.2.cloned.1.call-start
  7.2 2.2 %prepare.1 = (bf16[128,2048]{1,0:T(8,128)(2,1)}, f32[1,2048]{1,0:T(1,128)}) custom-call(bf16[2048,128]{1,0:T(8,128)(2,1)} %x_ref.2, bf16[1,128]{1,0:T(2,128)(2,1)} %bitcast.14), custom_call_target="tpu_custom_call" | custom-call | tf_op jit(solution)/shard_map/prepare/pallas_call | solution.py:61
  9.5 0.0 all-gather.2.cloned.1.call-update
  9.5 1.6 collective-permute-start.1
  11.1 1.4 broadcast_in_dim.8
  12.5 7.7 %all-to-all-start = ((f32[16,1,2048]{2,1,0:T(1,128)}), f32[16,1,2048]{2,1,0:T(1,128)S(1)}, u32[]{:S(2)}, u32[]{:S(2)}) async-start(f32[16,1,2048]{2,1,0:T(1,128)} %broadcast_in_dim.8), calls=%async_computation | async-start | bytes 262144 | tf_op jit(solution)/shard_map/all_to_all | solution.py:294
  20.2 0.0 copy-start.3
  20.2 1.2 copy-done.3
  21.4 0.9 pack_roots.1
  22.3 4.2 %all-to-all-done = f32[16,1,2048]{2,1,0:T(1,128)S(1)} async-done(((f32[16,1,2048]{2,1,0:T(1,128)}), f32[16,1,2048]{2,1,0:T(1,128)S(1)}, u32[]{:S(2)}, u32[]{:S(2)}) %all-to-all-start) | async-done | bytes 131104 | tf_op jit(solution)/shard_map/all_to_all | solution.py:294
  26.5 0.1 reduce_sum.9
  26.6 6.6 %all-to-all-start.1 = ((bf16[8,80,512]{2,1,0:T(8,128)(2,1)}), bf16[8,80,512]{2,1,0:T(8,128)(2,1)S(1)}, u32[]{:S(2)}, u32[]{:S(2)}) async-start(bf16[8,80,512]{2,1,0:T(8,128)(2,1)} %pack_roots.1), calls=%async_computation.1 | async-start | bytes 1310720 | tf_op jit(solution)/shard_map/all_to_all | solution.py:300
  33.3 0.2 collective-permute-start
  33.5 30.8 %collective-permute-done = f32[1,2048]{1,0:T(1,128)S(1)} collective-permute-done((f32[1,2048]{1,0:T(1,128)S(1)}, f32[1,2048]{1,0:T(1,128)S(1)}, u32[]{:S(2)}, u32[]{:S(2)}) %collective-permute-start) | collective-permute-done | bytes 8224 | tf_op jit(solution)/shard_map/ppermute | solution.py:299
  64.4 0.6 add_rsqrt_fusion.scale_ref
  65.0 4.4 %scaled.2.own_ref = bf16[2048,512]{1,0:T(8,128)(2,1)} custom-call(f32[1,2048]{1,0:T(1,128)} %add_rsqrt_fusion.scale_ref, bf16[2048,512]{1,0:T(8,128)(2,1)} %x_ref.3), custom_call_target="tpu_custom_call" | custom-call | tf_op jit(solution)/shard_map/scaled/pallas_call | solution.py:146
  69.3 0.0 all-to-all-done.1.x_ref
  69.3 1.4 pick.1
  70.8 7.0 %all-to-all-start.2 = ((bf16[8,80,512]{2,1,0:T(8,128)(2,1)}), bf16[8,80,512]{2,1,0:T(8,128)(2,1)S(1)}, u32[]{:S(2)}, u32[]{:S(2)}) async-start(bf16[8,80,512]{2,1,0:T(8,128)(2,1)} %pick.1), calls=%async_computation.2 | async-start | bytes 1310720 | tf_op jit(solution)/shard_map/all_to_all | solution.py:301
  77.7 0.0 collective-permute-done.1.x_ref
  77.8 4.5 %scaled.3.other_ref = bf16[2048,512]{1,0:T(8,128)(2,1)} custom-call(f32[1,2048]{1,0:T(1,128)} %add_rsqrt_fusion.scale_ref, bf16[2048,512]{1,0:T(8,128)(2,1)} %collective-permute-done.1.x_ref), custom_call_target="tpu_custom_call" | custom-call | tf_op jit(solution)/shard_map/scaled/pallas_call | solution.py:146
  82.2 0.0 copy-done
  82.2 1.6 copy-done.1
  83.8 12.8 %partials.1 = bf16[8,2,4,64,512]{4,3,2,1,0:T(8,128)(2,1)} custom-call(s32[1]{0:T(128)} %bitcast.1.xl_ref, bf16[2048,2048]{1,0:T(8,128)(2,1)} %all-gather.2.cloned.1.call-done.x_ref, bf16[2048,512]{1,0:T(8,128)(2,1)S(1)} %copy-done, bf16[2048,512]{1,0:T(8,128)(2,1)S(1)} %copy-done.1), custom_call_target="tpu_custom_call" | custom-call | flops 8589934592 | bytes 16777216 | tf_op jit(solution)/shard_map/partials/pallas_call | solution.py:166
  96.6 0.0 all-to-all-done.2.x_ref
  96.6 58.2 %all_to_all.26 = bf16[16,4,64,512]{3,2,1,0:T(8,128)(2,1)S(1)} all-to-all(bf16[16,4,64,512]{3,2,1,0:T(8,128)(2,1)} %bitcast.10), channel_id=1, replica_groups=mesh['y'=4,'xh'=2,'xl'=2,'z'=8,'core'=2] {'y','xh','xl'}, dimensions={0} | all-to-all | bytes 8388608 | tf_op jit(solution)/shard_map/all_to_all | solution.py:306
  154.8 2.5 %route.1 = bf16[8,2,64,512]{3,2,1,0:T(8,128)(2,1)} custom-call(s32[8]{0:T(128)S(1)} %bitcast.9, bf16[8,2,4,64,512]{4,3,2,1,0:T(8,128)(2,1)S(1)} %bitcast.7), custom_call_target="tpu_custom_call" | custom-call | tf_op jit(solution)/shard_map/route/pallas_call | solution.py:197
  157.2 3.6 %all-to-all-start.4 = ((bf16[8,2,64,512]{3,2,1,0:T(8,128)(2,1)}), bf16[8,2,64,512]{3,2,1,0:T(8,128)(2,1)S(1)}, u32[]{:S(2)}, u32[]{:S(2)}) async-start(bf16[8,2,64,512]{3,2,1,0:T(8,128)(2,1)} %route.1), calls=%async_computation.4 | async-start | bytes 2097152 | tf_op jit(solution)/shard_map/all_to_all | solution.py:308
  161.4 0.3 unpack_roots.1
  161.7 14.0 %all-to-all-done.4.u_ref = bf16[8,2,64,512]{3,2,1,0:T(8,128)(2,1)S(1)} async-done(((bf16[8,2,64,512]{3,2,1,0:T(8,128)(2,1)}), bf16[8,2,64,512]{3,2,1,0:T(8,128)(2,1)S(1)}, u32[]{:S(2)}, u32[]{:S(2)}) %all-to-all-start.4) | async-done | bytes 1048608 | tf_op jit(solution)/shard_map/all_to_all | solution.py:308
  175.7 7.6 %block_step.1 = (bf16[512,512]{1,0:T(8,128)(2,1)}, f32[512,512]{1,0:T(8,128)}, f32[512,512]{1,0:T(8,128)}, f32[512,512]{1,0:T(8,128)}, f32[512,512]{1,0:T(8,128)}) custom-call(s32[1,1]{1,0:T(1,128)S(6)} %copy.16.refresh_ref, bf16[8,2,64,512]{3,2,1,0:T(8,128)(2,1)S(1)} %all-to-all-done.4.u_ref, bf16[512,512]{1,0:T(8,128)(2,1)S(1)} %get-tuple-element.19.lroot_ref, ...), custom_call_target="tpu_custom_call" | custom-call | flops 2147483648 | bytes 11534336 | tf_op jit(solution)/shard_map/block_step/pallas_call | solution.py:271
  (6 shorter events, 0.0 us)
Async XLA Ops:
  7.2 13.0 %copy-start.2 = (f32[512,512]{1,0:T(8,128)S(1)}, f32[512,512]{1,0:T(8,128)}, u32[]{:S(2)}) copy-start(f32[512,512]{1,0:T(8,128)} %li_ref.1) | copy-start | bytes 3145732
  7.2 75.0 %all-gather.2.cloned.1.call-start = ((), (), s32[]{:S(2)}) async-start(), calls=%async_computation.5 | async-start | bytes 8912896 | tf_op jit(solution)/shard_map/all_gather | solution.py:292
  9.5 68.3 %collective-permute-start.1 = (bf16[2048,512]{1,0:T(8,128)(2,1)}, bf16[2048,512]{1,0:T(8,128)(2,1)}, u32[]{:S(2)}, u32[]{:S(2)}) collective-permute-start(bf16[2048,512]{1,0:T(8,128)(2,1)} %x_ref.3), channel_id=1, source_target_pairs={{0,16},{16,0},{1,17},{17,1},{2,18},{18,2},{3,19},{19,3},{4,20},{20... | collective-permute-start | bytes 6291464 | tf_op jit(solution)/shard_map/ppermute | solution.py:290
  12.5 14.1 %all-to-all-start = ((f32[16,1,2048]{2,1,0:T(1,128)}), f32[16,1,2048]{2,1,0:T(1,128)S(1)}, u32[]{:S(2)}, u32[]{:S(2)}) async-start(f32[16,1,2048]{2,1,0:T(1,128)} %broadcast_in_dim.8), calls=%async_computation | async-start | bytes 262144 | tf_op jit(solution)/shard_map/all_to_all | solution.py:294
  20.2 1.2 copy-start.3
  26.6 42.7 %all-to-all-start.1 = ((bf16[8,80,512]{2,1,0:T(8,128)(2,1)}), bf16[8,80,512]{2,1,0:T(8,128)(2,1)S(1)}, u32[]{:S(2)}, u32[]{:S(2)}) async-start(bf16[8,80,512]{2,1,0:T(8,128)(2,1)} %pack_roots.1), calls=%async_computation.1 | async-start | bytes 1310720 | tf_op jit(solution)/shard_map/all_to_all | solution.py:300
  33.3 31.1 %collective-permute-start = (f32[1,2048]{1,0:T(1,128)S(1)}, f32[1,2048]{1,0:T(1,128)S(1)}, u32[]{:S(2)}, u32[]{:S(2)}) collective-permute-start(f32[1,2048]{1,0:T(1,128)S(1)} %bitcast.11), channel_id=1, source_target_pairs={{0,16},{16,0},{1,17},{17,1},{2,18},{18,2},{3,19},{19,3},{4,20},{20... | collective-permute-start | bytes 24584 | tf_op jit(solution)/shard_map/ppermute | solution.py:299
  65.0 4.4 %copy-start.4 = (s32[1,8]{1,0:T(1,128)S(1)}, s32[1,8]{1,0:T(1,128)}, u32[]{:S(2)}) copy-start(s32[1,8]{1,0:T(1,128)} %param.12) | copy-start | bytes 100
  70.8 25.8 %all-to-all-start.2 = ((bf16[8,80,512]{2,1,0:T(8,128)(2,1)}), bf16[8,80,512]{2,1,0:T(8,128)(2,1)S(1)}, u32[]{:S(2)}, u32[]{:S(2)}) async-start(bf16[8,80,512]{2,1,0:T(8,128)(2,1)} %pick.1), calls=%async_computation.2 | async-start | bytes 1310720 | tf_op jit(solution)/shard_map/all_to_all | solution.py:301
  77.7 4.5 %copy-start = (bf16[2048,512]{1,0:T(8,128)(2,1)S(1)}, bf16[2048,512]{1,0:T(8,128)(2,1)}, u32[]{:S(2)}) copy-start(bf16[2048,512]{1,0:T(8,128)(2,1)} %scaled.2.own_ref) | copy-start | bytes 6291460
  82.2 1.6 copy-start.1
  157.2 18.5 %all-to-all-start.4 = ((bf16[8,2,64,512]{3,2,1,0:T(8,128)(2,1)}), bf16[8,2,64,512]{3,2,1,0:T(8,128)(2,1)S(1)}, u32[]{:S(2)}, u32[]{:S(2)}) async-start(bf16[8,2,64,512]{3,2,1,0:T(8,128)(2,1)} %route.1), calls=%async_computation.4 | async-start | bytes 2097152 | tf_op jit(solution)/shard_map/all_to_all | solution.py:308
Sparse Core Ops, SparseCore 0:
  10.4 57.3 all-gather.1

commit v6 on v5

--- a/solution.py
+++ b/solution.py
@@ -134,48 +134,37 @@
     )(x)
 
 
-def scale_kernel(scale_ref, x_ref, o_ref):
-    column = jnp.broadcast_to(scale_ref[...], (8, scale_ref.shape[1])).T[:, :1]
-    o_ref[...] = (x_ref[...].astype(F32) * column).astype(BF16)
-
-
-def scaled(scale, x):
-    tokens, cols = x.shape
-    step = tokens // 4
-    block = pl.BlockSpec((step, cols), lambda i: (i, 0))
-    return pl.pallas_call(
-        scale_kernel,
-        grid=(4,),
-        in_specs=[pl.BlockSpec((1, step), lambda i: (0, i)), block],
-        out_specs=block,
-        out_shape=jax.ShapeDtypeStruct(x.shape, BF16),
-        name="scaled",
-    )(scale, x)
-
-
-def partial_kernel(xl_ref, x_ref, own_ref, other_ref, o_ref):
-    for cot_ref, place in ((own_ref, xl_ref[0]), (other_ref, 1 - xl_ref[0])):
-        part = dot(x_ref[...], cot_ref[...]).astype(BF16)
-        for j in range(part.shape[0] // CHUNK):
-            o_ref[j, place, 0] = part[j * CHUNK : (j + 1) * CHUNK]
-
-
-def partials(xl, x, own, other):
+def partial_kernel(place_ref, x_ref, scale_ref, cot_ref, *refs):
+    o_ref, scaled = refs[-2:]
+
+    @pl.when(pl.program_id(0) == 0)
+    def _():
+        column = jnp.broadcast_to(scale_ref[...], (8, scale_ref.shape[1])).T[:, :1]
+        scaled[...] = (cot_ref[...].astype(F32) * column).astype(BF16)
+
+    part = dot(x_ref[...], scaled[...]).astype(BF16)
+    for j in range(N_GROUP):
+        o_ref[j, 0, 0] = part[j * CHUNK : (j + 1) * CHUNK]
+
+
+def partials(place, x, scale, cot, *filled):
     rows, tokens = x.shape
     slabs = rows // BLK
     return pl.pallas_call(
         partial_kernel,
         grid_spec=pltpu.PrefetchScalarGridSpec(
             num_scalar_prefetch=1,
-            grid=(2 * slabs,),
-            in_specs=[pl.BlockSpec((BLK // 2, tokens), lambda i, xl: (i, 0)), VMEM, VMEM],
-            out_specs=pl.BlockSpec((N_GROUP // 2, 2, 1, CHUNK, BLK), lambda i, xl: (i % 2, 0, i // 2, 0, 0)),
+            grid=(slabs,),
+            in_specs=[pl.BlockSpec((BLK, tokens), lambda i, place: (i, 0)), VMEM, VMEM] + [HBM] * len(filled),
+            out_specs=pl.BlockSpec((N_GROUP, 1, 1, CHUNK, BLK), lambda i, place: (0, place[0], i, 0, 0)),
+            scratch_shapes=[pltpu.VMEM((tokens, BLK), BF16)],
         ),
         out_shape=pltpu.HBM((N_GROUP, 2, slabs, CHUNK, BLK), BF16),
-        compiler_params=params(),
-        cost_estimate=pl.CostEstimate(flops=4 * rows * tokens * BLK, bytes_accessed=16 * 2**20, transcendentals=0),
+        input_output_aliases={4: 0} if filled else {},
+        compiler_params=params(),
+        cost_estimate=pl.CostEstimate(flops=2 * rows * tokens * BLK, bytes_accessed=12 * 2**20, transcendentals=0),
         name="partials",
-    )(xl, x, own, other)
+    )(place, x, scale, cot, *filled)
 
 
 def total(x_ref, slab):
@@ -287,20 +276,23 @@
     count = lax.axis_size(FSDP) * width
     peers = lax.axis_size(("z", "core"))
 
-    other = lax.ppermute(cotangent, "xl", SWAP)
     block, squares = prepare(inputs, norm_gain)
     features = lax.all_gather(block, ("z", "core"), axis=0, tiled=True)
-    squares = jnp.broadcast_to(squares, (peers, tokens))
+    squares_other = lax.ppermute(squares, "xl", SWAP)
+    roots = pack_roots(left_inverse, right_inverse)
+    roots = lax.all_to_all(roots, GROUP, split_axis=0, concat_axis=0, tiled=True)
+    roots, other, squares, squares_other = lax.optimization_barrier((roots, cotangent, squares, squares_other))
+    other = lax.ppermute(other, "xl", SWAP)
+    squares = jnp.broadcast_to(squares + squares_other, (peers, tokens))
     squares = lax.all_to_all(squares, ("z", "core"), split_axis=0, concat_axis=0, tiled=True)
-    squares = jnp.sum(squares, axis=0, keepdims=True)
-
-    roots = pack_roots(left_inverse, right_inverse)
-    roots, squares = lax.optimization_barrier((roots, squares))
-    scale = lax.rsqrt((squares + lax.ppermute(squares, "xl", SWAP)) / count + NORM_EPSILON)
+    scale = lax.rsqrt(jnp.sum(squares, axis=0, keepdims=True) / count + NORM_EPSILON)
+    roots = pick(owner, roots)
+    roots, scale = lax.optimization_barrier((roots, scale))
     roots = lax.all_to_all(roots, GROUP, split_axis=0, concat_axis=0, tiled=True)
-    roots = lax.all_to_all(pick(owner, roots), GROUP, split_axis=0, concat_axis=0, tiled=True)
-
-    pieces = partials(xl, features, scaled(scale, cotangent), scaled(scale, other))
+
+    pieces = partials(xl, features, scale, cotangent)
+    pieces, other = lax.optimization_barrier((pieces, other))
+    pieces = partials(1 - xl, features, scale, other, pieces)
     shape = pieces.shape
     pieces, roots = lax.optimization_barrier((pieces.reshape(2 * N_GROUP, *shape[2:]), roots))
     pieces = lax.all_to_all(pieces, ("y", "xh", "xl"), split_axis=0, concat_axis=0, tiled=True)

time: 191 us -> 186 us (0.974)
  the two profiles are of different devices: /device:TPU:96 before, /device:TPU:1 now
where the time goes in v6:
time: 186 us; the launch traced here: 185 us
  blocking collectives  56.7 us (30%)
  waiting for transfers between devices  49.8 us (27%)
  Pallas kernels  32.6 us (18%)
  starting transfers between devices  26.3 us (14%)
  between operations  14.8 us (8%)
  local copies, waits for them, and re-layouts  4.77 us (3%)
    all_to_all x1, blocking collectives, body(): lax.all_to_all(pieces, ('y', 'xh', 'xl'), split_axis=0, concat_axis=0, ti...  56.7 us
    pallas_call x2, Pallas kernels, partials(): pl.pallas_call(partial_kernel, grid_spec=pltpu.PrefetchScalarGridSpec(num...  17.7 us
    all_gather x1, waiting for transfers between devices, body(): features = lax.all_gather(block, ('z', 'core'), axis=0, tiled=True)  14.9 us
    all_to_all x1, waiting for transfers between devices, body(): lax.all_to_all(grads, GROUP, split_axis=0, concat_axis=0, tiled=True)  14.3 us
    all_to_all x2, starting transfers between devices, body(): lax.all_to_all(roots, GROUP, split_axis=0, concat_axis=0, tiled=True)  11 us
    all_to_all x1, starting transfers between devices, body(): lax.all_to_all(squares, ('z', 'core'), split_axis=0, concat_axis=0, tiled...  11 us
    all_to_all x1, waiting for transfers between devices, body(): lax.all_to_all(squares, ('z', 'core'), split_axis=0, concat_axis=0, tiled...  9.21 us
    pallas_call x1, Pallas kernels, block_step(): pl.pallas_call(block_kernel, in_specs=[SMEM, VMEM, VMEM, VMEM] + [HBM] *...  7.61 us
  transfers between devices with their start and end apart: 7, of which 5 were waited for; matrix products, arithmetic and copies ran while one was open for 0% of the time, Pallas kernels for 11%

profile of v6, /device:TPU:1, one launch (start us, length us, event | category | flops | bytes accessed | tf_op | source)
XLA Modules:
  0.0 185.1 jit_solution(11550813102093751227)
XLA Ops:
  7.2 0.0 copy-start.2
  7.2 0.0 all-gather.2.cloned.1.call-start
  7.2 2.2 %prepare.1 = (bf16[128,2048]{1,0:T(8,128)(2,1)}, f32[1,2048]{1,0:T(1,128)}) custom-call(bf16[2048,128]{1,0:T(8,128)(2,1)} %x_ref.1, bf16[1,128]{1,0:T(2,128)(2,1)} %bitcast.14), custom_call_target="tpu_custom_call" | custom-call | tf_op jit(solution)/shard_map/prepare/pallas_call | solution.py:61
  9.4 0.0 all-gather.2.cloned.1.call-update
  9.4 0.0 copy-start
  9.4 1.2 copy-done
  10.6 1.2 copy-done.1
  11.9 1.0 pack_roots.1
  12.8 7.5 %all-to-all-start = ((bf16[8,80,512]{2,1,0:T(8,128)(2,1)}), bf16[8,80,512]{2,1,0:T(8,128)(2,1)S(1)}, u32[]{:S(2)}, u32[]{:S(2)}) async-start(bf16[8,80,512]{2,1,0:T(8,128)(2,1)} %pack_roots.1), calls=%async_computation | async-start | bytes 1310720 | tf_op jit(solution)/shard_map/all_to_all | solution.py:283
  20.3 0.0 copy-done.4
  20.3 0.4 collective-permute-start
  20.7 7.4 %collective-permute-done = f32[1,2048]{1,0:T(1,128)S(1)} collective-permute-done((f32[1,2048]{1,0:T(1,128)S(1)}, f32[1,2048]{1,0:T(1,128)S(1)}, u32[]{:S(2)}, u32[]{:S(2)}) %collective-permute-start) | collective-permute-done | bytes 8224 | tf_op jit(solution)/shard_map/ppermute | solution.py:281
  28.1 4.0 %all-to-all-done.x_ref = bf16[8,80,512]{2,1,0:T(8,128)(2,1)S(1)} async-done(((bf16[8,80,512]{2,1,0:T(8,128)(2,1)}), bf16[8,80,512]{2,1,0:T(8,128)(2,1)S(1)}, u32[]{:S(2)}, u32[]{:S(2)}) %all-to-all-start) | async-done | bytes 655392 | tf_op jit(solution)/shard_map/all_to_all | solution.py:283
  32.1 0.3 collective-permute-start.1
  32.4 0.7 broadcast_in_dim.2
  33.1 11.0 %all-to-all-start.1 = ((f32[16,1,2048]{2,1,0:T(1,128)}), f32[16,1,2048]{2,1,0:T(1,128)S(1)}, u32[]{:S(2)}, u32[]{:S(2)}) async-start(f32[16,1,2048]{2,1,0:T(1,128)} %broadcast_in_dim.2), calls=%async_computation.1 | async-start | bytes 262144 | tf_op jit(solution)/shard_map/all_to_all | solution.py:287
  44.1 1.4 pick.1
  45.6 9.2 %all-to-all-done.1 = f32[16,1,2048]{2,1,0:T(1,128)S(1)} async-done(((f32[16,1,2048]{2,1,0:T(1,128)}), f32[16,1,2048]{2,1,0:T(1,128)S(1)}, u32[]{:S(2)}, u32[]{:S(2)}) %all-to-all-start.1) | async-done | bytes 131104 | tf_op jit(solution)/shard_map/all_to_all | solution.py:287
  54.8 0.1 reduce_sum.9
  54.9 3.6 %all-to-all-start.2 = ((bf16[8,80,512]{2,1,0:T(8,128)(2,1)}), bf16[8,80,512]{2,1,0:T(8,128)(2,1)S(1)}, u32[]{:S(2)}, u32[]{:S(2)}) async-start(bf16[8,80,512]{2,1,0:T(8,128)(2,1)} %pick.1), calls=%async_computation.2 | async-start | bytes 1310720 | tf_op jit(solution)/shard_map/all_to_all | solution.py:291
  58.5 14.9 %all-gather.2.cloned.1.call-done.x_ref = bf16[2048,2048]{1,0:T(8,128)(2,1)} async-done(((bf16[128,2048]{1,0:T(8,128)(2,1)}), bf16[2048,2048]{1,0:T(8,128)(2,1)}) %all-gather.2.cloned.1.call-update) | async-done | bytes 8388624 | tf_op jit(solution)/shard_map/all_gather | solution.py:280
  73.4 1.6 copy-done.3
  75.0 8.8 %partials.2.refs_0_ = bf16[8,2,4,64,512]{4,3,2,1,0:T(8,128)(2,1)} custom-call(s32[1]{0:T(128)} %bitcast.1.place_ref, bf16[2048,2048]{1,0:T(8,128)(2,1)} %all-gather.2.cloned.1.call-done.x_ref, f32[1,2048]{1,0:T(1,128)S(1)} %bitcast.8, bf16[2048,512]{1,0:T(8,128)(2,1)S(1)} %copy-done.3), custom_call_target="tpu_custom_call" | custom-call | flops 4294967296 | bytes 12582912 | tf_op jit(solution)/shard_map/partials/pallas_call | solution.py:153
  83.8 0.0 collective-permute-done.1.cot_ref
  83.8 8.8 %partials.3 = bf16[8,2,4,64,512]{4,3,2,1,0:T(8,128)(2,1)} custom-call(s32[1]{0:T(128)S(6)} %sub.3.place_ref, bf16[2048,2048]{1,0:T(8,128)(2,1)} %all-gather.2.cloned.1.call-done.x_ref, f32[1,2048]{1,0:T(1,128)S(1)} %bitcast.9, bf16[2048,512]{1,0:T(8,128)(2,1)S(1)} %collective-permute-done.1.cot_ref, ...), custom_call_target="tpu_custom_call", output_to_operand_aliasing={{}: (4, {})} | custom-call | flops 4294967296 | bytes 12582912 | tf_op jit(solution)/shard_map/partials/pallas_call | solution.py:153
  92.7 0.0 all-to-all-done.2.x_ref
  92.7 56.7 %all_to_all.26 = bf16[16,4,64,512]{3,2,1,0:T(8,128)(2,1)S(1)} all-to-all(bf16[16,4,64,512]{3,2,1,0:T(8,128)(2,1)} %bitcast.12), channel_id=1, replica_groups=mesh['y'=4,'xh'=2,'xl'=2,'z'=8,'core'=2] {'y','xh','xl'}, dimensions={0} | all-to-all | bytes 8388608 | tf_op jit(solution)/shard_map/all_to_all | solution.py:298
  149.3 2.5 %route.1 = bf16[8,2,64,512]{3,2,1,0:T(8,128)(2,1)} custom-call(s32[8]{0:T(128)S(1)} %bitcast.11, bf16[8,2,4,64,512]{4,3,2,1,0:T(8,128)(2,1)S(1)} %bitcast.7), custom_call_target="tpu_custom_call" | custom-call | tf_op jit(solution)/shard_map/route/pallas_call | solution.py:186
  151.8 3.6 %all-to-all-start.4 = ((bf16[8,2,64,512]{3,2,1,0:T(8,128)(2,1)}), bf16[8,2,64,512]{3,2,1,0:T(8,128)(2,1)S(1)}, u32[]{:S(2)}, u32[]{:S(2)}) async-start(bf16[8,2,64,512]{3,2,1,0:T(8,128)(2,1)} %route.1), calls=%async_computation.4 | async-start | bytes 2097152 | tf_op jit(solution)/shard_map/all_to_all | solution.py:300
  156.0 0.3 unpack_roots.1
  156.3 14.3 %all-to-all-done.4.u_ref = bf16[8,2,64,512]{3,2,1,0:T(8,128)(2,1)S(1)} async-done(((bf16[8,2,64,512]{3,2,1,0:T(8,128)(2,1)}), bf16[8,2,64,512]{3,2,1,0:T(8,128)(2,1)S(1)}, u32[]{:S(2)}, u32[]{:S(2)}) %all-to-all-start.4) | async-done | bytes 1048608 | tf_op jit(solution)/shard_map/all_to_all | solution.py:300
  170.6 7.6 %block_step.1 = (bf16[512,512]{1,0:T(8,128)(2,1)}, f32[512,512]{1,0:T(8,128)}, f32[512,512]{1,0:T(8,128)}, f32[512,512]{1,0:T(8,128)}, f32[512,512]{1,0:T(8,128)}) custom-call(s32[1,1]{1,0:T(1,128)S(6)} %copy.18.refresh_ref, bf16[8,2,64,512]{3,2,1,0:T(8,128)(2,1)S(1)} %all-to-all-done.4.u_ref, bf16[512,512]{1,0:T(8,128)(2,1)S(1)} %get-tuple-element.31.lroot_ref, ...), custom_call_target="tpu_custom_call" | custom-call | flops 2147483648 | bytes 11534336 | tf_op jit(solution)/shard_map/block_step/pallas_call | solution.py:260
  (6 shorter events, 0.0 us)
Async XLA Ops:
  7.2 37.0 %copy-start.2 = (s32[1,8]{1,0:T(1,128)S(1)}, s32[1,8]{1,0:T(1,128)}, u32[]{:S(2)}) copy-start(s32[1,8]{1,0:T(1,128)} %param.12) | copy-start | bytes 100
  7.2 66.2 %all-gather.2.cloned.1.call-start = ((), (), s32[]{:S(2)}) async-start(), calls=%async_computation.5 | async-start | bytes 8912896 | tf_op jit(solution)/shard_map/all_gather | solution.py:280
  9.4 10.9 %copy-start.4 = (f32[1,2048]{1,0:T(1,128)S(1)}, f32[1,2048]{1,0:T(1,128)}, u32[]{:S(2)}) copy-start(f32[1,2048]{1,0:T(1,128)} %get-tuple-element.22) | copy-start | bytes 24580
  9.4 1.2 copy-start
  10.6 1.2 copy-start.1
  12.8 19.3 %all-to-all-start = ((bf16[8,80,512]{2,1,0:T(8,128)(2,1)}), bf16[8,80,512]{2,1,0:T(8,128)(2,1)S(1)}, u32[]{:S(2)}, u32[]{:S(2)}) async-start(bf16[8,80,512]{2,1,0:T(8,128)(2,1)} %pack_roots.1), calls=%async_computation | async-start | bytes 1310720 | tf_op jit(solution)/shard_map/all_to_all | solution.py:283
  20.3 7.8 %collective-permute-start = (f32[1,2048]{1,0:T(1,128)S(1)}, f32[1,2048]{1,0:T(1,128)S(1)}, u32[]{:S(2)}, u32[]{:S(2)}) collective-permute-start(f32[1,2048]{1,0:T(1,128)S(1)} %copy-done.4), channel_id=1, source_target_pairs={{0,16},{16,0},{1,17},{17,1},{2,18},{18,2},{3,19},{19,3},{4,20},{20... | collective-permute-start | bytes 24584 | tf_op jit(solution)/shard_map/ppermute | solution.py:281
  32.1 51.7 %collective-permute-start.1 = (bf16[2048,512]{1,0:T(8,128)(2,1)}, bf16[2048,512]{1,0:T(8,128)(2,1)S(1)}, u32[]{:S(2)}, u32[]{:S(2)}) collective-permute-start(bf16[2048,512]{1,0:T(8,128)(2,1)} %cot_ref.1), channel_id=1, source_target_pairs={{0,16},{16,0},{1,17},{17,1},{2,18},{18,2},{3,19},{19,3},{4,20},{20... | collective-permute-start | bytes 6291464 | tf_op jit(solution)/shard_map/ppermute | solution.py:285
  33.1 21.6 %all-to-all-start.1 = ((f32[16,1,2048]{2,1,0:T(1,128)}), f32[16,1,2048]{2,1,0:T(1,128)S(1)}, u32[]{:S(2)}, u32[]{:S(2)}) async-start(f32[16,1,2048]{2,1,0:T(1,128)} %broadcast_in_dim.2), calls=%async_computation.1 | async-start | bytes 262144 | tf_op jit(solution)/shard_map/all_to_all | solution.py:287
  54.9 37.8 %all-to-all-start.2 = ((bf16[8,80,512]{2,1,0:T(8,128)(2,1)}), bf16[8,80,512]{2,1,0:T(8,128)(2,1)S(1)}, u32[]{:S(2)}, u32[]{:S(2)}) async-start(bf16[8,80,512]{2,1,0:T(8,128)(2,1)} %pick.1), calls=%async_computation.2 | async-start | bytes 1310720 | tf_op jit(solution)/shard_map/all_to_all | solution.py:291
  73.4 1.6 copy-start.3
  151.8 18.8 %all-to-all-start.4 = ((bf16[8,2,64,512]{3,2,1,0:T(8,128)(2,1)}), bf16[8,2,64,512]{3,2,1,0:T(8,128)(2,1)S(1)}, u32[]{:S(2)}, u32[]{:S(2)}) async-start(bf16[8,2,64,512]{3,2,1,0:T(8,128)(2,1)} %route.1), calls=%async_computation.4 | async-start | bytes 2097152 | tf_op jit(solution)/shard_map/all_to_all | solution.py:300
Sparse Core Ops, SparseCore 0:
  10.4 62.9 all-gather.1

commit v7 on v6

--- a/solution.py
+++ b/solution.py
@@ -47,12 +47,8 @@
     return high, (a - high.astype(F32)).astype(BF16)
 
 
-def prepare_kernel(x_ref, gain_ref, xt_ref, sq_ref):
-    values = x_ref[...].astype(F32)
-    xt_ref[...] = (values * gain_ref[...].astype(F32)).astype(BF16).T
-    high, low = split2(values * values)
-    ones = jnp.ones((8, values.shape[1]), BF16)
-    sq_ref[...] = (dot_dims(ones, high, NT) + dot_dims(ones, low, NT))[:1]
+def prepare_kernel(x_ref, gain_ref, xt_ref):
+    xt_ref[...] = (x_ref[...].astype(F32) * gain_ref[...].astype(F32)).astype(BF16).T
 
 
 def prepare(x, gain):
@@ -62,8 +58,8 @@
         prepare_kernel,
         grid=(2,),
         in_specs=[pl.BlockSpec((step, width), lambda i: (i, 0)), pl.BlockSpec((1, width), lambda i: (0, 0))],
-        out_specs=[pl.BlockSpec((width, step), lambda i: (0, i)), pl.BlockSpec((1, step), lambda i: (0, i))],
-        out_shape=[pltpu.HBM((width, tokens), BF16), jax.ShapeDtypeStruct((1, tokens), F32)],
+        out_specs=pl.BlockSpec((width, step), lambda i: (0, i)),
+        out_shape=pltpu.HBM((width, tokens), BF16),
         name="prepare",
     )(x, gain.reshape(1, width))
 
@@ -74,11 +70,15 @@
     return rows, cols
 
 
-def pack_roots_kernel(l_ref, r_ref, o_ref):
+def pack_roots_kernel(l_ref, r_ref, o_ref, left, right, sems):
+    copies = [pltpu.make_async_copy(l_ref, left, sems.at[0]), pltpu.make_async_copy(r_ref, right, sems.at[1])]
+    for copy in copies:
+        copy.start()
+    for copy in copies:
+        copy.wait()
     rows, cols = triangle()
-    left = l_ref[...]
-    packed = jnp.where(cols > rows, left, r_ref[...]).astype(BF16)
-    diagonal = jnp.sum(jnp.where(cols == rows, left, 0.0), axis=0, keepdims=True)
+    packed = jnp.where(cols > rows, left[...], right[...]).astype(BF16)
+    diagonal = jnp.sum(jnp.where(cols == rows, left[...], 0.0), axis=0, keepdims=True)
     diagonal = jnp.broadcast_to(diagonal, (PACKED - CHUNK, BLK)).astype(BF16)
     for i in range(N_GROUP):
         o_ref[i, :CHUNK] = packed[i * CHUNK : (i + 1) * CHUNK]
@@ -88,12 +88,13 @@
 def pack_roots(left, right):
     return pl.pallas_call(
         pack_roots_kernel,
-        in_specs=[VMEM, VMEM],
+        in_specs=[HBM, HBM],
         out_specs=VMEM,
         out_shape=pltpu.HBM((N_GROUP, PACKED, BLK), BF16),
+        scratch_shapes=[pltpu.VMEM((BLK, BLK), F32)] * 2 + [pltpu.SemaphoreType.DMA((2,))],
         compiler_params=params(),
         name="pack_roots",
-    )(left, right)
+    )(in_hbm(left), in_hbm(right))
 
 
 def pick_kernel(owner_ref, x_ref, o_ref):
@@ -134,37 +135,85 @@
     )(x)
 
 
-def partial_kernel(place_ref, x_ref, scale_ref, cot_ref, *refs):
-    o_ref, scaled = refs[-2:]
-
-    @pl.when(pl.program_id(0) == 0)
-    def _():
-        column = jnp.broadcast_to(scale_ref[...], (8, scale_ref.shape[1])).T[:, :1]
-        scaled[...] = (cot_ref[...].astype(F32) * column).astype(BF16)
-
-    part = dot(x_ref[...], scaled[...]).astype(BF16)
+def column_of(scale_ref):
+    return jnp.broadcast_to(scale_ref[...], (8, scale_ref.shape[1])).T[:, :1]
+
+
+def scale_kernel(scale_ref, x_ref, o_ref):
+    o_ref[...] = (x_ref[...].astype(F32) * column_of(scale_ref)).astype(BF16)
+
+
+def scaled(scale, x):
+    return pl.pallas_call(
+        scale_kernel,
+        in_specs=[VMEM, VMEM],
+        out_specs=VMEM,
+        out_shape=pltpu.HBM(x.shape, BF16),
+        compiler_params=params(),
+        name="scaled",
+    )(scale, x)
+
+
+def put_rows(o_ref, part):
+    part = part.astype(BF16)
     for j in range(N_GROUP):
         o_ref[j, 0, 0] = part[j * CHUNK : (j + 1) * CHUNK]
 
 
-def partials(place, x, scale, cot, *filled):
+def own_kernel(place_ref, x_ref, cot_ref, o_ref, local_ref, sems):
+    @pl.when(pl.program_id(0) == 0)
+    def _():
+        spans = [pl.ds(first, BLK) for first in range(0, cot_ref.shape[0], BLK)]
+        copies = [pltpu.make_async_copy(cot_ref.at[s], local_ref.at[s], sems.at[n]) for n, s in enumerate(spans)]
+        for copy in copies:
+            copy.start()
+        part = jnp.zeros((BLK, BLK), F32)
+        for copy, span in zip(copies, spans):
+            copy.wait()
+            part = part + dot(x_ref[:, span], local_ref[span])
+        put_rows(o_ref, part)
+
+    @pl.when(pl.program_id(0) > 0)
+    def _():
+        put_rows(o_ref, dot(x_ref[...], local_ref[...]))
+
+
+def other_kernel(place_ref, x_ref, cot_ref, scale_ref, filled_ref, o_ref, scaled_ref):
+    @pl.when(pl.program_id(0) == 0)
+    def _():
+        column = column_of(scale_ref)
+        part = jnp.zeros((BLK, BLK), F32)
+        for first in range(0, cot_ref.shape[0], BLK):
+            span = slice(first, first + BLK)
+            piece = (cot_ref[span].astype(F32) * column[span]).astype(BF16)
+            scaled_ref[span] = piece
+            part = part + dot(x_ref[:, span], piece)
+        put_rows(o_ref, part)
+
+    @pl.when(pl.program_id(0) > 0)
+    def _():
+        put_rows(o_ref, dot(x_ref[...], scaled_ref[...]))
+
+
+def partials(place, x, cot, *rest):
     rows, tokens = x.shape
     slabs = rows // BLK
     return pl.pallas_call(
-        partial_kernel,
+        other_kernel if rest else own_kernel,
         grid_spec=pltpu.PrefetchScalarGridSpec(
             num_scalar_prefetch=1,
             grid=(slabs,),
-            in_specs=[pl.BlockSpec((BLK, tokens), lambda i, place: (i, 0)), VMEM, VMEM] + [HBM] * len(filled),
+            in_specs=[pl.BlockSpec((BLK, tokens), lambda i, place: (i, 0))] + ([VMEM, VMEM, HBM] if rest else [HBM]),
             out_specs=pl.BlockSpec((N_GROUP, 1, 1, CHUNK, BLK), lambda i, place: (0, place[0], i, 0, 0)),
-            scratch_shapes=[pltpu.VMEM((tokens, BLK), BF16)],
+            scratch_shapes=[pltpu.VMEM((tokens, BLK), BF16)]
+            + ([] if rest else [pltpu.SemaphoreType.DMA((tokens // BLK,))]),
         ),
         out_shape=pltpu.HBM((N_GROUP, 2, slabs, CHUNK, BLK), BF16),
-        input_output_aliases={4: 0} if filled else {},
+        input_output_aliases={4: 0} if rest else {},
         compiler_params=params(),
         cost_estimate=pl.CostEstimate(flops=2 * rows * tokens * BLK, bytes_accessed=12 * 2**20, transcendentals=0),
         name="partials",
-    )(place, x, scale, cot, *filled)
+    )(place, x, cot if rest else in_hbm(cot), *rest)
 
 
 def total(x_ref, slab):
@@ -276,10 +325,11 @@
     count = lax.axis_size(FSDP) * width
     peers = lax.axis_size(("z", "core"))
 
-    block, squares = prepare(inputs, norm_gain)
-    features = lax.all_gather(block, ("z", "core"), axis=0, tiled=True)
+    features = lax.all_gather(prepare(inputs, norm_gain), ("z", "core"), axis=0, tiled=True)
+    values = inputs.astype(F32)
+    squares = jnp.sum(values * values, axis=1).reshape(1, tokens)
+    roots = pack_roots(left_inverse, right_inverse)
     squares_other = lax.ppermute(squares, "xl", SWAP)
-    roots = pack_roots(left_inverse, right_inverse)
     roots = lax.all_to_all(roots, GROUP, split_axis=0, concat_axis=0, tiled=True)
     roots, other, squares, squares_other = lax.optimization_barrier((roots, cotangent, squares, squares_other))
     other = lax.ppermute(other, "xl", SWAP)
@@ -290,9 +340,9 @@
     roots, scale = lax.optimization_barrier((roots, scale))
     roots = lax.all_to_all(roots, GROUP, split_axis=0, concat_axis=0, tiled=True)
 
-    pieces = partials(xl, features, scale, cotangent)
+    pieces = partials(xl, features, scaled(scale, cotangent))
     pieces, other = lax.optimization_barrier((pieces, other))
-    pieces = partials(1 - xl, features, scale, other, pieces)
+    pieces = partials(1 - xl, features, other, scale, pieces)
     shape = pieces.shape
     pieces, roots = lax.optimization_barrier((pieces.reshape(2 * N_GROUP, *shape[2:]), roots))
     pieces = lax.all_to_all(pieces, ("y", "xh", "xl"), split_axis=0, concat_axis=0, tiled=True)

time: 186 us -> 184 us (0.989); the launches traced: 185 us -> 181 us
  waiting for transfers between devices: 49.8 us -> 46.9 us
  local copies, waits for them, and re-layouts: 4.77 us -> 2.33 us
    pallas_call x3 -> x4, Pallas kernels: 18.6 us -> 22.6 us  [the longest x2 18 us: partials(): pl.pallas_call(other_kernel if rest else own_kernel, grid_spec=pltpu.Pref...]
    pallas_call x1, Pallas kernels: 7.61 us -> 4.76 us  [block_step(): pl.pallas_call(block_kernel, in_specs=[SMEM, VMEM, VMEM, VMEM] + [HBM] *...]
    all_gather x1, waiting for transfers between devices: 14.9 us -> 12.3 us  [body(): lax.all_gather(prepare(inputs, norm_gain), ('z', 'core'), axis=0, tiled=T...]
    unnamed x10 -> x6, local copies, waits for them, and re-layouts: 4.04 us -> 1.61 us
  transfers between devices with their start and end apart: 7 -> 7, of which waited for: 5 -> 5; matrix products, arithmetic and copies ran while one was open for 0% -> 1% of each run, Pallas kernels for 11% -> 13%
where the time goes in v7:
time: 184 us; the launch traced here: 181 us
  blocking collectives  56.7 us (31%)
  waiting for transfers between devices  46.9 us (25%)
  Pallas kernels  33.5 us (18%)
  starting transfers between devices  26.3 us (14%)
  between operations  14.8 us (8%)
  local copies, waits for them, and re-layouts  2.33 us (1%)
    all_to_all x1, blocking collectives, body(): lax.all_to_all(pieces, ('y', 'xh', 'xl'), split_axis=0, concat_axis=0, ti...  56.7 us
    pallas_call x2, Pallas kernels, partials(): pl.pallas_call(other_kernel if rest else own_kernel, grid_spec=pltpu.Pref...  18 us
    all_to_all x1, waiting for transfers between devices, body(): lax.all_to_all(grads, GROUP, split_axis=0, concat_axis=0, tiled=True)  14.3 us
    all_gather x1, waiting for transfers between devices, body(): lax.all_gather(prepare(inputs, norm_gain), ('z', 'core'), axis=0, tiled=T...  12.3 us
    all_to_all x2, starting transfers between devices, body(): lax.all_to_all(roots, GROUP, split_axis=0, concat_axis=0, tiled=True)  11 us
    all_to_all x1, starting transfers between devices, body(): lax.all_to_all(squares, ('z', 'core'), split_axis=0, concat_axis=0, tiled...  11 us
    all_to_all x1, waiting for transfers between devices, body(): lax.all_to_all(squares, ('z', 'core'), split_axis=0, concat_axis=0, tiled...  9.21 us
    ppermute x1, waiting for transfers between devices, body(): squares_other = lax.ppermute(squares, 'xl', SWAP)  7.05 us
  transfers between devices with their start and end apart: 7, of which 5 were waited for; matrix products, arithmetic and copies ran while one was open for 1% of the time, Pallas kernels for 13%

profile of v7, /device:TPU:1, one launch (start us, length us, event | category | flops | bytes accessed | tf_op | source)
XLA Modules:
  0.0 181.0 jit_solution(64284700954479077)
XLA Ops:
  7.2 0.0 copy-start.2
  7.2 0.0 copy-start.1
  7.2 0.0 all-gather.2.cloned.1.call-start
  7.2 2.0 %prepare.1 = bf16[128,2048]{1,0:T(8,128)(2,1)} custom-call(bf16[2048,128]{1,0:T(8,128)(2,1)} %x_ref.2, bf16[1,128]{1,0:T(2,128)(2,1)} %bitcast.17), custom_call_target="tpu_custom_call" | custom-call | tf_op jit(solution)/shard_map/prepare/pallas_call | solution.py:57
  9.2 0.0 all-gather.2.cloned.1.call-update
  9.2 2.5 %pack_roots.1 = bf16[8,80,512]{2,1,0:T(8,128)(2,1)} custom-call(f32[512,512]{1,0:T(8,128)} %li_ref.1, f32[512,512]{1,0:T(8,128)} %ri_ref.1), custom_call_target="tpu_custom_call" | custom-call | tf_op jit(solution)/shard_map/pack_roots/pallas_call | solution.py:89
  11.7 7.5 %all-to-all-start = ((bf16[8,80,512]{2,1,0:T(8,128)(2,1)}), bf16[8,80,512]{2,1,0:T(8,128)(2,1)S(1)}, u32[]{:S(2)}, u32[]{:S(2)}) async-start(bf16[8,80,512]{2,1,0:T(8,128)(2,1)} %pack_roots.1), calls=%async_computation | async-start | bytes 1310720 | tf_op jit(solution)/shard_map/all_to_all | solution.py:333
  19.2 0.3 multiply_reduce_fusion
  19.6 0.4 collective-permute-start
  20.0 7.1 %collective-permute-done = f32[1,2048]{1,0:T(1,128)S(1)} collective-permute-done((f32[1,2048]{1,0:T(1,128)S(1)}, f32[1,2048]{1,0:T(1,128)S(1)}, u32[]{:S(2)}, u32[]{:S(2)}) %collective-permute-start) | collective-permute-done | bytes 8224 | tf_op jit(solution)/shard_map/ppermute | solution.py:332
  27.0 4.0 %all-to-all-done.x_ref = bf16[8,80,512]{2,1,0:T(8,128)(2,1)S(1)} async-done(((bf16[8,80,512]{2,1,0:T(8,128)(2,1)}), bf16[8,80,512]{2,1,0:T(8,128)(2,1)S(1)}, u32[]{:S(2)}, u32[]{:S(2)}) %all-to-all-start) | async-done | bytes 655392 | tf_op jit(solution)/shard_map/all_to_all | solution.py:333
  31.0 0.3 collective-permute-start.1
  31.4 0.7 broadcast_in_dim.2
  32.1 11.0 %all-to-all-start.1 = ((f32[16,1,2048]{2,1,0:T(1,128)}), f32[16,1,2048]{2,1,0:T(1,128)S(1)}, u32[]{:S(2)}, u32[]{:S(2)}) async-start(f32[16,1,2048]{2,1,0:T(1,128)} %broadcast_in_dim.2), calls=%async_computation.1 | async-start | bytes 262144 | tf_op jit(solution)/shard_map/all_to_all | solution.py:337
  43.1 1.4 pick.1
  44.5 9.2 %all-to-all-done.1 = f32[16,1,2048]{2,1,0:T(1,128)S(1)} async-done(((f32[16,1,2048]{2,1,0:T(1,128)}), f32[16,1,2048]{2,1,0:T(1,128)S(1)}, u32[]{:S(2)}, u32[]{:S(2)}) %all-to-all-start.1) | async-done | bytes 131104 | tf_op jit(solution)/shard_map/all_to_all | solution.py:337
  53.7 0.1 reduce_sum.19
  53.8 0.0 copy-start
  53.8 1.6 copy-done
  55.4 2.1 %scaled.1.cot_ref = bf16[2048,512]{1,0:T(8,128)(2,1)} custom-call(f32[1,2048]{1,0:T(1,128)S(1)} %bitcast.9, bf16[2048,512]{1,0:T(8,128)(2,1)S(1)} %copy-done), custom_call_target="tpu_custom_call" | custom-call | tf_op jit(solution)/shard_map/scaled/pallas_call | solution.py:147
  57.5 3.5 %all-to-all-start.2 = ((bf16[8,80,512]{2,1,0:T(8,128)(2,1)}), bf16[8,80,512]{2,1,0:T(8,128)(2,1)S(1)}, u32[]{:S(2)}, u32[]{:S(2)}) async-start(bf16[8,80,512]{2,1,0:T(8,128)(2,1)} %pick.1), calls=%async_computation.2 | async-start | bytes 1310720 | tf_op jit(solution)/shard_map/all_to_all | solution.py:341
  61.1 12.3 %all-gather.2.cloned.1.call-done.x_ref = bf16[2048,2048]{1,0:T(8,128)(2,1)} async-done(((bf16[128,2048]{1,0:T(8,128)(2,1)}), bf16[2048,2048]{1,0:T(8,128)(2,1)}) %all-gather.2.cloned.1.call-update) | async-done | bytes 8388624 | tf_op jit(solution)/shard_map/all_gather | solution.py:328
  73.4 9.6 %partials.2.filled_ref = bf16[8,2,4,64,512]{4,3,2,1,0:T(8,128)(2,1)} custom-call(s32[1]{0:T(128)} %bitcast.1.place_ref, bf16[2048,2048]{1,0:T(8,128)(2,1)} %all-gather.2.cloned.1.call-done.x_ref, bf16[2048,512]{1,0:T(8,128)(2,1)} %scaled.1.cot_ref), custom_call_target="tpu_custom_call" | custom-call | flops 4294967296 | bytes 12582912 | tf_op jit(solution)/shard_map/partials/pallas_call | solution.py:201
  83.0 0.0 collective-permute-done.1.cot_ref
  83.0 8.4 %partials.3 = bf16[8,2,4,64,512]{4,3,2,1,0:T(8,128)(2,1)} custom-call(s32[1]{0:T(128)S(6)} %sub.3.place_ref, bf16[2048,2048]{1,0:T(8,128)(2,1)} %all-gather.2.cloned.1.call-done.x_ref, bf16[2048,512]{1,0:T(8,128)(2,1)S(1)} %collective-permute-done.1.cot_ref, f32[1,2048]{1,0:T(1,128)S(1)} %bitcast.10, ...), custom_call_target="tpu_custom_call", output_to_operand_aliasing={{}: (4, {})} | custom-call | flops 4294967296 | bytes 12582912 | tf_op jit(solution)/shard_map/partials/pallas_call | solution.py:201
  91.4 0.0 all-to-all-done.2.x_ref
  91.4 56.7 %all_to_all.26 = bf16[16,4,64,512]{3,2,1,0:T(8,128)(2,1)S(1)} all-to-all(bf16[16,4,64,512]{3,2,1,0:T(8,128)(2,1)} %bitcast.13), channel_id=1, replica_groups=mesh['y'=4,'xh'=2,'xl'=2,'z'=8,'core'=2] {'y','xh','xl'}, dimensions={0} | all-to-all | bytes 8388608 | tf_op jit(solution)/shard_map/all_to_all | solution.py:348
  148.1 2.5 %route.1 = bf16[8,2,64,512]{3,2,1,0:T(8,128)(2,1)} custom-call(s32[8]{0:T(128)S(1)} %bitcast.12, bf16[8,2,4,64,512]{4,3,2,1,0:T(8,128)(2,1)S(1)} %bitcast.8), custom_call_target="tpu_custom_call" | custom-call | tf_op jit(solution)/shard_map/route/pallas_call | solution.py:235
  150.6 3.6 %all-to-all-start.4 = ((bf16[8,2,64,512]{3,2,1,0:T(8,128)(2,1)}), bf16[8,2,64,512]{3,2,1,0:T(8,128)(2,1)S(1)}, u32[]{:S(2)}, u32[]{:S(2)}) async-start(bf16[8,2,64,512]{3,2,1,0:T(8,128)(2,1)} %route.1), calls=%async_computation.4 | async-start | bytes 2097152 | tf_op jit(solution)/shard_map/all_to_all | solution.py:350
  154.8 0.3 unpack_roots.1
  155.1 14.3 %all-to-all-done.4.u_ref = bf16[8,2,64,512]{3,2,1,0:T(8,128)(2,1)S(1)} async-done(((bf16[8,2,64,512]{3,2,1,0:T(8,128)(2,1)}), bf16[8,2,64,512]{3,2,1,0:T(8,128)(2,1)S(1)}, u32[]{:S(2)}, u32[]{:S(2)}) %all-to-all-start.4) | async-done | bytes 1048608 | tf_op jit(solution)/shard_map/all_to_all | solution.py:350
  169.4 4.8 %block_step.1 = (bf16[512,512]{1,0:T(8,128)(2,1)}, f32[512,512]{1,0:T(8,128)}, f32[512,512]{1,0:T(8,128)}, f32[512,512]{1,0:T(8,128)}, f32[512,512]{1,0:T(8,128)}) custom-call(s32[1,1]{1,0:T(1,128)S(6)} %copy.18.refresh_ref, bf16[8,2,64,512]{3,2,1,0:T(8,128)(2,1)S(1)} %all-to-all-done.4.u_ref, bf16[512,512]{1,0:T(8,128)(2,1)S(1)} %get-tuple-element.27.lroot_ref, ...), custom_call_target="tpu_custom_call" | custom-call | flops 2147483648 | bytes 11534336 | tf_op jit(solution)/shard_map/block_step/pallas_call | solution.py:309
  (4 shorter events, 0.0 us)
Async XLA Ops:
  7.2 12.1 %copy-start.2 = (bf16[2048,128]{1,0:T(8,128)(2,1)S(1)}, bf16[2048,128]{1,0:T(8,128)(2,1)}, u32[]{:S(2)}) copy-start(bf16[2048,128]{1,0:T(8,128)(2,1)} %x_ref.2) | copy-start | bytes 1572868
  7.2 35.9 %copy-start.1 = (s32[1,8]{1,0:T(1,128)S(1)}, s32[1,8]{1,0:T(1,128)}, u32[]{:S(2)}) copy-start(s32[1,8]{1,0:T(1,128)} %param.12) | copy-start | bytes 100
  7.2 66.2 %all-gather.2.cloned.1.call-start = ((), (), s32[]{:S(2)}) async-start(), calls=%async_computation.5 | async-start | bytes 8912896 | tf_op jit(solution)/shard_map/all_gather | solution.py:328
  11.7 19.3 %all-to-all-start = ((bf16[8,80,512]{2,1,0:T(8,128)(2,1)}), bf16[8,80,512]{2,1,0:T(8,128)(2,1)S(1)}, u32[]{:S(2)}, u32[]{:S(2)}) async-start(bf16[8,80,512]{2,1,0:T(8,128)(2,1)} %pack_roots.1), calls=%async_computation | async-start | bytes 1310720 | tf_op jit(solution)/shard_map/all_to_all | solution.py:333
  19.6 7.5 %collective-permute-start = (f32[1,2048]{1,0:T(1,128)S(1)}, f32[1,2048]{1,0:T(1,128)S(1)}, u32[]{:S(2)}, u32[]{:S(2)}) collective-permute-start(f32[1,2048]{1,0:T(1,128)S(1)} %bitcast.14), channel_id=1, source_target_pairs={{0,16},{16,0},{1,17},{17,1},{2,18},{18,2},{3,19},{19,3},{4,20},{20... | collective-permute-start | bytes 24584 | tf_op jit(solution)/shard_map/ppermute | solution.py:332
  31.0 51.9 %collective-permute-start.1 = (bf16[2048,512]{1,0:T(8,128)(2,1)}, bf16[2048,512]{1,0:T(8,128)(2,1)S(1)}, u32[]{:S(2)}, u32[]{:S(2)}) collective-permute-start(bf16[2048,512]{1,0:T(8,128)(2,1)} %x_ref.3), channel_id=1, source_target_pairs={{0,16},{16,0},{1,17},{17,1},{2,18},{18,2},{3,19},{19,3},{4,20},{20... | collective-permute-start | bytes 6291464 | tf_op jit(solution)/shard_map/ppermute | solution.py:335
  32.1 21.6 %all-to-all-start.1 = ((f32[16,1,2048]{2,1,0:T(1,128)}), f32[16,1,2048]{2,1,0:T(1,128)S(1)}, u32[]{:S(2)}, u32[]{:S(2)}) async-start(f32[16,1,2048]{2,1,0:T(1,128)} %broadcast_in_dim.2), calls=%async_computation.1 | async-start | bytes 262144 | tf_op jit(solution)/shard_map/all_to_all | solution.py:337
  53.8 1.6 copy-start
  57.5 33.9 %all-to-all-start.2 = ((bf16[8,80,512]{2,1,0:T(8,128)(2,1)}), bf16[8,80,512]{2,1,0:T(8,128)(2,1)S(1)}, u32[]{:S(2)}, u32[]{:S(2)}) async-start(bf16[8,80,512]{2,1,0:T(8,128)(2,1)} %pick.1), calls=%async_computation.2 | async-start | bytes 1310720 | tf_op jit(solution)/shard_map/all_to_all | solution.py:341
  150.6 18.8 %all-to-all-start.4 = ((bf16[8,2,64,512]{3,2,1,0:T(8,128)(2,1)}), bf16[8,2,64,512]{3,2,1,0:T(8,128)(2,1)S(1)}, u32[]{:S(2)}, u32[]{:S(2)}) async-start(bf16[8,2,64,512]{3,2,1,0:T(8,128)(2,1)} %route.1), calls=%async_computation.4 | async-start | bytes 2097152 | tf_op jit(solution)/shard_map/all_to_all | solution.py:350
Sparse Core Ops, SparseCore 0:
  10.4 62.9 all-gather.1

commit v8 on v7

--- a/solution.py
+++ b/solution.py
@@ -12,6 +12,7 @@
 RIDGE_TERM = 1e-06
 BLK = 512
 N_GROUP = 8
+LOAD = 512
 CHUNK = BLK // N_GROUP
 PACKED = CHUNK + 16
 GROUP = ("y", "xh")
@@ -154,92 +155,86 @@
     )(scale, x)
 
 
-def put_rows(o_ref, part):
-    part = part.astype(BF16)
-    for j in range(N_GROUP):
-        o_ref[j, 0, 0] = part[j * CHUNK : (j + 1) * CHUNK]
-
-
-def own_kernel(place_ref, x_ref, cot_ref, o_ref, local_ref, sems):
-    @pl.when(pl.program_id(0) == 0)
-    def _():
-        spans = [pl.ds(first, BLK) for first in range(0, cot_ref.shape[0], BLK)]
-        copies = [pltpu.make_async_copy(cot_ref.at[s], local_ref.at[s], sems.at[n]) for n, s in enumerate(spans)]
-        for copy in copies:
+def partials_kernel(place_ref, x_ref, cot_ref, *refs):
+    *rest, o_ref, local, scaled_ref, part_ref, sems = refs
+    rows, tokens = local.shape
+    slabs, pieces = rows // BLK, rows // LOAD
+    loads = [
+        pltpu.make_async_copy(x_ref.at[pl.ds(n * LOAD, LOAD)], local.at[pl.ds(n * LOAD, LOAD)], sems.at[n])
+        for n in range(pieces)
+    ]
+    spans = [pl.ds(first, BLK) for first in range(0, tokens, BLK)]
+    cots = [
+        pltpu.make_async_copy(cot_ref.at[span], scaled_ref.at[span], sems.at[pieces + n])
+        for n, span in enumerate(spans)
+    ]
+    stores = [
+        pltpu.make_async_copy(part_ref.at[i], o_ref.at[:, place_ref[0], i], sems.at[pieces + len(spans) + i])
+        for i in range(slabs)
+    ]
+    for load in loads[: BLK // LOAD]:
+        load.start()
+    if not rest:
+        for copy in cots:
             copy.start()
-        part = jnp.zeros((BLK, BLK), F32)
-        for copy, span in zip(copies, spans):
+    for load in loads[BLK // LOAD :]:
+        load.start()
+    if rest:
+        column = column_of(rest[0])
+        for span in spans:
+            scaled_ref[span] = (cot_ref[span].astype(F32) * column[span.start : span.start + BLK]).astype(BF16)
+    else:
+        for copy in cots:
             copy.wait()
-            part = part + dot(x_ref[:, span], local_ref[span])
-        put_rows(o_ref, part)
-
-    @pl.when(pl.program_id(0) > 0)
-    def _():
-        put_rows(o_ref, dot(x_ref[...], local_ref[...]))
-
-
-def other_kernel(place_ref, x_ref, cot_ref, scale_ref, filled_ref, o_ref, scaled_ref):
-    @pl.when(pl.program_id(0) == 0)
-    def _():
-        column = column_of(scale_ref)
-        part = jnp.zeros((BLK, BLK), F32)
-        for first in range(0, cot_ref.shape[0], BLK):
-            span = slice(first, first + BLK)
-            piece = (cot_ref[span].astype(F32) * column[span]).astype(BF16)
-            scaled_ref[span] = piece
-            part = part + dot(x_ref[:, span], piece)
-        put_rows(o_ref, part)
-
-    @pl.when(pl.program_id(0) > 0)
-    def _():
-        put_rows(o_ref, dot(x_ref[...], scaled_ref[...]))
+    for i in range(slabs):
+        for load in loads[i * (BLK // LOAD) : (i + 1) * (BLK // LOAD)]:
+            load.wait()
+        part = dot(local[i * BLK : (i + 1) * BLK], scaled_ref[...]).astype(BF16)
+        for j in range(N_GROUP):
+            part_ref[i, j] = part[j * CHUNK : (j + 1) * CHUNK]
+        stores[i].start()
+    for store in stores:
+        store.wait()
 
 
 def partials(place, x, cot, *rest):
     rows, tokens = x.shape
     slabs = rows // BLK
     return pl.pallas_call(
-        other_kernel if rest else own_kernel,
-        grid_spec=pltpu.PrefetchScalarGridSpec(
-            num_scalar_prefetch=1,
-            grid=(slabs,),
-            in_specs=[pl.BlockSpec((BLK, tokens), lambda i, place: (i, 0))] + ([VMEM, VMEM, HBM] if rest else [HBM]),
-            out_specs=pl.BlockSpec((N_GROUP, 1, 1, CHUNK, BLK), lambda i, place: (0, place[0], i, 0, 0)),
-            scratch_shapes=[pltpu.VMEM((tokens, BLK), BF16)]
-            + ([] if rest else [pltpu.SemaphoreType.DMA((tokens // BLK,))]),
-        ),
+        partials_kernel,
+        in_specs=[SMEM, HBM] + ([VMEM, VMEM, HBM] if rest else [HBM]),
+        out_specs=HBM,
+        scratch_shapes=[
+            pltpu.VMEM((rows, tokens), BF16),
+            pltpu.VMEM((tokens, BLK), BF16),
+            pltpu.VMEM((slabs, N_GROUP, CHUNK, BLK), BF16),
+            pltpu.SemaphoreType.DMA((rows // LOAD + tokens // BLK + slabs,)),
+        ],
         out_shape=pltpu.HBM((N_GROUP, 2, slabs, CHUNK, BLK), BF16),
         input_output_aliases={4: 0} if rest else {},
         compiler_params=params(),
         cost_estimate=pl.CostEstimate(flops=2 * rows * tokens * BLK, bytes_accessed=12 * 2**20, transcendentals=0),
         name="partials",
-    )(place, x, cot if rest else in_hbm(cot), *rest)
-
-
-def total(x_ref, slab):
-    acc = x_ref[0, 0, slab].astype(F32)
-    for g in range(1, N_GROUP):
-        acc = acc + x_ref[g, 0, slab].astype(F32)
-    return acc.astype(BF16)
+    )(place, in_hbm(x), cot if rest else in_hbm(cot), *rest)
 
 
 def route_kernel(owner_ref, x_ref, o_ref):
-    base = 2 * pl.program_id(0)
-    for n in range(2):
-        value = total(x_ref, n)
-        o_ref[base + n, 1] = value
-        o_ref[owner_ref[base + n], 0] = value
+    for half in range(2):
+        for n in range(x_ref.shape[2]):
+            value = x_ref[0, half, n].astype(F32)
+            for g in range(1, N_GROUP):
+                value = value + x_ref[g, half, n].astype(F32)
+            value = value.astype(BF16)
+            slab = half * x_ref.shape[2] + n
+            o_ref[slab, 1] = value
+            o_ref[owner_ref[slab], 0] = value
 
 
 def route(owner, x):
     return pl.pallas_call(
         route_kernel,
-        grid_spec=pltpu.PrefetchScalarGridSpec(
-            num_scalar_prefetch=1,
-            grid=(4,),
-            in_specs=[pl.BlockSpec((N_GROUP, 1, 2, CHUNK, BLK), lambda i, owner: (0, i // 2, i % 2, 0, 0))],
-            out_specs=pl.BlockSpec((N_GROUP, 2, CHUNK, BLK), lambda i, owner: (0, 0, 0, 0)),
-        ),
+        in_specs=[SMEM, VMEM],
+        out_specs=VMEM,
         out_shape=pltpu.HBM((N_GROUP, 2, CHUNK, BLK), BF16),
         compiler_params=params(),
         name="route",
@@ -251,12 +246,13 @@
     eye = (rows == cols).astype(F32)
     matrix = statistic + RIDGE_TERM * eye
     scaling = 2.5 * lax.rsqrt(jnp.sum(matrix * matrix, keepdims=True))
-    scaled = scaling * matrix
-    factor = (1.25 * eye - 0.25 * scaled).astype(BF16)
-    square = dot(factor, factor).astype(BF16)
+    matrix = scaling * matrix
+    rounded = matrix.astype(BF16)
+    product = dot(rounded, rounded)
+    square = (1.5625 * eye - 0.625 * matrix + 0.0625 * product).astype(BF16)
+    once = (1.25 * matrix - 0.25 * product).astype(BF16)
     fourth = dot(square, square).astype(BF16)
-    second = 1.25 * eye - 0.25 * dot(fourth, scaled.astype(BF16))
-    return jnp.sqrt(jnp.sqrt(scaling)) * dot(factor, second.astype(BF16))
+    return jnp.sqrt(jnp.sqrt(scaling)) * (1.5625 * eye - 0.3125 * matrix - 0.25 * dot(fourth, once))
 
 
 def block_kernel(

time: 184 us -> 181 us (0.984)
  Pallas kernels: 33.5 us -> 30.6 us
    pallas_call x3, Pallas kernels: 20.5 us -> 17.6 us  [the longest x2 15.5 us: partials(): pl.pallas_call(partials_kernel, in_specs=[SMEM, HBM] + ([VMEM, VMEM, HBM]...]
  transfers between devices with their start and end apart: 7 -> 7, of which waited for: 5 -> 5; matrix products, arithmetic and copies ran while one was open for 1% -> 1% of each run, Pallas kernels for 13% -> 12%
where the time goes in v8:
time: 181 us; the launch traced here: 178 us
  blocking collectives  56.7 us (31%)
  waiting for transfers between devices  46.9 us (26%)
  Pallas kernels  30.6 us (17%)
  starting transfers between devices  26.3 us (15%)
  between operations  14.8 us (8%)
  local copies, waits for them, and re-layouts  2.33 us (1%)
    all_to_all x1, blocking collectives, body(): lax.all_to_all(pieces, ('y', 'xh', 'xl'), split_axis=0, concat_axis=0, ti...  56.7 us
    pallas_call x2, Pallas kernels, partials(): pl.pallas_call(partials_kernel, in_specs=[SMEM, HBM] + ([VMEM, VMEM, HBM]...  15.5 us
    all_to_all x1, waiting for transfers between devices, body(): lax.all_to_all(grads, GROUP, split_axis=0, concat_axis=0, tiled=True)  14.3 us
    all_gather x1, waiting for transfers between devices, body(): lax.all_gather(prepare(inputs, norm_gain), ('z', 'core'), axis=0, tiled=T...  12.3 us
    all_to_all x2, starting transfers between devices, body(): lax.all_to_all(roots, GROUP, split_axis=0, concat_axis=0, tiled=True)  11 us
    all_to_all x1, starting transfers between devices, body(): lax.all_to_all(squares, ('z', 'core'), split_axis=0, concat_axis=0, tiled...  11 us
    all_to_all x1, waiting for transfers between devices, body(): lax.all_to_all(squares, ('z', 'core'), split_axis=0, concat_axis=0, tiled...  9.21 us
    ppermute x1, waiting for transfers between devices, body(): squares_other = lax.ppermute(squares, 'xl', SWAP)  7.05 us
  transfers between devices with their start and end apart: 7, of which 5 were waited for; matrix products, arithmetic and copies ran while one was open for 1% of the time, Pallas kernels for 12%

profile of v8, /device:TPU:1, one launch (start us, length us, event | category | flops | bytes accessed | tf_op | source)
XLA Modules:
  0.0 178.1 jit_solution(6691737116567197168)
XLA Ops:
  7.2 0.0 copy-start.2
  7.2 0.0 copy-start.1
  7.2 0.0 all-gather.2.cloned.1.call-start
  7.2 2.0 %prepare.1 = bf16[128,2048]{1,0:T(8,128)(2,1)} custom-call(bf16[2048,128]{1,0:T(8,128)(2,1)} %x_ref.2, bf16[1,128]{1,0:T(2,128)(2,1)} %bitcast.17), custom_call_target="tpu_custom_call" | custom-call | tf_op jit(solution)/shard_map/prepare/pallas_call | solution.py:58
  9.2 0.0 all-gather.2.cloned.1.call-update
  9.2 2.5 %pack_roots.1 = bf16[8,80,512]{2,1,0:T(8,128)(2,1)} custom-call(f32[512,512]{1,0:T(8,128)} %li_ref.1, f32[512,512]{1,0:T(8,128)} %ri_ref.1), custom_call_target="tpu_custom_call" | custom-call | tf_op jit(solution)/shard_map/pack_roots/pallas_call | solution.py:90
  11.7 7.5 %all-to-all-start = ((bf16[8,80,512]{2,1,0:T(8,128)(2,1)}), bf16[8,80,512]{2,1,0:T(8,128)(2,1)S(1)}, u32[]{:S(2)}, u32[]{:S(2)}) async-start(bf16[8,80,512]{2,1,0:T(8,128)(2,1)} %pack_roots.1), calls=%async_computation | async-start | bytes 1310720 | tf_op jit(solution)/shard_map/all_to_all | solution.py:329
  19.2 0.3 multiply_reduce_fusion
  19.6 0.4 collective-permute-start
  20.0 7.1 %collective-permute-done = f32[1,2048]{1,0:T(1,128)S(1)} collective-permute-done((f32[1,2048]{1,0:T(1,128)S(1)}, f32[1,2048]{1,0:T(1,128)S(1)}, u32[]{:S(2)}, u32[]{:S(2)}) %collective-permute-start) | collective-permute-done | bytes 8224 | tf_op jit(solution)/shard_map/ppermute | solution.py:328
  27.0 4.0 %all-to-all-done.x_ref = bf16[8,80,512]{2,1,0:T(8,128)(2,1)S(1)} async-done(((bf16[8,80,512]{2,1,0:T(8,128)(2,1)}), bf16[8,80,512]{2,1,0:T(8,128)(2,1)S(1)}, u32[]{:S(2)}, u32[]{:S(2)}) %all-to-all-start) | async-done | bytes 655392 | tf_op jit(solution)/shard_map/all_to_all | solution.py:329
  31.0 0.3 collective-permute-start.1
  31.4 0.7 broadcast_in_dim.2
  32.1 11.0 %all-to-all-start.1 = ((f32[16,1,2048]{2,1,0:T(1,128)}), f32[16,1,2048]{2,1,0:T(1,128)S(1)}, u32[]{:S(2)}, u32[]{:S(2)}) async-start(f32[16,1,2048]{2,1,0:T(1,128)} %broadcast_in_dim.2), calls=%async_computation.1 | async-start | bytes 262144 | tf_op jit(solution)/shard_map/all_to_all | solution.py:333
  43.1 1.4 pick.1
  44.5 9.2 %all-to-all-done.1 = f32[16,1,2048]{2,1,0:T(1,128)S(1)} async-done(((f32[16,1,2048]{2,1,0:T(1,128)}), f32[16,1,2048]{2,1,0:T(1,128)S(1)}, u32[]{:S(2)}, u32[]{:S(2)}) %all-to-all-start.1) | async-done | bytes 131104 | tf_op jit(solution)/shard_map/all_to_all | solution.py:333
  53.7 0.1 reduce_sum.19
  53.8 0.0 copy-start
  53.8 1.6 copy-done
  55.4 2.1 %scaled.1.cot_ref = bf16[2048,512]{1,0:T(8,128)(2,1)} custom-call(f32[1,2048]{1,0:T(1,128)S(1)} %bitcast.9, bf16[2048,512]{1,0:T(8,128)(2,1)S(1)} %copy-done), custom_call_target="tpu_custom_call" | custom-call | tf_op jit(solution)/shard_map/scaled/pallas_call | solution.py:148
  57.5 3.5 %all-to-all-start.2 = ((bf16[8,80,512]{2,1,0:T(8,128)(2,1)}), bf16[8,80,512]{2,1,0:T(8,128)(2,1)S(1)}, u32[]{:S(2)}, u32[]{:S(2)}) async-start(bf16[8,80,512]{2,1,0:T(8,128)(2,1)} %pick.1), calls=%async_computation.2 | async-start | bytes 1310720 | tf_op jit(solution)/shard_map/all_to_all | solution.py:337
  61.1 12.3 %all-gather.2.cloned.1.call-done.x_ref = bf16[2048,2048]{1,0:T(8,128)(2,1)} async-done(((bf16[128,2048]{1,0:T(8,128)(2,1)}), bf16[2048,2048]{1,0:T(8,128)(2,1)}) %all-gather.2.cloned.1.call-update) | async-done | bytes 8388624 | tf_op jit(solution)/shard_map/all_gather | solution.py:324
  73.4 8.0 %partials.2.refs_1_ = bf16[8,2,4,64,512]{4,3,2,1,0:T(8,128)(2,1)} custom-call(s32[1]{0:T(128)} %bitcast.1.place_ref, bf16[2048,2048]{1,0:T(8,128)(2,1)} %all-gather.2.cloned.1.call-done.x_ref, bf16[2048,512]{1,0:T(8,128)(2,1)} %scaled.1.cot_ref), custom_call_target="tpu_custom_call" | custom-call | flops 4294967296 | bytes 12582912 | tf_op jit(solution)/shard_map/partials/pallas_call | solution.py:203
  81.4 0.0 collective-permute-done.1.cot_ref
  81.5 7.5 %partials.3 = bf16[8,2,4,64,512]{4,3,2,1,0:T(8,128)(2,1)} custom-call(s32[1]{0:T(128)S(6)} %sub.3.place_ref, bf16[2048,2048]{1,0:T(8,128)(2,1)} %all-gather.2.cloned.1.call-done.x_ref, bf16[2048,512]{1,0:T(8,128)(2,1)S(1)} %collective-permute-done.1.cot_ref, f32[1,2048]{1,0:T(1,128)S(1)} %bitcast.10, ...), custom_call_target="tpu_custom_call", output_to_operand_aliasing={{}: (4, {})} | custom-call | flops 4294967296 | bytes 12582912 | tf_op jit(solution)/shard_map/partials/pallas_call | solution.py:203
  89.0 0.0 all-to-all-done.2.x_ref
  89.0 56.7 %all_to_all.26 = bf16[16,4,64,512]{3,2,1,0:T(8,128)(2,1)S(1)} all-to-all(bf16[16,4,64,512]{3,2,1,0:T(8,128)(2,1)} %bitcast.13), channel_id=1, replica_groups=mesh['y'=4,'xh'=2,'xl'=2,'z'=8,'core'=2] {'y','xh','xl'}, dimensions={0} | all-to-all | bytes 8388608 | tf_op jit(solution)/shard_map/all_to_all | solution.py:344
  145.7 2.0 %route.1 = bf16[8,2,64,512]{3,2,1,0:T(8,128)(2,1)} custom-call(s32[8]{0:T(128)S(1)} %bitcast.12, bf16[8,2,4,64,512]{4,3,2,1,0:T(8,128)(2,1)S(1)} %bitcast.8), custom_call_target="tpu_custom_call" | custom-call | tf_op jit(solution)/shard_map/route/pallas_call | solution.py:234
  147.7 3.6 %all-to-all-start.4 = ((bf16[8,2,64,512]{3,2,1,0:T(8,128)(2,1)}), bf16[8,2,64,512]{3,2,1,0:T(8,128)(2,1)S(1)}, u32[]{:S(2)}, u32[]{:S(2)}) async-start(bf16[8,2,64,512]{3,2,1,0:T(8,128)(2,1)} %route.1), calls=%async_computation.4 | async-start | bytes 2097152 | tf_op jit(solution)/shard_map/all_to_all | solution.py:346
  151.9 0.3 unpack_roots.1
  152.2 14.3 %all-to-all-done.4.u_ref = bf16[8,2,64,512]{3,2,1,0:T(8,128)(2,1)S(1)} async-done(((bf16[8,2,64,512]{3,2,1,0:T(8,128)(2,1)}), bf16[8,2,64,512]{3,2,1,0:T(8,128)(2,1)S(1)}, u32[]{:S(2)}, u32[]{:S(2)}) %all-to-all-start.4) | async-done | bytes 1048608 | tf_op jit(solution)/shard_map/all_to_all | solution.py:346
  166.5 4.8 %block_step.1 = (bf16[512,512]{1,0:T(8,128)(2,1)}, f32[512,512]{1,0:T(8,128)}, f32[512,512]{1,0:T(8,128)}, f32[512,512]{1,0:T(8,128)}, f32[512,512]{1,0:T(8,128)}) custom-call(s32[1,1]{1,0:T(1,128)S(6)} %copy.18.refresh_ref, bf16[8,2,64,512]{3,2,1,0:T(8,128)(2,1)S(1)} %all-to-all-done.4.u_ref, bf16[512,512]{1,0:T(8,128)(2,1)S(1)} %get-tuple-element.27.lroot_ref, ...), custom_call_target="tpu_custom_call" | custom-call | flops 2147483648 | bytes 11534336 | tf_op jit(solution)/shard_map/block_step/pallas_call | solution.py:305
  (4 shorter events, 0.0 us)
Async XLA Ops:
  7.2 12.1 %copy-start.2 = (bf16[2048,128]{1,0:T(8,128)(2,1)S(1)}, bf16[2048,128]{1,0:T(8,128)(2,1)}, u32[]{:S(2)}) copy-start(bf16[2048,128]{1,0:T(8,128)(2,1)} %x_ref.2) | copy-start | bytes 1572868
  7.2 35.9 %copy-start.1 = (s32[1,8]{1,0:T(1,128)S(1)}, s32[1,8]{1,0:T(1,128)}, u32[]{:S(2)}) copy-start(s32[1,8]{1,0:T(1,128)} %param.12) | copy-start | bytes 100
  7.2 66.2 %all-gather.2.cloned.1.call-start = ((), (), s32[]{:S(2)}) async-start(), calls=%async_computation.5 | async-start | bytes 8912896 | tf_op jit(solution)/shard_map/all_gather | solution.py:324
  11.7 19.3 %all-to-all-start = ((bf16[8,80,512]{2,1,0:T(8,128)(2,1)}), bf16[8,80,512]{2,1,0:T(8,128)(2,1)S(1)}, u32[]{:S(2)}, u32[]{:S(2)}) async-start(bf16[8,80,512]{2,1,0:T(8,128)(2,1)} %pack_roots.1), calls=%async_computation | async-start | bytes 1310720 | tf_op jit(solution)/shard_map/all_to_all | solution.py:329
  19.6 7.5 %collective-permute-start = (f32[1,2048]{1,0:T(1,128)S(1)}, f32[1,2048]{1,0:T(1,128)S(1)}, u32[]{:S(2)}, u32[]{:S(2)}) collective-permute-start(f32[1,2048]{1,0:T(1,128)S(1)} %bitcast.14), channel_id=1, source_target_pairs={{0,16},{16,0},{1,17},{17,1},{2,18},{18,2},{3,19},{19,3},{4,20},{20... | collective-permute-start | bytes 24584 | tf_op jit(solution)/shard_map/ppermute | solution.py:328
  31.0 50.4 %collective-permute-start.1 = (bf16[2048,512]{1,0:T(8,128)(2,1)}, bf16[2048,512]{1,0:T(8,128)(2,1)S(1)}, u32[]{:S(2)}, u32[]{:S(2)}) collective-permute-start(bf16[2048,512]{1,0:T(8,128)(2,1)} %x_ref.3), channel_id=1, source_target_pairs={{0,16},{16,0},{1,17},{17,1},{2,18},{18,2},{3,19},{19,3},{4,20},{20... | collective-permute-start | bytes 6291464 | tf_op jit(solution)/shard_map/ppermute | solution.py:331
  32.1 21.6 %all-to-all-start.1 = ((f32[16,1,2048]{2,1,0:T(1,128)}), f32[16,1,2048]{2,1,0:T(1,128)S(1)}, u32[]{:S(2)}, u32[]{:S(2)}) async-start(f32[16,1,2048]{2,1,0:T(1,128)} %broadcast_in_dim.2), calls=%async_computation.1 | async-start | bytes 262144 | tf_op jit(solution)/shard_map/all_to_all | solution.py:333
  53.8 1.6 copy-start
  57.5 31.4 %all-to-all-start.2 = ((bf16[8,80,512]{2,1,0:T(8,128)(2,1)}), bf16[8,80,512]{2,1,0:T(8,128)(2,1)S(1)}, u32[]{:S(2)}, u32[]{:S(2)}) async-start(bf16[8,80,512]{2,1,0:T(8,128)(2,1)} %pick.1), calls=%async_computation.2 | async-start | bytes 1310720 | tf_op jit(solution)/shard_map/all_to_all | solution.py:337
  147.7 18.8 %all-to-all-start.4 = ((bf16[8,2,64,512]{3,2,1,0:T(8,128)(2,1)}), bf16[8,2,64,512]{3,2,1,0:T(8,128)(2,1)S(1)}, u32[]{:S(2)}, u32[]{:S(2)}) async-start(bf16[8,2,64,512]{3,2,1,0:T(8,128)(2,1)} %route.1), calls=%async_computation.4 | async-start | bytes 2097152 | tf_op jit(solution)/shard_map/all_to_all | solution.py:346
Sparse Core Ops, SparseCore 0:
  10.4 62.9 all-gather.1

commit v9 on v8

--- a/solution.py
+++ b/solution.py
@@ -16,6 +16,7 @@
 CHUNK = BLK // N_GROUP
 PACKED = CHUNK + 16
 GROUP = ("y", "xh")
+TURNED = ("xh", "y")
 FSDP = ("xl", "z", "core")
 SWAP = [(0, 1), (1, 0)]
 BF16 = jnp.bfloat16
@@ -25,6 +26,10 @@
 HBM = pl.BlockSpec(memory_space=pltpu.HBM)
 VMEM = pl.BlockSpec(memory_space=pltpu.VMEM)
 SMEM = pl.BlockSpec(memory_space=pltpu.SMEM)
+
+
+def turned(group):
+    return (group & 1) * (N_GROUP // 2) + (group >> 1)
 
 
 def in_hbm(x):
@@ -100,7 +105,7 @@
 
 def pick_kernel(owner_ref, x_ref, o_ref):
     for i in range(N_GROUP):
-        o_ref[i] = x_ref[owner_ref[i]]
+        o_ref[turned(i)] = x_ref[turned(owner_ref[i])]
 
 
 def pick(owner, x):
@@ -169,7 +174,7 @@
         for n, span in enumerate(spans)
     ]
     stores = [
-        pltpu.make_async_copy(part_ref.at[i], o_ref.at[:, place_ref[0], i], sems.at[pieces + len(spans) + i])
+        pltpu.make_async_copy(part_ref.at[i], o_ref.at[place_ref[0], :, i], sems.at[pieces + len(spans) + i])
         for i in range(slabs)
     ]
     for load in loads[: BLK // LOAD]:
@@ -210,7 +215,7 @@
             pltpu.VMEM((slabs, N_GROUP, CHUNK, BLK), BF16),
             pltpu.SemaphoreType.DMA((rows // LOAD + tokens // BLK + slabs,)),
         ],
-        out_shape=pltpu.HBM((N_GROUP, 2, slabs, CHUNK, BLK), BF16),
+        out_shape=pltpu.HBM((2, N_GROUP, slabs, CHUNK, BLK), BF16),
         input_output_aliases={4: 0} if rest else {},
         compiler_params=params(),
         cost_estimate=pl.CostEstimate(flops=2 * rows * tokens * BLK, bytes_accessed=12 * 2**20, transcendentals=0),
@@ -221,13 +226,13 @@
 def route_kernel(owner_ref, x_ref, o_ref):
     for half in range(2):
         for n in range(x_ref.shape[2]):
-            value = x_ref[0, half, n].astype(F32)
+            value = x_ref[half, 0, n].astype(F32)
             for g in range(1, N_GROUP):
-                value = value + x_ref[g, half, n].astype(F32)
+                value = value + x_ref[half, g, n].astype(F32)
             value = value.astype(BF16)
             slab = half * x_ref.shape[2] + n
-            o_ref[slab, 1] = value
-            o_ref[owner_ref[slab], 0] = value
+            o_ref[turned(slab), 1] = value
+            o_ref[turned(owner_ref[slab]), 0] = value
 
 
 def route(owner, x):
@@ -272,7 +277,7 @@
         for keep in keeps:
             keep.start()
 
-    grad = u_ref[:, 0].reshape(BLK, BLK)
+    grad, natural = (jnp.concatenate([u_ref[turned(g), n] for g in range(N_GROUP)], axis=0) for n in range(2))
     for n, (accum, dims) in enumerate(((left, NT), (right, TN))):
         gram = dot_dims(grad, grad, dims)
         loads[n].wait()
@@ -292,7 +297,7 @@
             copy.start()
 
     right_root = rroot_ref[...]
-    high, low = split2(dot(lroot_ref[...], u_ref[:, 1].reshape(BLK, BLK)))
+    high, low = split2(dot(lroot_ref[...], natural))
     conditioned = dot(high, right_root) + dot(low, right_root)
     mean = jnp.sum(conditioned * conditioned, keepdims=True) * (1.0 / (BLK * BLK))
     upd_ref[...] = (conditioned * lax.rsqrt(mean + SCALE_EPSILON)).astype(BF16)
@@ -326,7 +331,7 @@
     squares = jnp.sum(values * values, axis=1).reshape(1, tokens)
     roots = pack_roots(left_inverse, right_inverse)
     squares_other = lax.ppermute(squares, "xl", SWAP)
-    roots = lax.all_to_all(roots, GROUP, split_axis=0, concat_axis=0, tiled=True)
+    roots = lax.all_to_all(roots, TURNED, split_axis=0, concat_axis=0, tiled=True)
     roots, other, squares, squares_other = lax.optimization_barrier((roots, cotangent, squares, squares_other))
     other = lax.ppermute(other, "xl", SWAP)
     squares = jnp.broadcast_to(squares + squares_other, (peers, tokens))
@@ -334,16 +339,16 @@
     scale = lax.rsqrt(jnp.sum(squares, axis=0, keepdims=True) / count + NORM_EPSILON)
     roots = pick(owner, roots)
     roots, scale = lax.optimization_barrier((roots, scale))
-    roots = lax.all_to_all(roots, GROUP, split_axis=0, concat_axis=0, tiled=True)
+    roots = lax.all_to_all(roots, TURNED, split_axis=0, concat_axis=0, tiled=True)
 
     pieces = partials(xl, features, scaled(scale, cotangent))
     pieces, other = lax.optimization_barrier((pieces, other))
     pieces = partials(1 - xl, features, other, scale, pieces)
     shape = pieces.shape
     pieces, roots = lax.optimization_barrier((pieces.reshape(2 * N_GROUP, *shape[2:]), roots))
-    pieces = lax.all_to_all(pieces, ("y", "xh", "xl"), split_axis=0, concat_axis=0, tiled=True)
+    pieces = lax.all_to_all(pieces, ("xl", "y", "xh"), split_axis=0, concat_axis=0, tiled=True)
     grads = route(owner, pieces.reshape(shape))
-    grads = lax.all_to_all(grads, GROUP, split_axis=0, concat_axis=0, tiled=True)
+    grads = lax.all_to_all(grads, TURNED, split_axis=0, concat_axis=0, tiled=True)
     left_root, right_root = unpack_roots(roots)
     state = (left_stats, right_stats, left_inverse, right_inverse)
     return tuple(block_step(refresh, grads, left_root, right_root, *state))

time: 181 us -> 180 us (level)
  the two profiles are of different devices: /device:TPU:1 before, /device:TPU:8 now
where the time goes in v9:
time: 180 us; the launch traced here: 179 us
  blocking collectives  56.6 us (31%)
  waiting for transfers between devices  43.7 us (24%)
  Pallas kernels  33.2 us (18%)
  starting transfers between devices  28.2 us (16%)
  between operations  14.8 us (8%)
  local copies, waits for them, and re-layouts  2.35 us (1%)
    all_to_all x1, blocking collectives, body(): lax.all_to_all(pieces, ('xl', 'y', 'xh'), split_axis=0, concat_axis=0, ti...  56.6 us
    pallas_call x2, Pallas kernels, partials(): pl.pallas_call(partials_kernel, in_specs=[SMEM, HBM] + ([VMEM, VMEM, HBM]...  15.5 us
    all_to_all x2, starting transfers between devices, body(): lax.all_to_all(roots, TURNED, split_axis=0, concat_axis=0, tiled=True)  13.3 us
    all_to_all x1, waiting for transfers between devices, body(): lax.all_to_all(grads, TURNED, split_axis=0, concat_axis=0, tiled=True)  12.8 us
    all_gather x1, waiting for transfers between devices, body(): lax.all_gather(prepare(inputs, norm_gain), ('z', 'core'), axis=0, tiled=T...  12.4 us
    all_to_all x1, waiting for transfers between devices, body(): lax.all_to_all(squares, ('z', 'core'), split_axis=0, concat_axis=0, tiled...  9.03 us
    all_to_all x1, starting transfers between devices, body(): lax.all_to_all(squares, ('z', 'core'), split_axis=0, concat_axis=0, tiled...  8.57 us
    pallas_call x1, Pallas kernels, block_step(): pl.pallas_call(block_kernel, in_specs=[SMEM, VMEM, VMEM, VMEM] + [HBM] *...  7.38 us
  transfers between devices with their start and end apart: 7, of which 5 were waited for; matrix products, arithmetic and copies ran while one was open for 1% of the time, Pallas kernels for 12%

profile of v9, /device:TPU:8, one launch (start us, length us, event | category | flops | bytes accessed | tf_op | source)
XLA Modules:
  0.0 179.3 jit_solution(499128666490444884)
XLA Ops:
  7.2 0.0 copy-start.2
  7.2 0.0 all-gather.2.cloned.1.call-start
  7.2 2.0 %prepare.1 = bf16[128,2048]{1,0:T(8,128)(2,1)} custom-call(bf16[2048,128]{1,0:T(8,128)(2,1)} %x_ref.2, bf16[1,128]{1,0:T(2,128)(2,1)} %bitcast.17), custom_call_target="tpu_custom_call" | custom-call | tf_op jit(solution)/shard_map/prepare/pallas_call | solution.py:63
  9.2 0.0 all-gather.2.cloned.1.call-update
  9.2 2.5 %pack_roots.1 = bf16[8,80,512]{2,1,0:T(8,128)(2,1)} custom-call(f32[512,512]{1,0:T(8,128)} %li_ref.1, f32[512,512]{1,0:T(8,128)} %ri_ref.1), custom_call_target="tpu_custom_call" | custom-call | tf_op jit(solution)/shard_map/pack_roots/pallas_call | solution.py:95
  11.7 7.4 %all-to-all-start = ((bf16[8,80,512]{2,1,0:T(8,128)(2,1)}), bf16[8,80,512]{2,1,0:T(8,128)(2,1)S(1)}, u32[]{:S(2)}, u32[]{:S(2)}) async-start(bf16[8,80,512]{2,1,0:T(8,128)(2,1)} %pack_roots.1), calls=%async_computation | async-start | bytes 1310720 | tf_op jit(solution)/shard_map/all_to_all | solution.py:334
  19.1 0.0 copy-done.2
  19.1 0.3 multiply_reduce_fusion
  19.5 0.7 collective-permute-start
  20.2 7.1 %collective-permute-done = f32[1,2048]{1,0:T(1,128)S(1)} collective-permute-done((f32[1,2048]{1,0:T(1,128)S(1)}, f32[1,2048]{1,0:T(1,128)S(1)}, u32[]{:S(2)}, u32[]{:S(2)}) %collective-permute-start) | collective-permute-done | bytes 8224 | tf_op jit(solution)/shard_map/ppermute | solution.py:333
  27.3 2.3 %all-to-all-done.x_ref = bf16[8,80,512]{2,1,0:T(8,128)(2,1)S(1)} async-done(((bf16[8,80,512]{2,1,0:T(8,128)(2,1)}), bf16[8,80,512]{2,1,0:T(8,128)(2,1)S(1)}, u32[]{:S(2)}, u32[]{:S(2)}) %all-to-all-start) | async-done | bytes 655392 | tf_op jit(solution)/shard_map/all_to_all | solution.py:334
  29.5 0.6 collective-permute-start.1
  30.1 0.7 broadcast_in_dim.2
  30.9 8.6 %all-to-all-start.1 = ((f32[16,1,2048]{2,1,0:T(1,128)}), f32[16,1,2048]{2,1,0:T(1,128)S(1)}, u32[]{:S(2)}, u32[]{:S(2)}) async-start(f32[16,1,2048]{2,1,0:T(1,128)} %broadcast_in_dim.2), calls=%async_computation.1 | async-start | bytes 262144 | tf_op jit(solution)/shard_map/all_to_all | solution.py:338
  39.5 1.4 pick.1
  40.9 9.0 %all-to-all-done.1 = f32[16,1,2048]{2,1,0:T(1,128)S(1)} async-done(((f32[16,1,2048]{2,1,0:T(1,128)}), f32[16,1,2048]{2,1,0:T(1,128)S(1)}, u32[]{:S(2)}, u32[]{:S(2)}) %all-to-all-start.1) | async-done | bytes 131104 | tf_op jit(solution)/shard_map/all_to_all | solution.py:338
  49.9 0.1 reduce_sum.19
  50.0 0.0 copy-start
  50.0 1.6 copy-done
  51.7 2.1 %scaled.1.cot_ref = bf16[2048,512]{1,0:T(8,128)(2,1)} custom-call(f32[1,2048]{1,0:T(1,128)S(1)} %bitcast.9, bf16[2048,512]{1,0:T(8,128)(2,1)S(1)} %copy-done), custom_call_target="tpu_custom_call" | custom-call | tf_op jit(solution)/shard_map/scaled/pallas_call | solution.py:153
  53.7 5.9 %all-to-all-start.2 = ((bf16[8,80,512]{2,1,0:T(8,128)(2,1)}), bf16[8,80,512]{2,1,0:T(8,128)(2,1)S(1)}, u32[]{:S(2)}, u32[]{:S(2)}) async-start(bf16[8,80,512]{2,1,0:T(8,128)(2,1)} %pick.1), calls=%async_computation.2 | async-start | bytes 1310720 | tf_op jit(solution)/shard_map/all_to_all | solution.py:342
  59.6 12.4 %all-gather.2.cloned.1.call-done.x_ref = bf16[2048,2048]{1,0:T(8,128)(2,1)} async-done(((bf16[128,2048]{1,0:T(8,128)(2,1)}), bf16[2048,2048]{1,0:T(8,128)(2,1)}) %all-gather.2.cloned.1.call-update) | async-done | bytes 8388624 | tf_op jit(solution)/shard_map/all_gather | solution.py:329
  72.1 8.0 %partials.2.refs_1_ = bf16[2,8,4,64,512]{4,3,2,1,0:T(8,128)(2,1)} custom-call(s32[1]{0:T(128)} %bitcast.1.place_ref, bf16[2048,2048]{1,0:T(8,128)(2,1)} %all-gather.2.cloned.1.call-done.x_ref, bf16[2048,512]{1,0:T(8,128)(2,1)} %scaled.1.cot_ref), custom_call_target="tpu_custom_call" | custom-call | flops 4294967296 | bytes 12582912 | tf_op jit(solution)/shard_map/partials/pallas_call | solution.py:208
  80.1 0.0 collective-permute-done.1.cot_ref
  80.1 7.5 %partials.3 = bf16[2,8,4,64,512]{4,3,2,1,0:T(8,128)(2,1)} custom-call(s32[1]{0:T(128)S(6)} %sub.3.place_ref, bf16[2048,2048]{1,0:T(8,128)(2,1)} %all-gather.2.cloned.1.call-done.x_ref, bf16[2048,512]{1,0:T(8,128)(2,1)S(1)} %collective-permute-done.1.cot_ref, f32[1,2048]{1,0:T(1,128)S(1)} %bitcast.10, ...), custom_call_target="tpu_custom_call", output_to_operand_aliasing={{}: (4, {})} | custom-call | flops 4294967296 | bytes 12582912 | tf_op jit(solution)/shard_map/partials/pallas_call | solution.py:208
  87.6 0.0 all-to-all-done.2.x_ref
  87.6 56.6 %all_to_all.26 = bf16[16,4,64,512]{3,2,1,0:T(8,128)(2,1)S(1)} all-to-all(bf16[16,4,64,512]{3,2,1,0:T(8,128)(2,1)} %bitcast.13), channel_id=1, replica_groups=mesh['y'=4,'xh'=2,'xl'=2,'z'=8,'core'=2] {'xl','y','xh'}, dimensions={0} | all-to-all | bytes 8388608 | tf_op jit(solution)/shard_map/all_to_all | solution.py:349
  144.2 2.0 %route.1 = bf16[8,2,64,512]{3,2,1,0:T(8,128)(2,1)} custom-call(s32[8]{0:T(128)S(1)} %bitcast.12, bf16[2,8,4,64,512]{4,3,2,1,0:T(8,128)(2,1)S(1)} %bitcast.8), custom_call_target="tpu_custom_call" | custom-call | tf_op jit(solution)/shard_map/route/pallas_call | solution.py:239
  146.2 5.1 %all-to-all-start.4 = ((bf16[8,2,64,512]{3,2,1,0:T(8,128)(2,1)}), bf16[8,2,64,512]{3,2,1,0:T(8,128)(2,1)S(1)}, u32[]{:S(2)}, u32[]{:S(2)}) async-start(bf16[8,2,64,512]{3,2,1,0:T(8,128)(2,1)} %route.1), calls=%async_computation.4 | async-start | bytes 2097152 | tf_op jit(solution)/shard_map/all_to_all | solution.py:351
  152.0 0.3 unpack_roots.1
  152.3 12.8 %all-to-all-done.4.u_ref = bf16[8,2,64,512]{3,2,1,0:T(8,128)(2,1)S(1)} async-done(((bf16[8,2,64,512]{3,2,1,0:T(8,128)(2,1)}), bf16[8,2,64,512]{3,2,1,0:T(8,128)(2,1)S(1)}, u32[]{:S(2)}, u32[]{:S(2)}) %all-to-all-start.4) | async-done | bytes 1048608 | tf_op jit(solution)/shard_map/all_to_all | solution.py:351
  165.1 7.4 %block_step.1 = (bf16[512,512]{1,0:T(8,128)(2,1)}, f32[512,512]{1,0:T(8,128)}, f32[512,512]{1,0:T(8,128)}, f32[512,512]{1,0:T(8,128)}, f32[512,512]{1,0:T(8,128)}) custom-call(s32[1,1]{1,0:T(1,128)S(6)} %copy.18.refresh_ref, bf16[8,2,64,512]{3,2,1,0:T(8,128)(2,1)S(1)} %all-to-all-done.4.u_ref, bf16[512,512]{1,0:T(8,128)(2,1)S(1)} %get-tuple-element.27.lroot_ref, ...), custom_call_target="tpu_custom_call" | custom-call | flops 2147483648 | bytes 11534336 | tf_op jit(solution)/shard_map/block_step/pallas_call | solution.py:310
  (4 shorter events, 0.0 us)
Async XLA Ops:
  7.2 12.0 %copy-start.2 = (bf16[2048,128]{1,0:T(8,128)(2,1)S(1)}, bf16[2048,128]{1,0:T(8,128)(2,1)}, u32[]{:S(2)}) copy-start(bf16[2048,128]{1,0:T(8,128)(2,1)} %x_ref.2) | copy-start | bytes 1572868
  7.2 32.3 %copy-start.1 = (s32[1,8]{1,0:T(1,128)S(1)}, s32[1,8]{1,0:T(1,128)}, u32[]{:S(2)}) copy-start(s32[1,8]{1,0:T(1,128)} %param.12) | copy-start | bytes 100
  7.2 64.9 %all-gather.2.cloned.1.call-start = ((), (), s32[]{:S(2)}) async-start(), calls=%async_computation.5 | async-start | bytes 8912896 | tf_op jit(solution)/shard_map/all_gather | solution.py:329
  11.7 17.8 %all-to-all-start = ((bf16[8,80,512]{2,1,0:T(8,128)(2,1)}), bf16[8,80,512]{2,1,0:T(8,128)(2,1)S(1)}, u32[]{:S(2)}, u32[]{:S(2)}) async-start(bf16[8,80,512]{2,1,0:T(8,128)(2,1)} %pack_roots.1), calls=%async_computation | async-start | bytes 1310720 | tf_op jit(solution)/shard_map/all_to_all | solution.py:334
  19.5 7.8 %collective-permute-start = (f32[1,2048]{1,0:T(1,128)S(1)}, f32[1,2048]{1,0:T(1,128)S(1)}, u32[]{:S(2)}, u32[]{:S(2)}) collective-permute-start(f32[1,2048]{1,0:T(1,128)S(1)} %bitcast.14), channel_id=1, source_target_pairs={{0,16},{16,0},{1,17},{17,1},{2,18},{18,2},{3,19},{19,3},{4,20},{20... | collective-permute-start | bytes 24584 | tf_op jit(solution)/shard_map/ppermute | solution.py:333
  29.5 50.6 %collective-permute-start.1 = (bf16[2048,512]{1,0:T(8,128)(2,1)}, bf16[2048,512]{1,0:T(8,128)(2,1)S(1)}, u32[]{:S(2)}, u32[]{:S(2)}) collective-permute-start(bf16[2048,512]{1,0:T(8,128)(2,1)} %x_ref.3), channel_id=1, source_target_pairs={{0,16},{16,0},{1,17},{17,1},{2,18},{18,2},{3,19},{19,3},{4,20},{20... | collective-permute-start | bytes 6291464 | tf_op jit(solution)/shard_map/ppermute | solution.py:336
  30.9 19.1 %all-to-all-start.1 = ((f32[16,1,2048]{2,1,0:T(1,128)}), f32[16,1,2048]{2,1,0:T(1,128)S(1)}, u32[]{:S(2)}, u32[]{:S(2)}) async-start(f32[16,1,2048]{2,1,0:T(1,128)} %broadcast_in_dim.2), calls=%async_computation.1 | async-start | bytes 262144 | tf_op jit(solution)/shard_map/all_to_all | solution.py:338
  50.0 1.6 copy-start
  53.7 33.9 %all-to-all-start.2 = ((bf16[8,80,512]{2,1,0:T(8,128)(2,1)}), bf16[8,80,512]{2,1,0:T(8,128)(2,1)S(1)}, u32[]{:S(2)}, u32[]{:S(2)}) async-start(bf16[8,80,512]{2,1,0:T(8,128)(2,1)} %pick.1), calls=%async_computation.2 | async-start | bytes 1310720 | tf_op jit(solution)/shard_map/all_to_all | solution.py:342
  146.2 18.9 %all-to-all-start.4 = ((bf16[8,2,64,512]{3,2,1,0:T(8,128)(2,1)}), bf16[8,2,64,512]{3,2,1,0:T(8,128)(2,1)S(1)}, u32[]{:S(2)}, u32[]{:S(2)}) async-start(bf16[8,2,64,512]{3,2,1,0:T(8,128)(2,1)} %route.1), calls=%async_computation.4 | async-start | bytes 2097152 | tf_op jit(solution)/shard_map/all_to_all | solution.py:351
Sparse Core Ops, SparseCore 0:
  10.4 61.5 all-gather.1

commit v10 on v9

--- a/solution.py
+++ b/solution.py
@@ -12,7 +12,7 @@
 RIDGE_TERM = 1e-06
 BLK = 512
 N_GROUP = 8
-LOAD = 512
+STEPS = 2
 CHUNK = BLK // N_GROUP
 PACKED = CHUNK + 16
 GROUP = ("y", "xh")
@@ -59,10 +59,10 @@
 
 def prepare(x, gain):
     tokens, width = x.shape
-    step = tokens // 2
+    step = tokens // STEPS
     return pl.pallas_call(
         prepare_kernel,
-        grid=(2,),
+        grid=(STEPS,),
         in_specs=[pl.BlockSpec((step, width), lambda i: (i, 0)), pl.BlockSpec((1, width), lambda i: (0, 0))],
         out_specs=pl.BlockSpec((width, step), lambda i: (0, i)),
         out_shape=pltpu.HBM((width, tokens), BF16),
@@ -163,12 +163,11 @@
 def partials_kernel(place_ref, x_ref, cot_ref, *refs):
     *rest, o_ref, local, scaled_ref, part_ref, sems = refs
     rows, tokens = local.shape
-    slabs, pieces = rows // BLK, rows // LOAD
-    loads = [
-        pltpu.make_async_copy(x_ref.at[pl.ds(n * LOAD, LOAD)], local.at[pl.ds(n * LOAD, LOAD)], sems.at[n])
-        for n in range(pieces)
-    ]
+    slabs, pieces = rows // BLK, rows // BLK - 1 + tokens // BLK
     spans = [pl.ds(first, BLK) for first in range(0, tokens, BLK)]
+    parts = [(pl.ds(0, BLK), span) for span in spans]
+    parts += [(pl.ds(first, BLK), pl.ds(0, tokens)) for first in range(BLK, rows, BLK)]
+    loads = [pltpu.make_async_copy(x_ref.at[at], local.at[at], sems.at[n]) for n, at in enumerate(parts)]
     cots = [
         pltpu.make_async_copy(cot_ref.at[span], scaled_ref.at[span], sems.at[pieces + n])
         for n, span in enumerate(spans)
@@ -177,24 +176,26 @@
         pltpu.make_async_copy(part_ref.at[i], o_ref.at[place_ref[0], :, i], sems.at[pieces + len(spans) + i])
         for i in range(slabs)
     ]
-    for load in loads[: BLK // LOAD]:
+    for n, span in enumerate(spans):
+        loads[n].start()
+        if not rest:
+            cots[n].start()
+    for load in loads[len(spans) :]:
         load.start()
-    if not rest:
-        for copy in cots:
-            copy.start()
-    for load in loads[BLK // LOAD :]:
-        load.start()
-    if rest:
-        column = column_of(rest[0])
-        for span in spans:
+    column = column_of(rest[0]) if rest else None
+    part = jnp.zeros((BLK, BLK), F32)
+    for n, span in enumerate(spans):
+        if rest:
             scaled_ref[span] = (cot_ref[span].astype(F32) * column[span.start : span.start + BLK]).astype(BF16)
-    else:
-        for copy in cots:
-            copy.wait()
+        else:
+            cots[n].wait()
+        loads[n].wait()
+        part = part + dot(local[:BLK, span], scaled_ref[span])
     for i in range(slabs):
-        for load in loads[i * (BLK // LOAD) : (i + 1) * (BLK // LOAD)]:
-            load.wait()
-        part = dot(local[i * BLK : (i + 1) * BLK], scaled_ref[...]).astype(BF16)
+        if i > 0:
+            loads[len(spans) + i - 1].wait()
+            part = dot(local[i * BLK : (i + 1) * BLK], scaled_ref[...])
+        part = part.astype(BF16)
         for j in range(N_GROUP):
             part_ref[i, j] = part[j * CHUNK : (j + 1) * CHUNK]
         stores[i].start()
@@ -213,7 +214,7 @@
             pltpu.VMEM((rows, tokens), BF16),
             pltpu.VMEM((tokens, BLK), BF16),
             pltpu.VMEM((slabs, N_GROUP, CHUNK, BLK), BF16),
-            pltpu.SemaphoreType.DMA((rows // LOAD + tokens // BLK + slabs,)),
+            pltpu.SemaphoreType.DMA((2 * slabs - 1 + 2 * tokens // BLK,)),
         ],
         out_shape=pltpu.HBM((2, N_GROUP, slabs, CHUNK, BLK), BF16),
         input_output_aliases={4: 0} if rest else {},
@@ -246,18 +247,23 @@
     )(owner, x)
 
 
-def inverse_fourth_root(statistic):
+def inverse_fourth_roots(statistics):
     rows, cols = triangle()
     eye = (rows == cols).astype(F32)
-    matrix = statistic + RIDGE_TERM * eye
-    scaling = 2.5 * lax.rsqrt(jnp.sum(matrix * matrix, keepdims=True))
-    matrix = scaling * matrix
-    rounded = matrix.astype(BF16)
-    product = dot(rounded, rounded)
-    square = (1.5625 * eye - 0.625 * matrix + 0.0625 * product).astype(BF16)
-    once = (1.25 * matrix - 0.25 * product).astype(BF16)
-    fourth = dot(square, square).astype(BF16)
-    return jnp.sqrt(jnp.sqrt(scaling)) * (1.5625 * eye - 0.3125 * matrix - 0.25 * dot(fourth, once))
+    matrices = [statistic + RIDGE_TERM * eye for statistic in statistics]
+    scalings = [2.5 * lax.rsqrt(jnp.sum(matrix * matrix, keepdims=True)) for matrix in matrices]
+    matrices = [scaling * matrix for scaling, matrix in zip(scalings, matrices)]
+    rounded = [matrix.astype(BF16) for matrix in matrices]
+    products = [dot(matrix, matrix) for matrix in rounded]
+    pairs = list(zip(matrices, products))
+    squares = [(1.5625 * eye - 0.625 * matrix + 0.0625 * product).astype(BF16) for matrix, product in pairs]
+    once = [(1.25 * matrix - 0.25 * product).astype(BF16) for matrix, product in pairs]
+    fourths = [dot(square, square).astype(BF16) for square in squares]
+    lasts = [dot(fourth, factor) for fourth, factor in zip(fourths, once)]
+    return [
+        jnp.sqrt(jnp.sqrt(scaling)) * (1.5625 * eye - 0.3125 * matrix - 0.25 * last)
+        for scaling, matrix, last in zip(scalings, matrices, lasts)
+    ]
 
 
 def block_kernel(
@@ -286,8 +292,9 @@
 
     @pl.when(fresh)
     def _():
-        for accum, new, copy in ((left, left_new, news[0]), (right, right_new, news[1])):
-            new[...] = inverse_fourth_root(accum[...])
+        values = inverse_fourth_roots([left[...], right[...]])
+        for value, new, copy in zip(values, (left_new, right_new), news):
+            new[...] = value
             copy.start()
 
     @pl.when(jnp.logical_not(fresh))

time: 180 us -> 179 us (level)
  the two profiles are of different devices: /device:TPU:8 before, /device:TPU:1 now
where the time goes in v10:
time: 179 us; the launch traced here: 177 us
  blocking collectives  55.5 us (31%)
  waiting for transfers between devices  44.1 us (25%)
  Pallas kernels  32.3 us (18%)
  starting transfers between devices  27.8 us (16%)
  between operations  14.8 us (8%)
  local copies, waits for them, and re-layouts  2.38 us (1%)
    all_to_all x1, blocking collectives, body(): lax.all_to_all(pieces, ('xl', 'y', 'xh'), split_axis=0, concat_axis=0, ti...  55.5 us
    pallas_call x2, Pallas kernels, partials(): pl.pallas_call(partials_kernel, in_specs=[SMEM, HBM] + ([VMEM, VMEM, HBM]...  14.8 us
    all_gather x1, waiting for transfers between devices, body(): lax.all_gather(prepare(inputs, norm_gain), ('z', 'core'), axis=0, tiled=T...  12.9 us
    all_to_all x1, waiting for transfers between devices, body(): lax.all_to_all(grads, TURNED, split_axis=0, concat_axis=0, tiled=True)  12.4 us
    all_to_all x1, starting transfers between devices, body(): lax.all_to_all(squares, ('z', 'core'), split_axis=0, concat_axis=0, tiled...  11.6 us
    all_to_all x2, starting transfers between devices, body(): lax.all_to_all(roots, TURNED, split_axis=0, concat_axis=0, tiled=True)  11.3 us
    all_to_all x1, waiting for transfers between devices, body(): lax.all_to_all(squares, ('z', 'core'), split_axis=0, concat_axis=0, tiled...  9.23 us
    pallas_call x1, Pallas kernels, block_step(): pl.pallas_call(block_kernel, in_specs=[SMEM, VMEM, VMEM, VMEM] + [HBM] *...  7.14 us
  transfers between devices with their start and end apart: 7, of which 5 were waited for; matrix products, arithmetic and copies ran while one was open for 1% of the time, Pallas kernels for 12%

profile of v10, /device:TPU:1, one launch (start us, length us, event | category | flops | bytes accessed | tf_op | source)
XLA Modules:
  0.0 177.3 jit_solution(10623671903442953644)
XLA Ops:
  7.2 0.0 copy-start.2
  7.2 0.0 copy-start.1
  7.2 0.0 all-gather.2.cloned.1.call-start
  7.2 2.0 %prepare.1 = bf16[128,2048]{1,0:T(8,128)(2,1)} custom-call(bf16[2048,128]{1,0:T(8,128)(2,1)} %x_ref.2, bf16[1,128]{1,0:T(2,128)(2,1)} %bitcast.17), custom_call_target="tpu_custom_call" | custom-call | tf_op jit(solution)/shard_map/prepare/pallas_call | solution.py:63
  9.2 0.0 all-gather.2.cloned.1.call-update
  9.2 2.5 %pack_roots.1 = bf16[8,80,512]{2,1,0:T(8,128)(2,1)} custom-call(f32[512,512]{1,0:T(8,128)} %li_ref.1, f32[512,512]{1,0:T(8,128)} %ri_ref.1), custom_call_target="tpu_custom_call" | custom-call | tf_op jit(solution)/shard_map/pack_roots/pallas_call | solution.py:95
  11.7 7.5 %all-to-all-start = ((bf16[8,80,512]{2,1,0:T(8,128)(2,1)}), bf16[8,80,512]{2,1,0:T(8,128)(2,1)S(1)}, u32[]{:S(2)}, u32[]{:S(2)}) async-start(bf16[8,80,512]{2,1,0:T(8,128)(2,1)} %pack_roots.1), calls=%async_computation | async-start | bytes 1310720 | tf_op jit(solution)/shard_map/all_to_all | solution.py:341
  19.2 0.3 multiply_reduce_fusion
  19.6 0.4 collective-permute-start
  20.0 7.1 %collective-permute-done = f32[1,2048]{1,0:T(1,128)S(1)} collective-permute-done((f32[1,2048]{1,0:T(1,128)S(1)}, f32[1,2048]{1,0:T(1,128)S(1)}, u32[]{:S(2)}, u32[]{:S(2)}) %collective-permute-start) | collective-permute-done | bytes 8224 | tf_op jit(solution)/shard_map/ppermute | solution.py:340
  27.0 2.5 %all-to-all-done.x_ref = bf16[8,80,512]{2,1,0:T(8,128)(2,1)S(1)} async-done(((bf16[8,80,512]{2,1,0:T(8,128)(2,1)}), bf16[8,80,512]{2,1,0:T(8,128)(2,1)S(1)}, u32[]{:S(2)}, u32[]{:S(2)}) %all-to-all-start) | async-done | bytes 655392 | tf_op jit(solution)/shard_map/all_to_all | solution.py:341
  29.6 0.3 collective-permute-start.1
  29.9 0.7 broadcast_in_dim.2
  30.6 11.6 %all-to-all-start.1 = ((f32[16,1,2048]{2,1,0:T(1,128)}), f32[16,1,2048]{2,1,0:T(1,128)S(1)}, u32[]{:S(2)}, u32[]{:S(2)}) async-start(f32[16,1,2048]{2,1,0:T(1,128)} %broadcast_in_dim.2), calls=%async_computation.1 | async-start | bytes 262144 | tf_op jit(solution)/shard_map/all_to_all | solution.py:345
  42.2 1.4 pick.1
  43.6 9.2 %all-to-all-done.1 = f32[16,1,2048]{2,1,0:T(1,128)S(1)} async-done(((f32[16,1,2048]{2,1,0:T(1,128)}), f32[16,1,2048]{2,1,0:T(1,128)S(1)}, u32[]{:S(2)}, u32[]{:S(2)}) %all-to-all-start.1) | async-done | bytes 131104 | tf_op jit(solution)/shard_map/all_to_all | solution.py:345
  52.9 0.1 reduce_sum.19
  53.0 0.0 copy-start
  53.0 1.6 copy-done
  54.6 2.1 %scaled.1.cot_ref = bf16[2048,512]{1,0:T(8,128)(2,1)} custom-call(f32[1,2048]{1,0:T(1,128)S(1)} %bitcast.9, bf16[2048,512]{1,0:T(8,128)(2,1)S(1)} %copy-done), custom_call_target="tpu_custom_call" | custom-call | tf_op jit(solution)/shard_map/scaled/pallas_call | solution.py:153
  56.7 3.8 %all-to-all-start.2 = ((bf16[8,80,512]{2,1,0:T(8,128)(2,1)}), bf16[8,80,512]{2,1,0:T(8,128)(2,1)S(1)}, u32[]{:S(2)}, u32[]{:S(2)}) async-start(bf16[8,80,512]{2,1,0:T(8,128)(2,1)} %pick.1), calls=%async_computation.2 | async-start | bytes 1310720 | tf_op jit(solution)/shard_map/all_to_all | solution.py:349
  60.5 12.9 %all-gather.2.cloned.1.call-done.x_ref = bf16[2048,2048]{1,0:T(8,128)(2,1)} async-done(((bf16[128,2048]{1,0:T(8,128)(2,1)}), bf16[2048,2048]{1,0:T(8,128)(2,1)}) %all-gather.2.cloned.1.call-update) | async-done | bytes 8388624 | tf_op jit(solution)/shard_map/all_gather | solution.py:336
  73.4 7.6 %partials.2.refs_1_ = bf16[2,8,4,64,512]{4,3,2,1,0:T(8,128)(2,1)} custom-call(s32[1]{0:T(128)} %bitcast.1.place_ref, bf16[2048,2048]{1,0:T(8,128)(2,1)} %all-gather.2.cloned.1.call-done.x_ref, bf16[2048,512]{1,0:T(8,128)(2,1)} %scaled.1.cot_ref), custom_call_target="tpu_custom_call" | custom-call | flops 4294967296 | bytes 12582912 | tf_op jit(solution)/shard_map/partials/pallas_call | solution.py:209
  81.0 0.0 collective-permute-done.1.cot_ref
  81.0 7.3 %partials.3 = bf16[2,8,4,64,512]{4,3,2,1,0:T(8,128)(2,1)} custom-call(s32[1]{0:T(128)S(6)} %sub.3.place_ref, bf16[2048,2048]{1,0:T(8,128)(2,1)} %all-gather.2.cloned.1.call-done.x_ref, bf16[2048,512]{1,0:T(8,128)(2,1)S(1)} %collective-permute-done.1.cot_ref, f32[1,2048]{1,0:T(1,128)S(1)} %bitcast.10, ...), custom_call_target="tpu_custom_call", output_to_operand_aliasing={{}: (4, {})} | custom-call | flops 4294967296 | bytes 12582912 | tf_op jit(solution)/shard_map/partials/pallas_call | solution.py:209
  88.2 0.0 all-to-all-done.2.x_ref
  88.2 55.5 %all_to_all.26 = bf16[16,4,64,512]{3,2,1,0:T(8,128)(2,1)S(1)} all-to-all(bf16[16,4,64,512]{3,2,1,0:T(8,128)(2,1)} %bitcast.13), channel_id=1, replica_groups=mesh['y'=4,'xh'=2,'xl'=2,'z'=8,'core'=2] {'xl','y','xh'}, dimensions={0} | all-to-all | bytes 8388608 | tf_op jit(solution)/shard_map/all_to_all | solution.py:356
  143.8 2.0 %route.1 = bf16[8,2,64,512]{3,2,1,0:T(8,128)(2,1)} custom-call(s32[8]{0:T(128)S(1)} %bitcast.12, bf16[2,8,4,64,512]{4,3,2,1,0:T(8,128)(2,1)S(1)} %bitcast.8), custom_call_target="tpu_custom_call" | custom-call | tf_op jit(solution)/shard_map/route/pallas_call | solution.py:240
  145.8 4.1 %all-to-all-start.4 = ((bf16[8,2,64,512]{3,2,1,0:T(8,128)(2,1)}), bf16[8,2,64,512]{3,2,1,0:T(8,128)(2,1)S(1)}, u32[]{:S(2)}, u32[]{:S(2)}) async-start(bf16[8,2,64,512]{3,2,1,0:T(8,128)(2,1)} %route.1), calls=%async_computation.4 | async-start | bytes 2097152 | tf_op jit(solution)/shard_map/all_to_all | solution.py:358
  150.6 0.3 unpack_roots.1
  150.9 12.4 %all-to-all-done.4.u_ref = bf16[8,2,64,512]{3,2,1,0:T(8,128)(2,1)S(1)} async-done(((bf16[8,2,64,512]{3,2,1,0:T(8,128)(2,1)}), bf16[8,2,64,512]{3,2,1,0:T(8,128)(2,1)S(1)}, u32[]{:S(2)}, u32[]{:S(2)}) %all-to-all-start.4) | async-done | bytes 1048608 | tf_op jit(solution)/shard_map/all_to_all | solution.py:358
  163.3 7.1 %block_step.1 = (bf16[512,512]{1,0:T(8,128)(2,1)}, f32[512,512]{1,0:T(8,128)}, f32[512,512]{1,0:T(8,128)}, f32[512,512]{1,0:T(8,128)}, f32[512,512]{1,0:T(8,128)}) custom-call(s32[1,1]{1,0:T(1,128)S(6)} %copy.18.refresh_ref, bf16[8,2,64,512]{3,2,1,0:T(8,128)(2,1)S(1)} %all-to-all-done.4.u_ref, bf16[512,512]{1,0:T(8,128)(2,1)S(1)} %get-tuple-element.27.lroot_ref, ...), custom_call_target="tpu_custom_call" | custom-call | flops 2147483648 | bytes 11534336 | tf_op jit(solution)/shard_map/block_step/pallas_call | solution.py:317
  (4 shorter events, 0.0 us)
Async XLA Ops:
  7.2 12.1 %copy-start.2 = (bf16[2048,128]{1,0:T(8,128)(2,1)S(1)}, bf16[2048,128]{1,0:T(8,128)(2,1)}, u32[]{:S(2)}) copy-start(bf16[2048,128]{1,0:T(8,128)(2,1)} %x_ref.2) | copy-start | bytes 1572868
  7.2 35.0 %copy-start.1 = (s32[1,8]{1,0:T(1,128)S(1)}, s32[1,8]{1,0:T(1,128)}, u32[]{:S(2)}) copy-start(s32[1,8]{1,0:T(1,128)} %param.12) | copy-start | bytes 100
  7.2 66.2 %all-gather.2.cloned.1.call-start = ((), (), s32[]{:S(2)}) async-start(), calls=%async_computation.5 | async-start | bytes 8912896 | tf_op jit(solution)/shard_map/all_gather | solution.py:336
  11.7 17.8 %all-to-all-start = ((bf16[8,80,512]{2,1,0:T(8,128)(2,1)}), bf16[8,80,512]{2,1,0:T(8,128)(2,1)S(1)}, u32[]{:S(2)}, u32[]{:S(2)}) async-start(bf16[8,80,512]{2,1,0:T(8,128)(2,1)} %pack_roots.1), calls=%async_computation | async-start | bytes 1310720 | tf_op jit(solution)/shard_map/all_to_all | solution.py:341
  19.6 7.5 %collective-permute-start = (f32[1,2048]{1,0:T(1,128)S(1)}, f32[1,2048]{1,0:T(1,128)S(1)}, u32[]{:S(2)}, u32[]{:S(2)}) collective-permute-start(f32[1,2048]{1,0:T(1,128)S(1)} %bitcast.14), channel_id=1, source_target_pairs={{0,16},{16,0},{1,17},{17,1},{2,18},{18,2},{3,19},{19,3},{4,20},{20... | collective-permute-start | bytes 24584 | tf_op jit(solution)/shard_map/ppermute | solution.py:340
  29.6 51.4 %collective-permute-start.1 = (bf16[2048,512]{1,0:T(8,128)(2,1)}, bf16[2048,512]{1,0:T(8,128)(2,1)S(1)}, u32[]{:S(2)}, u32[]{:S(2)}) collective-permute-start(bf16[2048,512]{1,0:T(8,128)(2,1)} %x_ref.3), channel_id=1, source_target_pairs={{0,16},{16,0},{1,17},{17,1},{2,18},{18,2},{3,19},{19,3},{4,20},{20... | collective-permute-start | bytes 6291464 | tf_op jit(solution)/shard_map/ppermute | solution.py:343
  30.6 22.2 %all-to-all-start.1 = ((f32[16,1,2048]{2,1,0:T(1,128)}), f32[16,1,2048]{2,1,0:T(1,128)S(1)}, u32[]{:S(2)}, u32[]{:S(2)}) async-start(f32[16,1,2048]{2,1,0:T(1,128)} %broadcast_in_dim.2), calls=%async_computation.1 | async-start | bytes 262144 | tf_op jit(solution)/shard_map/all_to_all | solution.py:345
  53.0 1.7 copy-start
  56.7 31.5 %all-to-all-start.2 = ((bf16[8,80,512]{2,1,0:T(8,128)(2,1)}), bf16[8,80,512]{2,1,0:T(8,128)(2,1)S(1)}, u32[]{:S(2)}, u32[]{:S(2)}) async-start(bf16[8,80,512]{2,1,0:T(8,128)(2,1)} %pick.1), calls=%async_computation.2 | async-start | bytes 1310720 | tf_op jit(solution)/shard_map/all_to_all | solution.py:349
  145.8 17.5 %all-to-all-start.4 = ((bf16[8,2,64,512]{3,2,1,0:T(8,128)(2,1)}), bf16[8,2,64,512]{3,2,1,0:T(8,128)(2,1)S(1)}, u32[]{:S(2)}, u32[]{:S(2)}) async-start(bf16[8,2,64,512]{3,2,1,0:T(8,128)(2,1)} %route.1), calls=%async_computation.4 | async-start | bytes 2097152 | tf_op jit(solution)/shard_map/all_to_all | solution.py:358
Sparse Core Ops, SparseCore 0:
  10.4 62.9 all-gather.1

commit v11 on v10

--- a/solution.py
+++ b/solution.py
@@ -12,7 +12,6 @@
 RIDGE_TERM = 1e-06
 BLK = 512
 N_GROUP = 8
-STEPS = 2
 CHUNK = BLK // N_GROUP
 PACKED = CHUNK + 16
 GROUP = ("y", "xh")
@@ -53,21 +52,41 @@
     return high, (a - high.astype(F32)).astype(BF16)
 
 
-def prepare_kernel(x_ref, gain_ref, xt_ref):
-    xt_ref[...] = (x_ref[...].astype(F32) * gain_ref[...].astype(F32)).astype(BF16).T
+def prepare_kernel(x_ref, gain_ref, xt_ref, local, turned_ref, gain_local, sems):
+    spans = [pl.ds(n * BLK, BLK) for n in range(local.shape[0] // BLK)]
+    count = len(spans)
+    loads = [pltpu.make_async_copy(x_ref.at[s], local.at[s], sems.at[n]) for n, s in enumerate(spans)]
+    stores = [pltpu.make_async_copy(turned_ref.at[:, s], xt_ref.at[:, s], sems.at[count + n]) for n, s in enumerate(spans)]
+    gain_load = pltpu.make_async_copy(gain_ref, gain_local, sems.at[2 * count])
+    gain_load.start()
+    for load in loads:
+        load.start()
+    gain_load.wait()
+    gain = gain_local[...].astype(F32)
+    for n, span in enumerate(spans):
+        loads[n].wait()
+        turned_ref[:, span] = (local[span].astype(F32) * gain).astype(BF16).T
+        stores[n].start()
+    for store in stores:
+        store.wait()
 
 
 def prepare(x, gain):
     tokens, width = x.shape
-    step = tokens // STEPS
     return pl.pallas_call(
         prepare_kernel,
-        grid=(STEPS,),
-        in_specs=[pl.BlockSpec((step, width), lambda i: (i, 0)), pl.BlockSpec((1, width), lambda i: (0, 0))],
-        out_specs=pl.BlockSpec((width, step), lambda i: (0, i)),
+        in_specs=[HBM, HBM],
+        out_specs=HBM,
         out_shape=pltpu.HBM((width, tokens), BF16),
+        scratch_shapes=[
+            pltpu.VMEM((tokens, width), BF16),
+            pltpu.VMEM((width, tokens), BF16),
+            pltpu.VMEM((1, width), BF16),
+            pltpu.SemaphoreType.DMA((2 * tokens // BLK + 1,)),
+        ],
+        compiler_params=params(),
         name="prepare",
-    )(x, gain.reshape(1, width))
+    )(in_hbm(x), in_hbm(gain.reshape(1, width)))
 
 
 def triangle():
@@ -224,24 +243,29 @@
     )(place, in_hbm(x), cot if rest else in_hbm(cot), *rest)
 
 
-def route_kernel(owner_ref, x_ref, o_ref):
+def route_kernel(owner_ref, x_ref, o_ref, sums, sems):
+    copies = []
     for half in range(2):
         for n in range(x_ref.shape[2]):
             value = x_ref[half, 0, n].astype(F32)
             for g in range(1, N_GROUP):
                 value = value + x_ref[half, g, n].astype(F32)
-            value = value.astype(BF16)
             slab = half * x_ref.shape[2] + n
-            o_ref[turned(slab), 1] = value
-            o_ref[turned(owner_ref[slab]), 0] = value
+            sums[slab] = value.astype(BF16)
+            for kind, dest in enumerate((turned(owner_ref[slab]), turned(slab))):
+                copies.append(pltpu.make_async_copy(sums.at[slab], o_ref.at[dest, kind], sems.at[2 * slab + kind]))
+                copies[-1].start()
+    for copy in copies:
+        copy.wait()
 
 
 def route(owner, x):
     return pl.pallas_call(
         route_kernel,
         in_specs=[SMEM, VMEM],
-        out_specs=VMEM,
+        out_specs=HBM,
         out_shape=pltpu.HBM((N_GROUP, 2, CHUNK, BLK), BF16),
+        scratch_shapes=[pltpu.VMEM((N_GROUP, CHUNK, BLK), BF16), pltpu.SemaphoreType.DMA((2 * N_GROUP,))],
         compiler_params=params(),
         name="route",
     )(owner, x)

time: 179 us -> 178 us (level)
  Pallas kernels: 32.3 us -> 30 us
    pallas_call x1, Pallas kernels: 7.14 us -> 4.9 us  [block_step(): pl.pallas_call(block_kernel, in_specs=[SMEM, VMEM, VMEM, VMEM] + [HBM] *...]
where the time goes in v11:
time: 178 us; the launch traced here: 175 us
  blocking collectives  55.5 us (31%)
  waiting for transfers between devices  44 us (25%)
  Pallas kernels  30 us (17%)
  starting transfers between devices  27.7 us (16%)
  between operations  14.8 us (8%)
  local copies, waits for them, and re-layouts  2.39 us (1%)
    all_to_all x1, blocking collectives, body(): lax.all_to_all(pieces, ('xl', 'y', 'xh'), split_axis=0, concat_axis=0, ti...  55.5 us
    pallas_call x2, Pallas kernels, partials(): pl.pallas_call(partials_kernel, in_specs=[SMEM, HBM] + ([VMEM, VMEM, HBM]...  14.8 us
    all_gather x1, waiting for transfers between devices, body(): lax.all_gather(prepare(inputs, norm_gain), ('z', 'core'), axis=0, tiled=T...  12.8 us
    all_to_all x1, waiting for transfers between devices, body(): lax.all_to_all(grads, TURNED, split_axis=0, concat_axis=0, tiled=True)  12.4 us
    all_to_all x1, starting transfers between devices, body(): lax.all_to_all(squares, ('z', 'core'), split_axis=0, concat_axis=0, tiled...  11.6 us
    all_to_all x2, starting transfers between devices, body(): lax.all_to_all(roots, TURNED, split_axis=0, concat_axis=0, tiled=True)  11.3 us
    all_to_all x1, waiting for transfers between devices, body(): lax.all_to_all(squares, ('z', 'core'), split_axis=0, concat_axis=0, tiled...  9.23 us
    ppermute x1, waiting for transfers between devices, body(): squares_other = lax.ppermute(squares, 'xl', SWAP)  7.05 us
  transfers between devices with their start and end apart: 7, of which 5 were waited for; matrix products, arithmetic and copies ran while one was open for 1% of the time, Pallas kernels for 12%

profile of v11, /device:TPU:1, one launch (start us, length us, event | category | flops | bytes accessed | tf_op | source)
XLA Modules:
  0.0 174.9 jit_solution(7634746985999532227)
XLA Ops:
  7.2 0.0 copy-start.2
  7.2 0.0 copy-start.1
  7.2 0.0 all-gather.2.cloned.1.call-start
  7.2 2.1 %prepare.1 = bf16[128,2048]{1,0:T(8,128)(2,1)} custom-call(bf16[2048,128]{1,0:T(8,128)(2,1)} %x_ref.2, bf16[1,128]{1,0:T(2,128)(2,1)} %bitcast.17), custom_call_target="tpu_custom_call" | custom-call | tf_op jit(solution)/shard_map/prepare/pallas_call | solution.py:76
  9.3 0.0 all-gather.2.cloned.1.call-update
  9.3 2.5 %pack_roots.1 = bf16[8,80,512]{2,1,0:T(8,128)(2,1)} custom-call(f32[512,512]{1,0:T(8,128)} %li_ref.1, f32[512,512]{1,0:T(8,128)} %ri_ref.1), custom_call_target="tpu_custom_call" | custom-call | tf_op jit(solution)/shard_map/pack_roots/pallas_call | solution.py:114
  11.8 7.5 %all-to-all-start = ((bf16[8,80,512]{2,1,0:T(8,128)(2,1)}), bf16[8,80,512]{2,1,0:T(8,128)(2,1)S(1)}, u32[]{:S(2)}, u32[]{:S(2)}) async-start(bf16[8,80,512]{2,1,0:T(8,128)(2,1)} %pack_roots.1), calls=%async_computation | async-start | bytes 1310720 | tf_op jit(solution)/shard_map/all_to_all | solution.py:365
  19.3 0.3 multiply_reduce_fusion
  19.7 0.4 collective-permute-start
  20.1 7.1 %collective-permute-done = f32[1,2048]{1,0:T(1,128)S(1)} collective-permute-done((f32[1,2048]{1,0:T(1,128)S(1)}, f32[1,2048]{1,0:T(1,128)S(1)}, u32[]{:S(2)}, u32[]{:S(2)}) %collective-permute-start) | collective-permute-done | bytes 8224 | tf_op jit(solution)/shard_map/ppermute | solution.py:364
  27.1 2.5 %all-to-all-done.x_ref = bf16[8,80,512]{2,1,0:T(8,128)(2,1)S(1)} async-done(((bf16[8,80,512]{2,1,0:T(8,128)(2,1)}), bf16[8,80,512]{2,1,0:T(8,128)(2,1)S(1)}, u32[]{:S(2)}, u32[]{:S(2)}) %all-to-all-start) | async-done | bytes 655392 | tf_op jit(solution)/shard_map/all_to_all | solution.py:365
  29.7 0.3 collective-permute-start.1
  30.0 0.7 broadcast_in_dim.2
  30.7 11.6 %all-to-all-start.1 = ((f32[16,1,2048]{2,1,0:T(1,128)}), f32[16,1,2048]{2,1,0:T(1,128)S(1)}, u32[]{:S(2)}, u32[]{:S(2)}) async-start(f32[16,1,2048]{2,1,0:T(1,128)} %broadcast_in_dim.2), calls=%async_computation.1 | async-start | bytes 262144 | tf_op jit(solution)/shard_map/all_to_all | solution.py:369
  42.3 1.4 pick.1
  43.7 9.2 %all-to-all-done.1 = f32[16,1,2048]{2,1,0:T(1,128)S(1)} async-done(((f32[16,1,2048]{2,1,0:T(1,128)}), f32[16,1,2048]{2,1,0:T(1,128)S(1)}, u32[]{:S(2)}, u32[]{:S(2)}) %all-to-all-start.1) | async-done | bytes 131104 | tf_op jit(solution)/shard_map/all_to_all | solution.py:369
  53.0 0.1 reduce_sum.19
  53.1 0.0 copy-start
  53.1 1.7 copy-done
  54.7 2.1 %scaled.1.cot_ref = bf16[2048,512]{1,0:T(8,128)(2,1)} custom-call(f32[1,2048]{1,0:T(1,128)S(1)} %bitcast.9, bf16[2048,512]{1,0:T(8,128)(2,1)S(1)} %copy-done), custom_call_target="tpu_custom_call" | custom-call | tf_op jit(solution)/shard_map/scaled/pallas_call | solution.py:172
  56.8 3.8 %all-to-all-start.2 = ((bf16[8,80,512]{2,1,0:T(8,128)(2,1)}), bf16[8,80,512]{2,1,0:T(8,128)(2,1)S(1)}, u32[]{:S(2)}, u32[]{:S(2)}) async-start(bf16[8,80,512]{2,1,0:T(8,128)(2,1)} %pick.1), calls=%async_computation.2 | async-start | bytes 1310720 | tf_op jit(solution)/shard_map/all_to_all | solution.py:373
  60.6 12.8 %all-gather.2.cloned.1.call-done.x_ref = bf16[2048,2048]{1,0:T(8,128)(2,1)} async-done(((bf16[128,2048]{1,0:T(8,128)(2,1)}), bf16[2048,2048]{1,0:T(8,128)(2,1)}) %all-gather.2.cloned.1.call-update) | async-done | bytes 8388624 | tf_op jit(solution)/shard_map/all_gather | solution.py:360
  73.4 7.6 %partials.2.refs_1_ = bf16[2,8,4,64,512]{4,3,2,1,0:T(8,128)(2,1)} custom-call(s32[1]{0:T(128)} %bitcast.1.place_ref, bf16[2048,2048]{1,0:T(8,128)(2,1)} %all-gather.2.cloned.1.call-done.x_ref, bf16[2048,512]{1,0:T(8,128)(2,1)} %scaled.1.cot_ref), custom_call_target="tpu_custom_call" | custom-call | flops 4294967296 | bytes 12582912 | tf_op jit(solution)/shard_map/partials/pallas_call | solution.py:228
  81.0 0.0 collective-permute-done.1.cot_ref
  81.0 7.3 %partials.3 = bf16[2,8,4,64,512]{4,3,2,1,0:T(8,128)(2,1)} custom-call(s32[1]{0:T(128)S(6)} %sub.3.place_ref, bf16[2048,2048]{1,0:T(8,128)(2,1)} %all-gather.2.cloned.1.call-done.x_ref, bf16[2048,512]{1,0:T(8,128)(2,1)S(1)} %collective-permute-done.1.cot_ref, f32[1,2048]{1,0:T(1,128)S(1)} %bitcast.10, ...), custom_call_target="tpu_custom_call", output_to_operand_aliasing={{}: (4, {})} | custom-call | flops 4294967296 | bytes 12582912 | tf_op jit(solution)/shard_map/partials/pallas_call | solution.py:228
  88.2 0.0 all-to-all-done.2.x_ref
  88.2 55.5 %all_to_all.26 = bf16[16,4,64,512]{3,2,1,0:T(8,128)(2,1)S(1)} all-to-all(bf16[16,4,64,512]{3,2,1,0:T(8,128)(2,1)} %bitcast.13), channel_id=1, replica_groups=mesh['y'=4,'xh'=2,'xl'=2,'z'=8,'core'=2] {'xl','y','xh'}, dimensions={0} | all-to-all | bytes 8388608 | tf_op jit(solution)/shard_map/all_to_all | solution.py:380
  143.8 1.9 %route.1 = bf16[8,2,64,512]{3,2,1,0:T(8,128)(2,1)} custom-call(s32[8]{0:T(128)S(1)} %bitcast.12, bf16[2,8,4,64,512]{4,3,2,1,0:T(8,128)(2,1)S(1)} %bitcast.8), custom_call_target="tpu_custom_call" | custom-call | tf_op jit(solution)/shard_map/route/pallas_call | solution.py:263
  145.6 4.1 %all-to-all-start.4 = ((bf16[8,2,64,512]{3,2,1,0:T(8,128)(2,1)}), bf16[8,2,64,512]{3,2,1,0:T(8,128)(2,1)S(1)}, u32[]{:S(2)}, u32[]{:S(2)}) async-start(bf16[8,2,64,512]{3,2,1,0:T(8,128)(2,1)} %route.1), calls=%async_computation.4 | async-start | bytes 2097152 | tf_op jit(solution)/shard_map/all_to_all | solution.py:382
  150.4 0.3 unpack_roots.1
  150.7 12.4 %all-to-all-done.4.u_ref = bf16[8,2,64,512]{3,2,1,0:T(8,128)(2,1)S(1)} async-done(((bf16[8,2,64,512]{3,2,1,0:T(8,128)(2,1)}), bf16[8,2,64,512]{3,2,1,0:T(8,128)(2,1)S(1)}, u32[]{:S(2)}, u32[]{:S(2)}) %all-to-all-start.4) | async-done | bytes 1048608 | tf_op jit(solution)/shard_map/all_to_all | solution.py:382
  163.1 4.9 %block_step.1 = (bf16[512,512]{1,0:T(8,128)(2,1)}, f32[512,512]{1,0:T(8,128)}, f32[512,512]{1,0:T(8,128)}, f32[512,512]{1,0:T(8,128)}, f32[512,512]{1,0:T(8,128)}) custom-call(s32[1,1]{1,0:T(1,128)S(6)} %copy.18.refresh_ref, bf16[8,2,64,512]{3,2,1,0:T(8,128)(2,1)S(1)} %all-to-all-done.4.u_ref, bf16[512,512]{1,0:T(8,128)(2,1)S(1)} %get-tuple-element.27.lroot_ref, ...), custom_call_target="tpu_custom_call" | custom-call | flops 2147483648 | bytes 11534336 | tf_op jit(solution)/shard_map/block_step/pallas_call | solution.py:341
  (4 shorter events, 0.0 us)
Async XLA Ops:
  7.2 12.2 %copy-start.2 = (bf16[2048,128]{1,0:T(8,128)(2,1)S(1)}, bf16[2048,128]{1,0:T(8,128)(2,1)}, u32[]{:S(2)}) copy-start(bf16[2048,128]{1,0:T(8,128)(2,1)} %x_ref.2) | copy-start | bytes 1572868
  7.2 35.1 %copy-start.1 = (s32[1,8]{1,0:T(1,128)S(1)}, s32[1,8]{1,0:T(1,128)}, u32[]{:S(2)}) copy-start(s32[1,8]{1,0:T(1,128)} %param.12) | copy-start | bytes 100
  7.2 66.2 %all-gather.2.cloned.1.call-start = ((), (), s32[]{:S(2)}) async-start(), calls=%async_computation.5 | async-start | bytes 8912896 | tf_op jit(solution)/shard_map/all_gather | solution.py:360
  11.8 17.8 %all-to-all-start = ((bf16[8,80,512]{2,1,0:T(8,128)(2,1)}), bf16[8,80,512]{2,1,0:T(8,128)(2,1)S(1)}, u32[]{:S(2)}, u32[]{:S(2)}) async-start(bf16[8,80,512]{2,1,0:T(8,128)(2,1)} %pack_roots.1), calls=%async_computation | async-start | bytes 1310720 | tf_op jit(solution)/shard_map/all_to_all | solution.py:365
  19.7 7.5 %collective-permute-start = (f32[1,2048]{1,0:T(1,128)S(1)}, f32[1,2048]{1,0:T(1,128)S(1)}, u32[]{:S(2)}, u32[]{:S(2)}) collective-permute-start(f32[1,2048]{1,0:T(1,128)S(1)} %bitcast.14), channel_id=1, source_target_pairs={{0,16},{16,0},{1,17},{17,1},{2,18},{18,2},{3,19},{19,3},{4,20},{20... | collective-permute-start | bytes 24584 | tf_op jit(solution)/shard_map/ppermute | solution.py:364
  29.7 51.3 %collective-permute-start.1 = (bf16[2048,512]{1,0:T(8,128)(2,1)}, bf16[2048,512]{1,0:T(8,128)(2,1)S(1)}, u32[]{:S(2)}, u32[]{:S(2)}) collective-permute-start(bf16[2048,512]{1,0:T(8,128)(2,1)} %x_ref.3), channel_id=1, source_target_pairs={{0,16},{16,0},{1,17},{17,1},{2,18},{18,2},{3,19},{19,3},{4,20},{20... | collective-permute-start | bytes 6291464 | tf_op jit(solution)/shard_map/ppermute | solution.py:367
  30.7 22.2 %all-to-all-start.1 = ((f32[16,1,2048]{2,1,0:T(1,128)}), f32[16,1,2048]{2,1,0:T(1,128)S(1)}, u32[]{:S(2)}, u32[]{:S(2)}) async-start(f32[16,1,2048]{2,1,0:T(1,128)} %broadcast_in_dim.2), calls=%async_computation.1 | async-start | bytes 262144 | tf_op jit(solution)/shard_map/all_to_all | solution.py:369
  53.1 1.7 copy-start
  56.8 31.4 %all-to-all-start.2 = ((bf16[8,80,512]{2,1,0:T(8,128)(2,1)}), bf16[8,80,512]{2,1,0:T(8,128)(2,1)S(1)}, u32[]{:S(2)}, u32[]{:S(2)}) async-start(bf16[8,80,512]{2,1,0:T(8,128)(2,1)} %pick.1), calls=%async_computation.2 | async-start | bytes 1310720 | tf_op jit(solution)/shard_map/all_to_all | solution.py:373
  145.6 17.5 %all-to-all-start.4 = ((bf16[8,2,64,512]{3,2,1,0:T(8,128)(2,1)}), bf16[8,2,64,512]{3,2,1,0:T(8,128)(2,1)S(1)}, u32[]{:S(2)}, u32[]{:S(2)}) async-start(bf16[8,2,64,512]{3,2,1,0:T(8,128)(2,1)} %route.1), calls=%async_computation.4 | async-start | bytes 2097152 | tf_op jit(solution)/shard_map/all_to_all | solution.py:382
Sparse Core Ops, SparseCore 0:
  10.4 62.9 all-gather.1
